TPU v7x, 128 devices: a whole 4x4x4 slice. The times are simulated.
128 devices in a mesh: dp: 4 (over x_hi, core), tensor: 8 (over y, x_lo), layer: 4 (over z).
Axes of the slice: x: 4 (x_hi: 2, x_lo: 2; x = x_hi * 2 + x_lo), y: 4, z: 4, core: 2. Of those that a mesh axis runs over, the one named last changes fastest.
Arguments:
- saved_inputs: bfloat16 [4, 2048, 8192], P(None, 'dp', ('tensor', 'layer')), may hold values from -6 to 6
- output_grad: bfloat16 [2048, 8192], P('dp', ('tensor', 'layer')), may hold values from -4 to 4
- weights: bfloat16 [4, 8192, 8, 4, 256], P(None, 'tensor', None, 'layer'), may hold values from -0.0625 to 0.0625
- proj_in: bfloat16 [4, 64, 8192], P(None, None, ('tensor', 'layer')), may hold values from -0.0625 to 0.0625
- proj_out: bfloat16 [4, 64, 8192], P(None, None, ('tensor', 'layer')), may hold values from -0.0625 to 0.0625
- query_grads: bfloat16 [4, 4096, 4096], P('layer', ('dp', 'tensor')), may hold values from -0.00390625 to 0.00390625
- owner_map: int32 [4], replicated, may hold values from 0 to 3, each once
Outputs:
- input_grad: bfloat16 [2048, 8192], P('dp', ('tensor', 'layer'))
- scores: float32 [4, 4096], P('layer', ('dp', 'tensor'))
Inputs may be any that keep to these rules, and one draw needn't show every extreme that they name: `owner_map`: each owner is named by exactly one layer.
All inputs are finite; a program needn't handle non-finite values.
Results may differ from a plain program's by a relative error of at most 0.035.
Values may be sent and summed in bfloat16 or wider, within the bound.
No kernel may reach another device: no remote copies, remote signals or barrier semaphores. Data moves between devices by JAX's collectives and lax.ppermute only.
A program may use at most 128 MiB of HBM per device.

v0:
```python
import jax
import jax.numpy as jnp
from jax import lax
from jax.sharding import PartitionSpec as P

LEN = 512


def copy_for_each(value, axis):
    copies = jnp.broadcast_to(value, (lax.axis_size(axis), *value.shape))
    return lax.all_to_all(copies, axis, split_axis=0, concat_axis=0, tiled=True)


def joined_along(blocks, dim):
    dims = list(blocks.shape[1:])
    dims[dim] *= blocks.shape[0]
    return jnp.moveaxis(blocks, 0, dim).reshape(dims)


def collect(value, axis, dim):
    blocks = copy_for_each(value, axis)
    return joined_along(blocks, dim)


def cut_along(value, dim, peers):
    dims = value.shape
    blocks = value.reshape(*dims[:dim], peers, dims[dim] // peers, *dims[dim + 1 :])
    return jnp.moveaxis(blocks, dim, 0)


def sum_at_owner(value, axis, dim):
    blocks = cut_along(value, dim, lax.axis_size(axis))
    arrived = lax.all_to_all(blocks, axis, split_axis=0, concat_axis=0, tiled=True)
    return arrived.astype(jnp.float32).sum(axis=0)


def of_everyone(value, axis):
    return copy_for_each(value, axis).sum(axis=0)


def sent_and_summed(value, axis, dim):
    peers = lax.axis_size(axis)
    blocks = lax.all_to_all(cut_along(value, dim, peers), axis, 0, 0, tiled=True)
    return jnp.sum(blocks, axis=0)


def on_device(saved_inputs, output_grad, weights, proj_in, proj_out, query_grads, owner_map):
    layers = weights.shape[0]
    tok_rows = output_grad.shape[0]
    rank = proj_in.shape[1]
    in_rows = weights.shape[1]
    n_tensor = lax.axis_size("tensor")
    n_layer = lax.axis_size("layer")
    grad_now = output_grad.astype(jnp.float32)
    grad_bf = output_grad
    factor_list = [None] * layers
    for level in reversed(range(layers)):
        out_factor = jnp.einsum(
            "td,rd->tr", grad_bf, proj_out[level], preferred_element_type=jnp.float32
        )
        in_factor = jnp.einsum(
            "td,rd->tr", saved_inputs[level], proj_in[level], preferred_element_type=jnp.float32
        )
        joined = jnp.concatenate([out_factor, in_factor], axis=1)
        factor_list[level] = joined
        weight_flat = weights[level].reshape(in_rows, -1)
        gathered = collect(grad_bf, "tensor", 1)
        partial_grad = lax.dot_general(
            gathered, weight_flat, (((1,), (1,)), ((), ())), preferred_element_type=jnp.float32
        )
        grad_now = grad_now + sum_at_owner(partial_grad.astype(jnp.bfloat16), "layer", 1)
        grad_bf = grad_now.astype(jnp.bfloat16)
    stacked = jnp.stack(factor_list, axis=0)
    layer_ids = jnp.arange(layers, dtype=jnp.int32)
    inverse = jnp.sum(
        layer_ids[None, :] * (owner_map[None, :] == layer_ids[:, None]).astype(jnp.int32), axis=1
    )
    sequences = tok_rows // LEN
    block_rows = tok_rows // n_tensor
    by_owner = jnp.take(stacked, inverse, axis=0).reshape(n_layer, n_tensor, block_rows, 2 * rank)
    ordered = jnp.swapaxes(by_owner, 0, 1).reshape(n_tensor * n_layer, block_rows, 2 * rank)
    mine = sum_at_owner(ordered.astype(jnp.bfloat16), ("tensor", "layer"), 0)[0]
    first_row = lax.axis_index("tensor") * block_rows
    row_seq = (first_row + jnp.arange(block_rows, dtype=jnp.int32)) // LEN
    member = (row_seq[:, None] == jnp.arange(sequences, dtype=jnp.int32)[None, :]).astype(
        jnp.float32
    )
    partial_blocks = jnp.einsum("rs,ra,rb->sab", member, mine[:, :rank], mine[:, rank:])
    blocks = of_everyone(partial_blocks.reshape(sequences, rank * rank), "tensor")
    blocks_bf = blocks.astype(jnp.bfloat16)
    queries = query_grads[0]
    partial_scores = jnp.einsum(
        "er,qr->eq", collect(blocks_bf, "dp", 0), queries, preferred_element_type=jnp.float32
    )
    scores = sent_and_summed(partial_scores, "layer", 0)
    return (grad_bf, scores)


def solution(mesh):
    in_specs = (
        P(None, "dp", ("tensor", "layer")),
        P("dp", ("tensor", "layer")),
        P(None, "tensor", None, "layer", None),
        P(None, None, ("tensor", "layer")),
        P(None, None, ("tensor", "layer")),
        P("layer", ("dp", "tensor"), None),
        P(),
    )
    out_specs = (P("dp", ("tensor", "layer")), P("layer", ("dp", "tensor")))
    return jax.shard_map(
        on_device, mesh=mesh, in_specs=in_specs, out_specs=out_specs, check_vma=False
    )
```

profile of v0, /device:TPU:0, one launch (start us, length us, event | category | flops | bytes accessed | tf_op | source)
XLA Modules:
  0.0 274.7 jit_solution(3957427582234803124)
XLA Ops:
  0.6 1.2 copy.39
  1.8 1.5 broadcast_in_dim.32
  3.3 5.5 %all-to-all-start = ((bf16[8,512,256]{1,2,0:T(8,128)(2,1)}), bf16[8,512,256]{1,2,0:T(8,128)(2,1)S(1)}, u32[]{:S(2)}, u32[]{:S(2)}) async-start(bf16[8,512,256]{1,2,0:T(8,128)(2,1)} %broadcast_in_dim.32), calls=%async_computation | async-start | bytes 4194304 | tf_op jit(solution)/shard_map/all_to_all | solution.py:11
  8.8 10.8 %fusion.47 = (bf16[1,1024,8,1,256]{4,2,3,1,0:T(8,128)(2,1)}, bf16[1,1024,8,1,256]{4,2,3,1,0:T(8,128)(2,1)}, bf16[1,1024,8,1,256]{4,2,3,1,0:T(8,128)(2,1)S(1)}, bf16[1,1024,8,1,256]{4,2,3,1,0:T(8,128)(2,1)}) fusion(bf16[4,1024,8,1,256]{4,2,3,1,0:T(8,128)(2,1)} %param.9), kind=kLoop, calls=%fused_computation.80 | loop fusion | bytes 33554432 | tf_op jit(solution)/shard_map/slice | solution.py:66
  19.6 3.4 %copy.58 = bf16[128,8,8,256]{3,1,2,0:T(8,128)(2,1)} copy(bf16[128,8,8,256]{3,2,1,0:T(8,128)(2,1)S(1)} %bitcast.135) | data formatting | bytes 8388608
  23.0 12.8 %all-to-all-done = bf16[8,512,256]{1,2,0:T(8,128)(2,1)S(1)} async-done(((bf16[8,512,256]{1,2,0:T(8,128)(2,1)}), bf16[8,512,256]{1,2,0:T(8,128)(2,1)S(1)}, u32[]{:S(2)}, u32[]{:S(2)}) %all-to-all-start) | async-done | bytes 2097184 | tf_op jit(solution)/shard_map/all_to_all | solution.py:11
  35.8 4.6 %convolution_convert_fusion.3 = bf16[512,1024]{1,0:T(8,128)(2,1)S(1)} fusion(bf16[512,2048]{0,1:T(8,128)(2,1)S(1)} %bitcast.143, bf16[1024,2048]{1,0:T(8,128)(2,1)} %bitcast.138), kind=kOutput, calls=%fused_computation.8 | convolution fusion | flops 2148007936 | bytes 7340032 | tf_op jit(solution)/shard_map/dot_general | solution.py:68
  40.5 19.1 %all_to_all.60 = bf16[4,512,256]{2,1,0:T(8,128)(2,1)S(1)} all-to-all(bf16[4,512,256]{2,1,0:T(8,128)(2,1)S(1)} %bitcast.142), channel_id=1, replica_groups=mesh['dp'=4,'tensor'=8,'layer'=4] {'layer'}, dimensions={0} | all-to-all | bytes 2097152 | tf_op jit(solution)/shard_map/all_to_all | solution.py:33
  60.0 1.5 broadcast_in_dim.33
  61.5 4.3 %all-to-all-start.2 = ((bf16[8,512,256]{1,2,0:T(8,128)(2,1)}), bf16[8,512,256]{1,2,0:T(8,128)(2,1)}, u32[]{:S(2)}, u32[]{:S(2)}) async-start(bf16[8,512,256]{1,2,0:T(8,128)(2,1)} %broadcast_in_dim.33), calls=%async_computation.2 | async-start | bytes 4194304 | tf_op jit(solution)/shard_map/all_to_all | solution.py:11
  65.8 5.6 %copy.59 = bf16[128,8,8,256]{3,1,2,0:T(8,128)(2,1)} copy(bf16[128,8,8,256]{3,2,1,0:T(8,128)(2,1)} %bitcast.134) | data formatting | bytes 8388608
  71.4 19.9 %all-to-all-done.2 = bf16[8,512,256]{1,2,0:T(8,128)(2,1)} async-done(((bf16[8,512,256]{1,2,0:T(8,128)(2,1)}), bf16[8,512,256]{1,2,0:T(8,128)(2,1)}, u32[]{:S(2)}, u32[]{:S(2)}) %all-to-all-start.2) | async-done | bytes 2097184 | tf_op jit(solution)/shard_map/all_to_all | solution.py:11
  91.3 5.2 %convolution_convert_fusion.2 = bf16[512,1024]{1,0:T(8,128)(2,1)S(1)} fusion(bf16[512,2048]{0,1:T(8,128)(2,1)} %bitcast.4, bf16[1024,2048]{1,0:T(8,128)(2,1)} %bitcast.139), kind=kOutput, calls=%fused_computation.7 | convolution fusion | flops 2148007936 | bytes 7340032 | tf_op jit(solution)/shard_map/dot_general | solution.py:68
  96.5 1.1 copy.72
  97.6 3.7 %all-to-all-start.3 = ((bf16[4,512,256]{2,1,0:T(8,128)(2,1)}), bf16[4,512,256]{2,1,0:T(8,128)(2,1)S(1)}, u32[]{:S(2)}, u32[]{:S(2)}) async-start(bf16[4,512,256]{2,1,0:T(8,128)(2,1)} %bitcast.141), calls=%async_computation.3 | async-start | bytes 2097152 | tf_op jit(solution)/shard_map/all_to_all | solution.py:33
  101.3 5.6 %copy.60 = bf16[128,8,8,256]{3,1,2,0:T(8,128)(2,1)} copy(bf16[128,8,8,256]{3,2,1,0:T(8,128)(2,1)} %bitcast.133) | data formatting | bytes 8388608
  106.9 6.6 %all-to-all-done.3 = bf16[4,512,256]{2,1,0:T(8,128)(2,1)S(1)} async-done(((bf16[4,512,256]{2,1,0:T(8,128)(2,1)}), bf16[4,512,256]{2,1,0:T(8,128)(2,1)S(1)}, u32[]{:S(2)}, u32[]{:S(2)}) %all-to-all-start.3) | async-done | bytes 1048608 | tf_op jit(solution)/shard_map/all_to_all | solution.py:33
  113.9 1.5 broadcast_in_dim.34
  115.4 6.0 %all-to-all-start.4 = ((bf16[8,512,256]{1,2,0:T(8,128)(2,1)}), bf16[8,512,256]{1,2,0:T(8,128)(2,1)}, u32[]{:S(2)}, u32[]{:S(2)}) async-start(bf16[8,512,256]{1,2,0:T(8,128)(2,1)} %broadcast_in_dim.34), calls=%async_computation.4 | async-start | bytes 4194304 | tf_op jit(solution)/shard_map/all_to_all | solution.py:11
  122.5 1.2 fusion.5
  123.7 1.8 fusion.11
  125.5 1.8 fusion.9
  127.3 1.8 fusion.7
  129.1 18.8 %all-to-all-done.4 = bf16[8,512,256]{1,2,0:T(8,128)(2,1)} async-done(((bf16[8,512,256]{1,2,0:T(8,128)(2,1)}), bf16[8,512,256]{1,2,0:T(8,128)(2,1)}, u32[]{:S(2)}, u32[]{:S(2)}) %all-to-all-start.4) | async-done | bytes 2097184 | tf_op jit(solution)/shard_map/all_to_all | solution.py:11
  147.9 5.2 %convolution_convert_fusion.1 = bf16[512,1024]{1,0:T(8,128)(2,1)S(1)} fusion(bf16[512,2048]{0,1:T(8,128)(2,1)} %bitcast.7, bf16[1024,2048]{1,0:T(8,128)(2,1)} %bitcast.136), kind=kOutput, calls=%fused_computation.6 | convolution fusion | flops 2148007936 | bytes 7340032 | tf_op jit(solution)/shard_map/dot_general | solution.py:68
  153.1 1.1 copy.71
  154.1 3.5 %all-to-all-start.5 = ((bf16[4,512,256]{2,1,0:T(8,128)(2,1)}), bf16[4,512,256]{2,1,0:T(8,128)(2,1)S(1)}, u32[]{:S(2)}, u32[]{:S(2)}) async-start(bf16[4,512,256]{2,1,0:T(8,128)(2,1)} %bitcast.140), calls=%async_computation.5 | async-start | bytes 2097152 | tf_op jit(solution)/shard_map/all_to_all | solution.py:33
  157.7 1.2 fusion.27
  158.8 1.5 maximum_bitcast_fusion.2
  160.3 1.2 fusion.30
  161.5 1.5 maximum_bitcast_fusion.1
  163.0 8.1 %all-to-all-done.5 = bf16[4,512,256]{2,1,0:T(8,128)(2,1)S(1)} async-done(((bf16[4,512,256]{2,1,0:T(8,128)(2,1)}), bf16[4,512,256]{2,1,0:T(8,128)(2,1)S(1)}, u32[]{:S(2)}, u32[]{:S(2)}) %all-to-all-start.5) | async-done | bytes 1048608 | tf_op jit(solution)/shard_map/all_to_all | solution.py:33
  171.4 1.0 fusion.33
  174.4 5.7 %all-to-all-start.8 = ((bf16[32,1,64,128]{3,2,1,0:T(8,128)(2,1)}), bf16[32,1,64,128]{3,2,1,0:T(8,128)(2,1)S(1)}, u32[]{:S(2)}, u32[]{:S(2)}) async-start(bf16[32,1,64,128]{3,2,1,0:T(8,128)(2,1)} %bitcast.33), calls=%async_computation.8 | async-start | bytes 1048576 | tf_op jit(solution)/shard_map/all_to_all | solution.py:33
  180.2 10.8 %all-to-all-done.8 = bf16[32,1,64,128]{3,2,1,0:T(8,128)(2,1)S(1)} async-done(((bf16[32,1,64,128]{3,2,1,0:T(8,128)(2,1)}), bf16[32,1,64,128]{3,2,1,0:T(8,128)(2,1)S(1)}, u32[]{:S(2)}, u32[]{:S(2)}) %all-to-all-start.8) | async-done | bytes 524320 | tf_op jit(solution)/shard_map/all_to_all | solution.py:33
  191.5 9.6 %all_to_all.61 = f32[8,1,4096]{2,1,0:T(1,128)S(1)} all-to-all(f32[8,1,4096]{2,1,0:T(1,128)S(1)} %broadcast_in_dim.38), channel_id=1, replica_groups=mesh['dp'=4,'tensor'=8,'layer'=4] {'tensor'}, dimensions={0} | all-to-all | bytes 262144 | tf_op jit(solution)/shard_map/all_to_all | solution.py:11
  203.3 4.0 %all-to-all-start.10 = ((bf16[4,2,2048]{2,1,0:T(2,128)(2,1)}), bf16[4,2,2048]{2,1,0:T(2,128)(2,1)S(1)}, u32[]{:S(2)}, u32[]{:S(2)}) async-start(bf16[4,2,2048]{2,1,0:T(2,128)(2,1)} %reshape.105), calls=%async_computation.10 | async-start | bytes 65536 | tf_op jit(solution)/shard_map/all_to_all | solution.py:11
  207.4 5.3 %all-to-all-done.10 = bf16[4,2,2048]{2,1,0:T(2,128)(2,1)S(1)} async-done(((bf16[4,2,2048]{2,1,0:T(2,128)(2,1)}), bf16[4,2,2048]{2,1,0:T(2,128)(2,1)S(1)}, u32[]{:S(2)}, u32[]{:S(2)}) %all-to-all-start.10) | async-done | bytes 32800 | tf_op jit(solution)/shard_map/all_to_all | solution.py:11
  212.7 1.5 broadcast_in_dim.35
  214.2 4.4 %all-to-all-start.6 = ((bf16[8,512,256]{1,2,0:T(8,128)(2,1)}), bf16[8,512,256]{1,2,0:T(8,128)(2,1)}, u32[]{:S(2)}, u32[]{:S(2)}) async-start(bf16[8,512,256]{1,2,0:T(8,128)(2,1)} %broadcast_in_dim.35), calls=%async_computation.6 | async-start | bytes 4194304 | tf_op jit(solution)/shard_map/all_to_all | solution.py:11
  218.6 5.6 %copy.61 = bf16[128,8,8,256]{3,1,2,0:T(8,128)(2,1)} copy(bf16[128,8,8,256]{3,2,1,0:T(8,128)(2,1)} %bitcast.132) | data formatting | bytes 8388608
  224.3 1.0 fusion
  225.2 20.5 %all-to-all-done.6 = bf16[8,512,256]{1,2,0:T(8,128)(2,1)} async-done(((bf16[8,512,256]{1,2,0:T(8,128)(2,1)}), bf16[8,512,256]{1,2,0:T(8,128)(2,1)}, u32[]{:S(2)}, u32[]{:S(2)}) %all-to-all-start.6) | async-done | bytes 2097184 | tf_op jit(solution)/shard_map/all_to_all | solution.py:11
  245.7 3.4 %all-to-all-start.11 = ((f32[4,1,128]{2,1,0:T(1,128)}), f32[4,1,128]{2,1,0:T(1,128)S(1)}, u32[]{:S(2)}, u32[]{:S(2)}) async-start(f32[4,1,128]{2,1,0:T(1,128)} %bitcast.36), calls=%async_computation.11 | async-start | bytes 4096 | tf_op jit(solution)/shard_map/all_to_all | solution.py:43
  249.2 5.2 %convolution_convert_fusion = bf16[512,1024]{1,0:T(8,128)(2,1)S(1)} fusion(bf16[512,2048]{0,1:T(8,128)(2,1)} %bitcast.10, bf16[1024,2048]{1,0:T(8,128)(2,1)} %bitcast.137), kind=kOutput, calls=%fused_computation.5 | convolution fusion | flops 2148007936 | bytes 7340032 | tf_op jit(solution)/shard_map/dot_general | solution.py:68
  254.4 1.0 copy.70
  255.4 4.5 %all-to-all-start.7 = ((bf16[4,512,256]{2,1,0:T(8,128)(2,1)}), bf16[4,512,256]{2,1,0:T(8,128)(2,1)S(1)}, u32[]{:S(2)}, u32[]{:S(2)}) async-start(bf16[4,512,256]{2,1,0:T(8,128)(2,1)} %bitcast.125), calls=%async_computation.7 | async-start | bytes 2097152 | tf_op jit(solution)/shard_map/all_to_all | solution.py:33
  260.5 13.3 %all-to-all-done.7 = bf16[4,512,256]{2,1,0:T(8,128)(2,1)S(1)} async-done(((bf16[4,512,256]{2,1,0:T(8,128)(2,1)}), bf16[4,512,256]{2,1,0:T(8,128)(2,1)S(1)}, u32[]{:S(2)}, u32[]{:S(2)}) %all-to-all-start.7) | async-done | bytes 1048608 | tf_op jit(solution)/shard_map/all_to_all | solution.py:33
  (55 shorter events, 8.4 us)
Async XLA Ops:
  0.6 223.6 %copy-start = (bf16[1,128,4096]{2,1,0:T(8,128)(2,1)S(1)}, bf16[1,128,4096]{2,1,0:T(8,128)(2,1)}, u32[]{:S(2)}) copy-start(bf16[1,128,4096]{2,1,0:T(8,128)(2,1)} %param.12) | copy-start | bytes 3145732
  3.3 32.5 %all-to-all-start = ((bf16[8,512,256]{1,2,0:T(8,128)(2,1)}), bf16[8,512,256]{1,2,0:T(8,128)(2,1)S(1)}, u32[]{:S(2)}, u32[]{:S(2)}) async-start(bf16[8,512,256]{1,2,0:T(8,128)(2,1)} %broadcast_in_dim.32), calls=%async_computation | async-start | bytes 4194304 | tf_op jit(solution)/shard_map/all_to_all | solution.py:11
  40.4 19.3 %copy-start.1 = (bf16[512,256]{1,0:T(8,128)(2,1)S(1)}, bf16[512,256]{1,0:T(8,128)(2,1)}, u32[]{:S(2)}) copy-start(bf16[512,256]{1,0:T(8,128)(2,1)} %param.8) | copy-start | bytes 786436
  59.8 1.6 copy-start.2
  61.5 29.8 %all-to-all-start.2 = ((bf16[8,512,256]{1,2,0:T(8,128)(2,1)}), bf16[8,512,256]{1,2,0:T(8,128)(2,1)}, u32[]{:S(2)}, u32[]{:S(2)}) async-start(bf16[8,512,256]{1,2,0:T(8,128)(2,1)} %broadcast_in_dim.33), calls=%async_computation.2 | async-start | bytes 4194304 | tf_op jit(solution)/shard_map/all_to_all | solution.py:11
  97.6 15.9 %all-to-all-start.3 = ((bf16[4,512,256]{2,1,0:T(8,128)(2,1)}), bf16[4,512,256]{2,1,0:T(8,128)(2,1)S(1)}, u32[]{:S(2)}, u32[]{:S(2)}) async-start(bf16[4,512,256]{2,1,0:T(8,128)(2,1)} %bitcast.141), calls=%async_computation.3 | async-start | bytes 2097152 | tf_op jit(solution)/shard_map/all_to_all | solution.py:33
  113.8 1.7 copy-start.3
  115.4 6.0 %copy-start.8 = (s32[4]{0:T(128)S(1)}, s32[4]{0:T(128)}, u32[]{:S(2)}) copy-start(s32[4]{0:T(128)} %param.13) | copy-start | bytes 52
  115.4 7.1 %copy-start.7 = (bf16[4,64,256]{2,1,0:T(8,128)(2,1)S(1)}, bf16[4,64,256]{2,1,0:T(8,128)(2,1)}, u32[]{:S(2)}) copy-start(bf16[4,64,256]{2,1,0:T(8,128)(2,1)} %param.10) | copy-start | bytes 393220
  115.4 32.4 %all-to-all-start.4 = ((bf16[8,512,256]{1,2,0:T(8,128)(2,1)}), bf16[8,512,256]{1,2,0:T(8,128)(2,1)}, u32[]{:S(2)}, u32[]{:S(2)}) async-start(bf16[8,512,256]{1,2,0:T(8,128)(2,1)} %broadcast_in_dim.34), calls=%async_computation.4 | async-start | bytes 4194304 | tf_op jit(solution)/shard_map/all_to_all | solution.py:11
  154.1 17.0 %all-to-all-start.5 = ((bf16[4,512,256]{2,1,0:T(8,128)(2,1)}), bf16[4,512,256]{2,1,0:T(8,128)(2,1)S(1)}, u32[]{:S(2)}, u32[]{:S(2)}) async-start(bf16[4,512,256]{2,1,0:T(8,128)(2,1)} %bitcast.140), calls=%async_computation.5 | async-start | bytes 2097152 | tf_op jit(solution)/shard_map/all_to_all | solution.py:33
  171.1 1.2 copy-start.6
  171.1 1.3 copy-start.4
  171.1 1.3 copy-start.5
  174.4 16.6 %all-to-all-start.8 = ((bf16[32,1,64,128]{3,2,1,0:T(8,128)(2,1)}), bf16[32,1,64,128]{3,2,1,0:T(8,128)(2,1)S(1)}, u32[]{:S(2)}, u32[]{:S(2)}) async-start(bf16[32,1,64,128]{3,2,1,0:T(8,128)(2,1)} %bitcast.33), calls=%async_computation.8 | async-start | bytes 1048576 | tf_op jit(solution)/shard_map/all_to_all | solution.py:33
  203.3 9.4 %all-to-all-start.10 = ((bf16[4,2,2048]{2,1,0:T(2,128)(2,1)}), bf16[4,2,2048]{2,1,0:T(2,128)(2,1)S(1)}, u32[]{:S(2)}, u32[]{:S(2)}) async-start(bf16[4,2,2048]{2,1,0:T(2,128)(2,1)} %reshape.105), calls=%async_computation.10 | async-start | bytes 65536 | tf_op jit(solution)/shard_map/all_to_all | solution.py:11
  214.2 31.5 %all-to-all-start.6 = ((bf16[8,512,256]{1,2,0:T(8,128)(2,1)}), bf16[8,512,256]{1,2,0:T(8,128)(2,1)}, u32[]{:S(2)}, u32[]{:S(2)}) async-start(bf16[8,512,256]{1,2,0:T(8,128)(2,1)} %broadcast_in_dim.35), calls=%async_computation.6 | async-start | bytes 4194304 | tf_op jit(solution)/shard_map/all_to_all | solution.py:11
  245.7 9.7 %all-to-all-start.11 = ((f32[4,1,128]{2,1,0:T(1,128)}), f32[4,1,128]{2,1,0:T(1,128)S(1)}, u32[]{:S(2)}, u32[]{:S(2)}) async-start(f32[4,1,128]{2,1,0:T(1,128)} %bitcast.36), calls=%async_computation.11 | async-start | bytes 4096 | tf_op jit(solution)/shard_map/all_to_all | solution.py:43
  255.4 18.4 %all-to-all-start.7 = ((bf16[4,512,256]{2,1,0:T(8,128)(2,1)}), bf16[4,512,256]{2,1,0:T(8,128)(2,1)S(1)}, u32[]{:S(2)}, u32[]{:S(2)}) async-start(bf16[4,512,256]{2,1,0:T(8,128)(2,1)} %bitcast.125), calls=%async_computation.7 | async-start | bytes 2097152 | tf_op jit(solution)/shard_map/all_to_all | solution.py:33
where the time goes:
time: 276 us; the launch traced here: 275 us
  waiting for transfers between devices  116 us (42%)
  local copies, waits for them, and re-layouts  45.1 us (16%)
  starting transfers between devices  45.1 us (16%)
  matrix products  32.1 us (12%)
  blocking collectives  28.7 us (10%)
  other arithmetic  6.6 us (2%)
    all_to_all x5, waiting for transfers between devices, copy_for_each(): return lax.all_to_all(copies, axis, split_axis=0, concat_axis=0, tiled=True)  77.2 us
    all_to_all x4, waiting for transfers between devices, sum_at_owner(): lax.all_to_all(blocks, axis, split_axis=0, concat_axis=0, tiled=True)  38.8 us
    all_to_all x5, starting transfers between devices, copy_for_each(): return lax.all_to_all(copies, axis, split_axis=0, concat_axis=0, tiled=True)  24.2 us
    unnamed x25, local copies, waits for them, and re-layouts  22.2 us
    dot_general x4, matrix products, on_device(): lax.dot_general(gathered, weight_flat, (((1,), (1,)), ((), ())), preferre...  20.2 us
    all_to_all x1, blocking collectives, sum_at_owner(): lax.all_to_all(blocks, axis, split_axis=0, concat_axis=0, tiled=True)  19.1 us
    all_to_all x4, starting transfers between devices, sum_at_owner(): lax.all_to_all(blocks, axis, split_axis=0, concat_axis=0, tiled=True)  17.5 us
    slice x1, local copies, waits for them, and re-layouts, on_device(): weight_flat = weights[level].reshape(in_rows, -1)  10.8 us
  transfers between devices with their start and end apart: 10, of which 9 were waited for; matrix products, arithmetic and copies ran while one was open for 19% of the time, Pallas kernels for 0%

commit v1 on v0

v1 whole, which is shorter than its diff:
```python
import jax
import jax.numpy as jnp
from jax import lax
from jax.experimental import pallas as pl
from jax.experimental.pallas import tpu as pltpu
from jax.sharding import PartitionSpec as P

NT = (((1,), (1,)), ((), ()))
F32 = jnp.float32
BF16 = jnp.bfloat16
VMEM_BYTES = 48 << 20


def features_first(weights, level, core):
    _, rows, cells, width = weights.shape
    step, half = 512, cells // 2

    def body(core_ref, w_ref, o_ref, s_ref):
        o_ref[...] = jnp.swapaxes(w_ref[0], 0, 1)
        s_ref[...] = o_ref[pl.ds(half * core_ref[0], half)]

    return pl.pallas_call(
        body,
        grid_spec=pltpu.PrefetchScalarGridSpec(
            num_scalar_prefetch=1,
            grid=(rows // step,),
            in_specs=[pl.BlockSpec((1, step, cells, width), lambda n, c: (level, n, 0, 0))],
            out_specs=[
                pl.BlockSpec((cells, step, width), lambda n, c: (0, n, 0)),
                pl.BlockSpec((half, step, width), lambda n, c: (0, n, 0)),
            ],
        ),
        out_shape=[
            jax.ShapeDtypeStruct((cells, rows, width), weights.dtype),
            jax.ShapeDtypeStruct((half, rows, width), weights.dtype),
        ],
        compiler_params=pltpu.CompilerParams(vmem_limit_bytes=VMEM_BYTES),
        cost_estimate=pl.CostEstimate(
            flops=0, bytes_accessed=5 * rows * cells * width, transcendentals=0
        ),
    )(core, weights)


def first_partial(gathered, weight):
    cells, tokens, width = gathered.shape
    rows = weight.shape[1]
    half = tokens // 2

    def body(g_ref, w_ref, o_ref):
        total = None
        for a in range(cells):
            term = lax.dot_general(g_ref[a], w_ref[a], NT, preferred_element_type=F32)
            total = term if total is None else total + term
        o_ref[0, 0] = total[:half].astype(o_ref.dtype)
        o_ref[1, 0] = total[half:].astype(o_ref.dtype)

    return pl.pallas_call(
        body,
        grid=(rows // width,),
        in_specs=[
            pl.BlockSpec((cells, tokens, width), lambda n: (0, 0, 0)),
            pl.BlockSpec((cells, width, width), lambda n: (0, n, 0)),
        ],
        out_specs=pl.BlockSpec((2, 1, half, width), lambda n: (0, n, 0, 0)),
        out_shape=jax.ShapeDtypeStruct((2, rows // width, half, width), BF16),
        compiler_params=pltpu.CompilerParams(vmem_limit_bytes=VMEM_BYTES),
        cost_estimate=pl.CostEstimate(
            flops=2 * cells * width * rows * tokens,
            bytes_accessed=2 * (cells * width * (rows + tokens) + rows * tokens),
            transcendentals=0,
        ),
    )(gathered, weight)


def pair_partial(place, gathered, own, near, far, kept=None):
    cells, tokens, width = gathered.shape
    rows = own.shape[1]
    groups = rows // width
    half = cells // 2
    last = kept is not None

    def body(s_ref, g_ref, own_ref, near_ref, far_ref, *refs):
        o_ref = refs[-1]
        phase, group = pl.program_id(0), pl.program_id(1)

        def put(total, column):
            if last:
                extra = refs[0][column]
                total = total + jnp.where(group == s_ref[2], extra, jnp.zeros_like(extra))
            o_ref[0, 0] = total.astype(o_ref.dtype)

        @pl.when(phase == 0)
        def _():
            total = None
            for a in range(cells):
                term = lax.dot_general(g_ref[a], own_ref[a], NT, preferred_element_type=F32)
                total = term if total is None else total + term
            put(total, s_ref[0])

        @pl.when(phase == 1)
        def _():
            total = None
            for ref, first in ((near_ref, s_ref[1]), (far_ref, 1 - s_ref[1])):
                for i in range(half):
                    term = lax.dot_general(
                        g_ref[half * first + i], ref[i], NT, preferred_element_type=F32
                    )
                    total = term if total is None else total + term
            put(total, 1 - s_ref[0])

    def column(p, s):
        return jnp.where(p == 0, s[0], 1 - s[0])

    if last:
        out_shape, out_map = (2, groups), lambda p, n, s: (column(p, s), n, 0, 0)
    else:
        out_shape, out_map = (groups, 2), lambda p, n, s: (n, column(p, s), 0, 0)
    in_specs = [
        pl.BlockSpec((cells, tokens, width), lambda p, n, s: (0, 0, 0)),
        pl.BlockSpec((cells, width, width), lambda p, n, s: (0, jnp.where(p == 0, n, groups - 1), 0)),
        pl.BlockSpec((half, width, width), lambda p, n, s: (0, jnp.where(p == 0, 0, n), 0)),
        pl.BlockSpec((half, width, width), lambda p, n, s: (0, jnp.where(p == 0, 0, n), 0)),
    ]
    operands = [gathered, own, near, far]
    if last:
        in_specs.append(pl.BlockSpec((2, tokens, width), lambda p, n, s: (0, 0, 0)))
        operands.append(kept)
    return pl.pallas_call(
        body,
        grid_spec=pltpu.PrefetchScalarGridSpec(
            num_scalar_prefetch=1,
            grid=(2, groups),
            in_specs=in_specs,
            out_specs=pl.BlockSpec((1, 1, tokens, width), out_map),
        ),
        out_shape=jax.ShapeDtypeStruct((*out_shape, tokens, width), BF16),
        compiler_params=pltpu.CompilerParams(vmem_limit_bytes=VMEM_BYTES),
        cost_estimate=pl.CostEstimate(
            flops=4 * cells * width * rows * tokens,
            bytes_accessed=2 * (cells * width * (2 * rows + tokens) + 2 * rows * tokens),
            transcendentals=0,
        ),
    )(place, *operands)


def exchange(blocks, axes, groups=None):
    return lax.all_to_all(blocks, axes, 0, 0, tiled=True, axis_index_groups=groups)


def spread(value, axes, peers, groups=None):
    return exchange(jnp.broadcast_to(value, (peers, *value.shape)), axes, groups)


def on_device(saved_inputs, output_grad, weights, proj_in, proj_out, query_grads, owner_map):
    layers, tokens, width = saved_inputs.shape
    rank = proj_in.shape[1]
    rows = weights.shape[1]
    n_dp, n_tensor, n_layer = (lax.axis_size(k) for k in ("dp", "tensor", "layer"))
    n_y = n_tensor // 2
    half = tokens // 2
    t, b = lax.axis_index("tensor"), lax.axis_index("layer")
    x, y = t % 2, t // 2
    core = lax.axis_index("dp") % 2
    place = jnp.stack([x, core, b]).astype(jnp.int32)
    core1 = core.astype(jnp.int32).reshape(1)
    along_y = [[2 * k + j for k in range(n_y)] for j in range(2)]
    along_xz = [[2 * n_layer * k + j for j in range(2 * n_layer)] for k in range(n_y)]
    across = [
        (d * n_tensor + k, (d ^ 2) * n_tensor + (k ^ 1)) for d in range(n_dp) for k in range(n_tensor)
    ]
    flat = weights.reshape(layers, rows, n_tensor, width)

    own, near, far = [None] * layers, [None] * layers, [None] * layers
    for level in (2, 3, 1, 0):
        own[level], passed = features_first(flat, level, core1)
        if level < layers - 1:
            near[level] = lax.ppermute(passed, ("dp", "tensor"), across)
            far[level] = lax.ppermute(near[level], "dp", [(d, d ^ 1) for d in range(n_dp)])
    other_proj = lax.ppermute(
        proj_out[: layers - 1], "tensor", [(k, k ^ 1) for k in range(n_tensor)]
    )
    pair_proj = jnp.where(
        x == 0, jnp.stack([proj_out[: layers - 1], other_proj]), jnp.stack([other_proj, proj_out[: layers - 1]])
    )

    outs = [None] * layers
    outs[layers - 1] = lax.dot_general(output_grad, proj_out[layers - 1], NT, preferred_element_type=F32)
    gathered = spread(output_grad, "tensor", n_tensor)
    partial = first_partial(gathered, own[layers - 1])
    arrived = exchange(partial.reshape(2 * n_layer, half, width), ("tensor", "layer"), along_xz)
    start = lax.dynamic_slice(
        gathered.reshape(n_y, 2, 2, half, width), (y, 0, x, 0, 0), (1, 2, 1, half, width)
    ).reshape(2, half, width)
    total = start.astype(F32) + arrived.reshape(2, n_layer, half, width).astype(F32).sum(axis=1)
    for level in reversed(range(layers - 1)):
        grad = total.astype(BF16)
        out_half = sum(
            lax.dot_general(grad[k], pair_proj[k, level], NT, preferred_element_type=F32)
            for k in range(2)
        )
        outs[level] = lax.dynamic_update_slice(jnp.zeros((tokens, rank), F32), out_half, (x * half, 0))
        gathered = spread(grad, "tensor", n_y, along_y).reshape(n_tensor, half, width)
        if level:
            partial = pair_partial(place, gathered, own[level], near[level], far[level])
            arrived = exchange(partial, "layer")
            total = total + arrived.astype(F32).sum(axis=0)
        else:
            partial = pair_partial(place, gathered, own[level], near[level], far[level], total)
            arrived = exchange(
                partial.reshape(2 * n_layer, half, width), ("tensor", "layer"), along_xz
            )
            total = arrived.reshape(2, n_layer, half, width).astype(F32).sum(axis=1)
    input_grad = total.astype(BF16).reshape(tokens, width)

    stacked = jnp.stack(
        [
            jnp.concatenate(
                [
                    outs[k],
                    lax.dot_general(saved_inputs[k], proj_in[k], NT, preferred_element_type=F32),
                ],
                axis=1,
            )
            for k in range(layers)
        ]
    ).astype(BF16)
    owners = jnp.arange(n_layer, dtype=jnp.int32)
    inverse = jnp.sum(
        owners[None, :] * (owner_map[None, :] == owners[:, None]).astype(jnp.int32), axis=1
    )
    block_rows = tokens // n_tensor
    by_owner = jnp.take(stacked, inverse, axis=0).reshape(n_layer, n_tensor, block_rows, 2 * rank)
    ordered = jnp.swapaxes(by_owner, 0, 1).reshape(n_tensor * n_layer, block_rows, 2 * rank)
    mine = exchange(ordered, ("tensor", "layer")).astype(F32).sum(axis=0)
    block = lax.dot_general(
        mine[:, :rank], mine[:, rank:], (((0,), (0,)), ((), ())),
        preferred_element_type=F32, precision=lax.Precision.HIGHEST,
    ).reshape(rank * rank)
    every = spread(block, ("dp", "tensor"), n_dp * n_tensor)
    whole = every.reshape(n_dp, n_tensor, rank * rank).sum(axis=1).astype(BF16)
    scored = lax.dot_general(whole, query_grads[0], NT, preferred_element_type=F32)
    scores = exchange(scored, "layer").sum(axis=0, keepdims=True)
    return input_grad, scores


def solution(mesh):
    in_specs = (
        P(None, "dp", ("tensor", "layer")),
        P("dp", ("tensor", "layer")),
        P(None, "tensor", None, "layer", None),
        P(None, None, ("tensor", "layer")),
        P(None, None, ("tensor", "layer")),
        P("layer", ("dp", "tensor"), None),
        P(),
    )
    out_specs = (P("dp", ("tensor", "layer")), P("layer", ("dp", "tensor")))
    return jax.shard_map(
        on_device, mesh=mesh, in_specs=in_specs, out_specs=out_specs, check_vma=False
    )
```

time: 276 us -> 278 us (level)
  Pallas kernels: 0 us -> 52.4 us
  local copies, waits for them, and re-layouts: 45.1 us -> 10.4 us
  matrix products: 32.1 us -> 15 us
  blocking collectives: 28.7 us -> 16.7 us
  starting transfers between devices: 45.1 us -> 54.3 us
  other arithmetic: 6.6 us -> 9.98 us
    pallas_call x0 -> x8, Pallas kernels: none -> 52.4 us  [the longest x3 27.5 us: pair_partial(): pl.pallas_call(body, grid_spec=pltpu.PrefetchScalarGridSpec(num_scalar_pr...]
    ppermute x0 -> x7, waiting for transfers between devices: none -> 34.3 us  [the longest x3 34.3 us: on_device(): near[level] = lax.ppermute(passed, ('dp', 'tensor'), across)]
    all_to_all x10, waiting for transfers between devices: 116 us -> 82.3 us  [exchange(): lax.all_to_all(blocks, axes, 0, 0, tiled=True, axis_index_groups=groups)]
    unnamed x25 -> x24, local copies, waits for them, and re-layouts: 22.2 us -> 1.74 us
    dot_general x14 -> x13, matrix products: 32.1 us -> 15 us  [the longest x4 7.15 us: on_device(): lax.dot_general(saved_inputs[k], proj_in[k], NT, preferred_element_type=F32)]
    all_to_all x2 -> x1, blocking collectives: 28.7 us -> 16.7 us  [exchange(): lax.all_to_all(blocks, axes, 0, 0, tiled=True, axis_index_groups=groups)]
    slice x1 -> x0, local copies, waits for them, and re-layouts: 10.8 us -> none  [on_device(): weight_flat = weights[level].reshape(in_rows, -1)]
    ppermute x0 -> x7, starting transfers between devices: none -> 9.44 us  [the longest x3 9.1 us: on_device(): near[level] = lax.ppermute(passed, ('dp', 'tensor'), across)]
  transfers between devices with their start and end apart: 10 -> 17, of which waited for: 9 -> 9; matrix products, arithmetic and copies ran while one was open for 19% -> 11% of each run, Pallas kernels for 0% -> 19%
where the time goes in v1:
time: 278 us; the launch traced here: 276 us
  waiting for transfers between devices  117 us (42%)
  starting transfers between devices  54.3 us (20%)
  Pallas kernels  52.4 us (19%)
  blocking collectives  16.7 us (6%)
  matrix products  15 us (5%)
  local copies, waits for them, and re-layouts  10.4 us (4%)
  other arithmetic  9.98 us (4%)
    all_to_all x10, waiting for transfers between devices, exchange(): lax.all_to_all(blocks, axes, 0, 0, tiled=True, axis_index_groups=groups)  82.3 us
    all_to_all x10, starting transfers between devices, exchange(): lax.all_to_all(blocks, axes, 0, 0, tiled=True, axis_index_groups=groups)  44.9 us
    ppermute x3, waiting for transfers between devices, on_device(): near[level] = lax.ppermute(passed, ('dp', 'tensor'), across)  34.3 us
    pallas_call x3, Pallas kernels, pair_partial(): pl.pallas_call(body, grid_spec=pltpu.PrefetchScalarGridSpec(num_scalar_pr...  27.5 us
    pallas_call x4, Pallas kernels, features_first(): pl.pallas_call(body, grid_spec=pltpu.PrefetchScalarGridSpec(num_scalar_pr...  19.4 us
    all_to_all x1, blocking collectives, exchange(): lax.all_to_all(blocks, axes, 0, 0, tiled=True, axis_index_groups=groups)  16.7 us
    ppermute x3, starting transfers between devices, on_device(): near[level] = lax.ppermute(passed, ('dp', 'tensor'), across)  9.1 us
    dot_general x4, matrix products, on_device(): lax.dot_general(saved_inputs[k], proj_in[k], NT, preferred_element_type=F32)  7.15 us
  transfers between devices with their start and end apart: 17, of which 9 were waited for; matrix products, arithmetic and copies ran while one was open for 11% of the time, Pallas kernels for 19%

profile of v1, /device:TPU:0, one launch (start us, length us, event | category | flops | bytes accessed | tf_op | source)
XLA Modules:
  0.0 276.3 jit_solution(18202434930341210787)
XLA Ops:
  0.6 2.5 broadcast_in_dim.33
  3.2 5.5 %all-to-all-start = ((bf16[8,512,256]{2,1,0:T(8,128)(2,1)}), bf16[8,512,256]{2,1,0:T(8,128)(2,1)S(1)}, u32[]{:S(2)}, u32[]{:S(2)}) async-start(bf16[8,512,256]{2,1,0:T(8,128)(2,1)} %broadcast_in_dim.33), calls=%async_computation | async-start | bytes 4194304 | tf_op jit(solution)/shard_map/all_to_all | solution.py:147
  8.6 4.9 %shard_map.88 = (bf16[8,1024,256]{2,1,0:T(8,128)(2,1)}, bf16[4,1024,256]{2,1,0:T(8,128)(2,1)}) custom-call(s32[1]{0:T(128)} %bitcast.1.core_ref, bf16[4,1024,8,256]{3,2,1,0:T(8,128)(2,1)} %bitcast.127), custom_call_target="tpu_custom_call" | custom-call | bytes 10485760 | tf_op jit(solution)/shard_map/pallas_call | solution.py:22
  13.5 3.3 %collective-permute-start = (bf16[4,1024,256]{2,1,0:T(8,128)(2,1)}, bf16[4,1024,256]{2,1,0:T(8,128)(2,1)}, u32[]{:S(2)}, u32[]{:S(2)}) collective-permute-start(bf16[4,1024,256]{2,1,0:T(8,128)(2,1)} %get-tuple-element.11), channel_id=1, source_target_pairs={{0,68},{4,64},{8,76},{12,72},{16,84},{20,80},{24,92},{28,88},{32,1... | collective-permute-start | bytes 6291464 | tf_op jit(solution)/shard_map/ppermute | solution.py:177
  16.8 4.7 %shard_map.86 = (bf16[8,1024,256]{2,1,0:T(8,128)(2,1)}, bf16[4,1024,256]{2,1,0:T(8,128)(2,1)}) custom-call(s32[1]{0:T(128)} %bitcast.1.core_ref, bf16[4,1024,8,256]{3,2,1,0:T(8,128)(2,1)} %bitcast.128), custom_call_target="tpu_custom_call" | custom-call | bytes 10485760 | tf_op jit(solution)/shard_map/pallas_call | solution.py:22
  21.5 14.1 %all-to-all-done.g_ref = bf16[8,512,256]{2,1,0:T(8,128)(2,1)S(1)} async-done(((bf16[8,512,256]{2,1,0:T(8,128)(2,1)}), bf16[8,512,256]{2,1,0:T(8,128)(2,1)S(1)}, u32[]{:S(2)}, u32[]{:S(2)}) %all-to-all-start) | async-done | bytes 2097184 | tf_op jit(solution)/shard_map/all_to_all | solution.py:147
  35.6 5.6 %shard_map.87 = bf16[2,4,256,256]{3,2,1,0:T(8,128)(2,1)S(1)} custom-call(bf16[8,512,256]{2,1,0:T(8,128)(2,1)S(1)} %all-to-all-done.g_ref, bf16[8,1024,256]{2,1,0:T(8,128)(2,1)} %get-tuple-element.9.w_ref), custom_call_target="tpu_custom_call" | custom-call | flops 2147483648 | bytes 7340032 | tf_op jit(solution)/shard_map/pallas_call | solution.py:57
  41.2 1.0 copy-done.2
  42.2 5.6 %all-to-all-start.1 = ((bf16[8,256,256]{2,1,0:T(8,128)(2,1)}), bf16[8,256,256]{2,1,0:T(8,128)(2,1)}, u32[]{:S(2)}, u32[]{:S(2)}) async-start(bf16[8,256,256]{2,1,0:T(8,128)(2,1)} %bitcast.126), calls=%async_computation.1 | async-start | bytes 2097152 | tf_op jit(solution)/shard_map/all_to_all | solution.py:147
  47.7 5.0 %shard_map.90 = (bf16[8,1024,256]{2,1,0:T(8,128)(2,1)}, bf16[4,1024,256]{2,1,0:T(8,128)(2,1)}) custom-call(s32[1]{0:T(128)} %bitcast.1.core_ref, bf16[4,1024,8,256]{3,2,1,0:T(8,128)(2,1)} %bitcast.129), custom_call_target="tpu_custom_call" | custom-call | bytes 10485760 | tf_op jit(solution)/shard_map/pallas_call | solution.py:22
  52.7 3.3 %collective-permute-start.2 = (bf16[4,1024,256]{2,1,0:T(8,128)(2,1)}, bf16[4,1024,256]{2,1,0:T(8,128)(2,1)}, u32[]{:S(2)}, u32[]{:S(2)}) collective-permute-start(bf16[4,1024,256]{2,1,0:T(8,128)(2,1)} %get-tuple-element.13), channel_id=1, source_target_pairs={{0,68},{4,64},{8,76},{12,72},{16,84},{20,80},{24,92},{28,88},{32,1... | collective-permute-start | bytes 6291464 | tf_op jit(solution)/shard_map/ppermute | solution.py:177
  56.0 7.7 %collective-permute-done.near_ref = bf16[4,1024,256]{2,1,0:T(8,128)(2,1)} collective-permute-done((bf16[4,1024,256]{2,1,0:T(8,128)(2,1)}, bf16[4,1024,256]{2,1,0:T(8,128)(2,1)}, u32[]{:S(2)}, u32[]{:S(2)}) %collective-permute-start) | collective-permute-done | bytes 2097184 | tf_op jit(solution)/shard_map/ppermute | solution.py:177
  63.6 1.4 convert_reduce_fusion
  65.9 1.0 broadcast_in_dim.34
  66.9 4.8 %all-to-all-start.2 = ((bf16[4,2,256,256]{3,2,1,0:T(8,128)(2,1)}), bf16[4,2,256,256]{3,2,1,0:T(8,128)(2,1)S(1)}, u32[]{:S(2)}, u32[]{:S(2)}) async-start(bf16[4,2,256,256]{3,2,1,0:T(8,128)(2,1)} %broadcast_in_dim.34), calls=%async_computation.2 | async-start | bytes 2097152 | tf_op jit(solution)/shard_map/all_to_all | solution.py:147
  72.6 4.8 %shard_map.92 = (bf16[8,1024,256]{2,1,0:T(8,128)(2,1)}, bf16[4,1024,256]{2,1,0:T(8,128)(2,1)}) custom-call(s32[1]{0:T(128)} %bitcast.1.core_ref, bf16[4,1024,8,256]{3,2,1,0:T(8,128)(2,1)} %bitcast.130), custom_call_target="tpu_custom_call" | custom-call | bytes 10485760 | tf_op jit(solution)/shard_map/pallas_call | solution.py:22
  77.4 2.5 collective-permute-start.4
  80.2 1.8 convolution_convert_fusion.4
  82.0 26.6 %collective-permute-done.2.near_ref = bf16[4,1024,256]{2,1,0:T(8,128)(2,1)} collective-permute-done((bf16[4,1024,256]{2,1,0:T(8,128)(2,1)}, bf16[4,1024,256]{2,1,0:T(8,128)(2,1)}, u32[]{:S(2)}, u32[]{:S(2)}) %collective-permute-start.2) | collective-permute-done | bytes 2097184 | tf_op jit(solution)/shard_map/ppermute | solution.py:177
  108.6 9.1 %shard_map.89 = bf16[4,2,256,256]{3,2,1,0:T(8,128)(2,1)} custom-call(s32[3]{0:T(128)S(1)} %pad_add_fusion.s_ref, bf16[8,256,256]{2,1,0:T(8,128)(2,1)S(1)} %bitcast.120, bf16[8,1024,256]{2,1,0:T(8,128)(2,1)} %get-tuple-element.10.own_ref, bf16[4,1024,256]{2,1,0:T(8,128)(2,1)} %collective-permute-done.near_ref, ...), custom_call_target="tpu_custom_call" | custom-call | flops 2147483648 | bytes 10485760 | tf_op jit(solution)/shard_map/pallas_call | solution.py:128
  117.7 5.4 %all-to-all-start.3 = ((bf16[4,2,256,256]{3,2,1,0:T(8,128)(2,1)}), bf16[4,2,256,256]{3,2,1,0:T(8,128)(2,1)S(1)}, u32[]{:S(2)}, u32[]{:S(2)}) async-start(bf16[4,2,256,256]{3,2,1,0:T(8,128)(2,1)} %shard_map.89), calls=%async_computation.3 | async-start | bytes 2097152 | tf_op jit(solution)/shard_map/all_to_all | solution.py:147
  123.2 1.8 convolution_convert_fusion.3
  125.0 1.8 convolution_convert_fusion
  127.6 11.3 %all-to-all-done.3 = bf16[4,2,256,256]{3,2,1,0:T(8,128)(2,1)S(1)} async-done(((bf16[4,2,256,256]{3,2,1,0:T(8,128)(2,1)}), bf16[4,2,256,256]{3,2,1,0:T(8,128)(2,1)S(1)}, u32[]{:S(2)}, u32[]{:S(2)}) %all-to-all-start.3) | async-done | bytes 1048608 | tf_op jit(solution)/shard_map/all_to_all | solution.py:147
  139.1 1.1 fusion.19
  140.2 1.1 broadcast_in_dim.35
  141.2 4.8 %all-to-all-start.4 = ((bf16[4,2,256,256]{3,2,1,0:T(8,128)(2,1)}), bf16[4,2,256,256]{3,2,1,0:T(8,128)(2,1)S(1)}, u32[]{:S(2)}, u32[]{:S(2)}) async-start(bf16[4,2,256,256]{3,2,1,0:T(8,128)(2,1)} %broadcast_in_dim.35), calls=%async_computation.4 | async-start | bytes 2097152 | tf_op jit(solution)/shard_map/all_to_all | solution.py:147
  146.9 1.8 convolution_convert_fusion.2
  148.7 1.1 maximum_select_fusion
  150.6 10.1 %all-to-all-done.4 = bf16[4,2,256,256]{3,2,1,0:T(8,128)(2,1)S(1)} async-done(((bf16[4,2,256,256]{3,2,1,0:T(8,128)(2,1)}), bf16[4,2,256,256]{3,2,1,0:T(8,128)(2,1)S(1)}, u32[]{:S(2)}, u32[]{:S(2)}) %all-to-all-start.4) | async-done | bytes 1048608 | tf_op jit(solution)/shard_map/all_to_all | solution.py:147
  160.7 9.2 %shard_map.91 = bf16[4,2,256,256]{3,2,1,0:T(8,128)(2,1)} custom-call(s32[3]{0:T(128)S(1)} %pad_add_fusion.s_ref, bf16[8,256,256]{2,1,0:T(8,128)(2,1)S(1)} %bitcast.121, bf16[8,1024,256]{2,1,0:T(8,128)(2,1)} %get-tuple-element.12.own_ref, bf16[4,1024,256]{2,1,0:T(8,128)(2,1)} %collective-permute-done.2.near_ref, ...), custom_call_target="tpu_custom_call" | custom-call | flops 2147483648 | bytes 10485760 | tf_op jit(solution)/shard_map/pallas_call | solution.py:128
  169.8 3.5 %all-to-all-start.5 = ((bf16[4,2,256,256]{3,2,1,0:T(8,128)(2,1)}), bf16[4,2,256,256]{3,2,1,0:T(8,128)(2,1)S(1)}, u32[]{:S(2)}, u32[]{:S(2)}) async-start(bf16[4,2,256,256]{3,2,1,0:T(8,128)(2,1)} %shard_map.91), calls=%async_computation.5 | async-start | bytes 2097152 | tf_op jit(solution)/shard_map/all_to_all | solution.py:147
  173.4 1.0 fusion
  175.3 1.1 fusion.16
  176.4 1.1 fusion.1
  178.3 8.7 %all-to-all-done.5 = bf16[4,2,256,256]{3,2,1,0:T(8,128)(2,1)S(1)} async-done(((bf16[4,2,256,256]{3,2,1,0:T(8,128)(2,1)}), bf16[4,2,256,256]{3,2,1,0:T(8,128)(2,1)S(1)}, u32[]{:S(2)}, u32[]{:S(2)}) %all-to-all-start.5) | async-done | bytes 1048608 | tf_op jit(solution)/shard_map/all_to_all | solution.py:147
  187.2 1.1 fusion.35
  192.2 3.9 %all-to-all-start.8 = ((bf16[32,64,128]{2,1,0:T(8,128)(2,1)}), bf16[32,64,128]{2,1,0:T(8,128)(2,1)S(1)}, u32[]{:S(2)}, u32[]{:S(2)}) async-start(bf16[32,64,128]{2,1,0:T(8,128)(2,1)} %bitcast.45), calls=%async_computation.8 | async-start | bytes 1048576 | tf_op jit(solution)/shard_map/all_to_all | solution.py:147
  196.2 10.0 %all-to-all-done.8 = bf16[32,64,128]{2,1,0:T(8,128)(2,1)S(1)} async-done(((bf16[32,64,128]{2,1,0:T(8,128)(2,1)}), bf16[32,64,128]{2,1,0:T(8,128)(2,1)S(1)}, u32[]{:S(2)}, u32[]{:S(2)}) %all-to-all-start.8) | async-done | bytes 524320 | tf_op jit(solution)/shard_map/all_to_all | solution.py:147
  207.1 16.7 %all_to_all.60 = f32[32,1,4096]{2,1,0:T(1,128)S(1)} all-to-all(f32[32,1,4096]{2,1,0:T(1,128)S(1)} %broadcast_in_dim.40), channel_id=1, replica_groups=mesh['dp'=4,'tensor'=8,'layer'=4] {'dp','tensor'}, dimensions={0} | all-to-all | bytes 1048576 | tf_op jit(solution)/shard_map/all_to_all | solution.py:147
  223.8 1.0 broadcast_in_dim.36
  224.8 3.5 %all-to-all-start.6 = ((bf16[4,2,256,256]{3,2,1,0:T(8,128)(2,1)}), bf16[4,2,256,256]{3,2,1,0:T(8,128)(2,1)S(1)}, u32[]{:S(2)}, u32[]{:S(2)}) async-start(bf16[4,2,256,256]{3,2,1,0:T(8,128)(2,1)} %broadcast_in_dim.36), calls=%async_computation.6 | async-start | bytes 2097152 | tf_op jit(solution)/shard_map/all_to_all | solution.py:147
  228.8 1.0 fusion.3
  229.7 14.4 %all-to-all-done.6 = bf16[4,2,256,256]{3,2,1,0:T(8,128)(2,1)S(1)} async-done(((bf16[4,2,256,256]{3,2,1,0:T(8,128)(2,1)}), bf16[4,2,256,256]{3,2,1,0:T(8,128)(2,1)S(1)}, u32[]{:S(2)}, u32[]{:S(2)}) %all-to-all-start.6) | async-done | bytes 1048608 | tf_op jit(solution)/shard_map/all_to_all | solution.py:147
  244.1 3.2 %all-to-all-start.10 = ((f32[4,1,128]{2,1,0:T(1,128)}), f32[4,1,128]{2,1,0:T(1,128)S(1)}, u32[]{:S(2)}, u32[]{:S(2)}) async-start(f32[4,1,128]{2,1,0:T(1,128)} %bitcast.48), calls=%async_computation.10 | async-start | bytes 4096 | tf_op jit(solution)/shard_map/all_to_all | solution.py:147
  247.4 9.2 %shard_map.93 = bf16[2,4,256,256]{3,2,1,0:T(8,128)(2,1)} custom-call(s32[3]{0:T(128)S(1)} %pad_add_fusion.s_ref, bf16[8,256,256]{2,1,0:T(8,128)(2,1)S(1)} %bitcast.122, bf16[8,1024,256]{2,1,0:T(8,128)(2,1)} %get-tuple-element.14.own_ref, bf16[4,1024,256]{2,1,0:T(8,128)(2,1)} %collective-permute-done.4.near_ref, ...), custom_call_target="tpu_custom_call" | custom-call | flops 2147483648 | bytes 10485760 | tf_op jit(solution)/shard_map/pallas_call | solution.py:128
  256.5 4.8 %all-to-all-start.7 = ((bf16[8,256,256]{2,1,0:T(8,128)(2,1)}), bf16[8,256,256]{2,1,0:T(8,128)(2,1)S(1)}, u32[]{:S(2)}, u32[]{:S(2)}) async-start(bf16[8,256,256]{2,1,0:T(8,128)(2,1)} %bitcast.11), calls=%async_computation.7 | async-start | bytes 2097152 | tf_op jit(solution)/shard_map/all_to_all | solution.py:147
  261.8 13.6 %all-to-all-done.7 = bf16[8,256,256]{2,1,0:T(8,128)(2,1)S(1)} async-done(((bf16[8,256,256]{2,1,0:T(8,128)(2,1)}), bf16[8,256,256]{2,1,0:T(8,128)(2,1)S(1)}, u32[]{:S(2)}, u32[]{:S(2)}) %all-to-all-start.7) | async-done | bytes 1048608 | tf_op jit(solution)/shard_map/all_to_all | solution.py:147
  (67 shorter events, 13.2 us)
Async XLA Ops:
  0.6 228.1 %copy-start = (bf16[1,128,4096]{2,1,0:T(8,128)(2,1)S(1)}, bf16[1,128,4096]{2,1,0:T(8,128)(2,1)}, u32[]{:S(2)}) copy-start(bf16[1,128,4096]{2,1,0:T(8,128)(2,1)} %param.12) | copy-start | bytes 3145732
  3.2 32.5 %all-to-all-start = ((bf16[8,512,256]{2,1,0:T(8,128)(2,1)}), bf16[8,512,256]{2,1,0:T(8,128)(2,1)S(1)}, u32[]{:S(2)}, u32[]{:S(2)}) async-start(bf16[8,512,256]{2,1,0:T(8,128)(2,1)} %broadcast_in_dim.33), calls=%async_computation | async-start | bytes 4194304 | tf_op jit(solution)/shard_map/all_to_all | solution.py:147
  13.5 50.1 %collective-permute-start = (bf16[4,1024,256]{2,1,0:T(8,128)(2,1)}, bf16[4,1024,256]{2,1,0:T(8,128)(2,1)}, u32[]{:S(2)}, u32[]{:S(2)}) collective-permute-start(bf16[4,1024,256]{2,1,0:T(8,128)(2,1)} %get-tuple-element.11), channel_id=1, source_target_pairs={{0,68},{4,64},{8,76},{12,72},{16,84},{20,80},{24,92},{28,88},{32,1... | collective-permute-start | bytes 6291464 | tf_op jit(solution)/shard_map/ppermute | solution.py:177
  35.6 29.5 %copy-start.1 = (bf16[8,512,256]{2,1,0:T(8,128)(2,1)}, bf16[8,512,256]{2,1,0:T(8,128)(2,1)S(1)}, u32[]{:S(2)}) copy-start(bf16[8,512,256]{2,1,0:T(8,128)(2,1)S(1)} %all-to-all-done.g_ref) | copy-start | bytes 6291460
  41.2 1.0 copy-start.2
  42.2 21.5 %all-to-all-start.1 = ((bf16[8,256,256]{2,1,0:T(8,128)(2,1)}), bf16[8,256,256]{2,1,0:T(8,128)(2,1)}, u32[]{:S(2)}, u32[]{:S(2)}) async-start(bf16[8,256,256]{2,1,0:T(8,128)(2,1)} %bitcast.126), calls=%async_computation.1 | async-start | bytes 2097152 | tf_op jit(solution)/shard_map/all_to_all | solution.py:147
  52.7 55.9 %collective-permute-start.2 = (bf16[4,1024,256]{2,1,0:T(8,128)(2,1)}, bf16[4,1024,256]{2,1,0:T(8,128)(2,1)}, u32[]{:S(2)}, u32[]{:S(2)}) collective-permute-start(bf16[4,1024,256]{2,1,0:T(8,128)(2,1)} %get-tuple-element.13), channel_id=1, source_target_pairs={{0,68},{4,64},{8,76},{12,72},{16,84},{20,80},{24,92},{28,88},{32,1... | collective-permute-start | bytes 6291464 | tf_op jit(solution)/shard_map/ppermute | solution.py:177
  63.6 45.0 %collective-permute-start.1 = (bf16[4,1024,256]{2,1,0:T(8,128)(2,1)}, bf16[4,1024,256]{2,1,0:T(8,128)(2,1)}, u32[]{:S(2)}, u32[]{:S(2)}) collective-permute-start(bf16[4,1024,256]{2,1,0:T(8,128)(2,1)} %collective-permute-done.near_ref), channel_id=1, source_target_pairs={{0,32},{32,0},{64,96},{96,64},{1,33},{33,1},{65,97},{97,65},{2,34}... | collective-permute-start | bytes 6291464 | tf_op jit(solution)/shard_map/ppermute | solution.py:178
  65.1 0.8 copy-start.3
  65.1 6.6 %copy-start.8 = (bf16[4,64,256]{2,1,0:T(8,128)(2,1)S(1)}, bf16[4,64,256]{2,1,0:T(8,128)(2,1)}, u32[]{:S(2)}) copy-start(bf16[4,64,256]{2,1,0:T(8,128)(2,1)} %param.11) | copy-start | bytes 393220
  66.9 41.7 %all-to-all-start.2 = ((bf16[4,2,256,256]{3,2,1,0:T(8,128)(2,1)}), bf16[4,2,256,256]{3,2,1,0:T(8,128)(2,1)S(1)}, u32[]{:S(2)}, u32[]{:S(2)}) async-start(bf16[4,2,256,256]{3,2,1,0:T(8,128)(2,1)} %broadcast_in_dim.34), calls=%async_computation.2 | async-start | bytes 2097152 | tf_op jit(solution)/shard_map/all_to_all | solution.py:147
  72.4 7.7 %copy-start.11 = (s32[4]{0:T(128)S(1)}, s32[4]{0:T(128)}, u32[]{:S(2)}) copy-start(s32[4]{0:T(128)} %param.13) | copy-start | bytes 52
  72.4 7.8 %copy-start.10 = (bf16[4,64,256]{2,1,0:T(8,128)(2,1)S(1)}, bf16[4,64,256]{2,1,0:T(8,128)(2,1)}, u32[]{:S(2)}) copy-start(bf16[4,64,256]{2,1,0:T(8,128)(2,1)} %param.10) | copy-start | bytes 393220
  72.4 76.3 %collective-permute-start.6 = (bf16[3,64,256]{2,1,0:T(8,128)(2,1)}, bf16[3,64,256]{2,1,0:T(8,128)(2,1)}, u32[]{:S(2)}, u32[]{:S(2)}) collective-permute-start(bf16[3,64,256]{2,1,0:T(8,128)(2,1)} %get-tuple-element.19), channel_id=1, source_target_pairs={{0,4},{4,0},{8,12},{12,8},{16,20},{20,16},{24,28},{28,24},{1,5},{5... | collective-permute-start | bytes 294920 | tf_op jit(solution)/shard_map/ppermute | solution.py:179
  77.4 118.7 %collective-permute-start.4 = (bf16[4,1024,256]{2,1,0:T(8,128)(2,1)}, bf16[4,1024,256]{2,1,0:T(8,128)(2,1)}, u32[]{:S(2)}, u32[]{:S(2)}) collective-permute-start(bf16[4,1024,256]{2,1,0:T(8,128)(2,1)} %get-tuple-element.15), channel_id=1, source_target_pairs={{0,68},{4,64},{8,76},{12,72},{16,84},{20,80},{24,92},{28,88},{32,1... | collective-permute-start | bytes 6291464 | tf_op jit(solution)/shard_map/ppermute | solution.py:177
  108.6 42.0 %collective-permute-start.3 = (bf16[4,1024,256]{2,1,0:T(8,128)(2,1)}, bf16[4,1024,256]{2,1,0:T(8,128)(2,1)}, u32[]{:S(2)}, u32[]{:S(2)}) collective-permute-start(bf16[4,1024,256]{2,1,0:T(8,128)(2,1)} %collective-permute-done.2.near_ref), channel_id=1, source_target_pairs={{0,32},{32,0},{64,96},{96,64},{1,33},{33,1},{65,97},{97,65},{2,34}... | collective-permute-start | bytes 6291464 | tf_op jit(solution)/shard_map/ppermute | solution.py:178
  117.7 9.0 %copy-start.6 = (bf16[512,256]{1,0:T(8,128)(2,1)S(1)}, bf16[512,256]{1,0:T(8,128)(2,1)}, u32[]{:S(2)}) copy-start(bf16[512,256]{1,0:T(8,128)(2,1)} %param.8) | copy-start | bytes 786436
  117.7 21.4 %copy-start.4 = (f32[2,256,256]{2,1,0:T(8,128)S(1)}, f32[2,256,256]{2,1,0:T(8,128)}, u32[]{:S(2)}) copy-start(f32[2,256,256]{2,1,0:T(8,128)} %copy-done.3) | copy-start | bytes 1572868
  117.7 21.2 %all-to-all-start.3 = ((bf16[4,2,256,256]{3,2,1,0:T(8,128)(2,1)}), bf16[4,2,256,256]{3,2,1,0:T(8,128)(2,1)S(1)}, u32[]{:S(2)}, u32[]{:S(2)}) async-start(bf16[4,2,256,256]{3,2,1,0:T(8,128)(2,1)} %shard_map.89), calls=%async_computation.3 | async-start | bytes 2097152 | tf_op jit(solution)/shard_map/all_to_all | solution.py:147
  140.2 1.1 copy-start.5
  141.2 19.4 %all-to-all-start.4 = ((bf16[4,2,256,256]{3,2,1,0:T(8,128)(2,1)}), bf16[4,2,256,256]{3,2,1,0:T(8,128)(2,1)S(1)}, u32[]{:S(2)}, u32[]{:S(2)}) async-start(bf16[4,2,256,256]{3,2,1,0:T(8,128)(2,1)} %broadcast_in_dim.35), calls=%async_computation.4 | async-start | bytes 2097152 | tf_op jit(solution)/shard_map/all_to_all | solution.py:147
  149.8 0.8 copy-start.7
  169.8 17.2 %all-to-all-start.5 = ((bf16[4,2,256,256]{3,2,1,0:T(8,128)(2,1)}), bf16[4,2,256,256]{3,2,1,0:T(8,128)(2,1)S(1)}, u32[]{:S(2)}, u32[]{:S(2)}) async-start(bf16[4,2,256,256]{3,2,1,0:T(8,128)(2,1)} %shard_map.91), calls=%async_computation.5 | async-start | bytes 2097152 | tf_op jit(solution)/shard_map/all_to_all | solution.py:147
  187.1 3.2 %copy-start.9 = (bf16[512,64]{0,1:T(8,128)(2,1)S(1)}, bf16[512,64]{0,1:T(8,128)(2,1)}, u32[]{:S(2)}) copy-start(bf16[512,64]{0,1:T(8,128)(2,1)} %convolution_convert_fusion.4) | copy-start | bytes 196612
  192.2 14.0 %all-to-all-start.8 = ((bf16[32,64,128]{2,1,0:T(8,128)(2,1)}), bf16[32,64,128]{2,1,0:T(8,128)(2,1)S(1)}, u32[]{:S(2)}, u32[]{:S(2)}) async-start(bf16[32,64,128]{2,1,0:T(8,128)(2,1)} %bitcast.45), calls=%async_computation.8 | async-start | bytes 1048576 | tf_op jit(solution)/shard_map/all_to_all | solution.py:147
  196.1 51.3 %collective-permute-start.5 = (bf16[4,1024,256]{2,1,0:T(8,128)(2,1)}, bf16[4,1024,256]{2,1,0:T(8,128)(2,1)}, u32[]{:S(2)}, u32[]{:S(2)}) collective-permute-start(bf16[4,1024,256]{2,1,0:T(8,128)(2,1)} %collective-permute-done.4.near_ref), channel_id=1, source_target_pairs={{0,32},{32,0},{64,96},{96,64},{1,33},{33,1},{65,97},{97,65},{2,34}... | collective-permute-start | bytes 6291464 | tf_op jit(solution)/shard_map/ppermute | solution.py:178
  224.8 19.3 %all-to-all-start.6 = ((bf16[4,2,256,256]{3,2,1,0:T(8,128)(2,1)}), bf16[4,2,256,256]{3,2,1,0:T(8,128)(2,1)S(1)}, u32[]{:S(2)}, u32[]{:S(2)}) async-start(bf16[4,2,256,256]{3,2,1,0:T(8,128)(2,1)} %broadcast_in_dim.36), calls=%async_computation.6 | async-start | bytes 2097152 | tf_op jit(solution)/shard_map/all_to_all | solution.py:147
  244.1 12.4 %all-to-all-start.10 = ((f32[4,1,128]{2,1,0:T(1,128)}), f32[4,1,128]{2,1,0:T(1,128)S(1)}, u32[]{:S(2)}, u32[]{:S(2)}) async-start(f32[4,1,128]{2,1,0:T(1,128)} %bitcast.48), calls=%async_computation.10 | async-start | bytes 4096 | tf_op jit(solution)/shard_map/all_to_all | solution.py:147
  256.5 18.9 %all-to-all-start.7 = ((bf16[8,256,256]{2,1,0:T(8,128)(2,1)}), bf16[8,256,256]{2,1,0:T(8,128)(2,1)S(1)}, u32[]{:S(2)}, u32[]{:S(2)}) async-start(bf16[8,256,256]{2,1,0:T(8,128)(2,1)} %bitcast.11), calls=%async_computation.7 | async-start | bytes 2097152 | tf_op jit(solution)/shard_map/all_to_all | solution.py:147

commit v2 on v1

v2 whole, which is shorter than its diff:
```python
import jax
import jax.numpy as jnp
from jax import lax
from jax.experimental import pallas as pl
from jax.experimental.pallas import tpu as pltpu
from jax.sharding import PartitionSpec as P

NT = (((1,), (1,)), ((), ()))
F32 = jnp.float32
BF16 = jnp.bfloat16
WIDE = pl.BlockSpec(memory_space=pltpu.VMEM)
SCALARS = pl.BlockSpec(memory_space=pltpu.SMEM)
after = lax.optimization_barrier


def limit(mib):
    return pltpu.CompilerParams(vmem_limit_bytes=mib << 20)


def features_first(weights, level, core):
    _, rows, cells, width = weights.shape
    step, half = 512, cells // 2

    def body(core_ref, w_ref, o_ref, s_ref):
        o_ref[...] = jnp.swapaxes(w_ref[0], 0, 1)
        s_ref[...] = o_ref[pl.ds(half * core_ref[0], half)]

    return pl.pallas_call(
        body,
        grid_spec=pltpu.PrefetchScalarGridSpec(
            num_scalar_prefetch=1,
            grid=(rows // step,),
            in_specs=[pl.BlockSpec((1, step, cells, width), lambda n, c: (level, n, 0, 0))],
            out_specs=[
                pl.BlockSpec((cells, step, width), lambda n, c: (0, n, 0)),
                pl.BlockSpec((half, step, width), lambda n, c: (0, n, 0)),
            ],
        ),
        out_shape=[
            jax.ShapeDtypeStruct((cells, rows, width), weights.dtype),
            jax.ShapeDtypeStruct((half, rows, width), weights.dtype),
        ],
        compiler_params=limit(20),
        cost_estimate=pl.CostEstimate(
            flops=0, bytes_accessed=5 * rows * cells * width, transcendentals=0
        ),
    )(core, weights)


def first_partial(gathered, weight, extra):
    cells, tokens, width = gathered.shape
    rows = weight.shape[1]
    groups = rows // width
    half = tokens // 2
    tail = extra.shape[1]

    def body(g_ref, w_ref, e_ref, o_ref):
        for n in range(groups):
            total = None
            for a in range(cells):
                term = lax.dot_general(
                    g_ref[a], w_ref[a, n * width : (n + 1) * width], NT,
                    preferred_element_type=F32,
                )
                total = term if total is None else total + term
            o_ref[n, :half] = total[:half].astype(o_ref.dtype)
            o_ref[groups + n, :half] = total[half:].astype(o_ref.dtype)
        o_ref[:, half:] = e_ref[...]

    return pl.pallas_call(
        body,
        in_specs=[WIDE, WIDE, WIDE],
        out_specs=WIDE,
        out_shape=jax.ShapeDtypeStruct((2 * groups, half + tail, width), BF16),
        compiler_params=limit(16),
        cost_estimate=pl.CostEstimate(
            flops=2 * cells * width * rows * tokens,
            bytes_accessed=2 * (cells * width * (rows + tokens) + rows * tokens),
            transcendentals=0,
        ),
    )(gathered, weight, extra)


def pair_partial(place, gathered, own, near, far, kept=None, extra=None):
    n_y, _, width = gathered.shape
    cells, rows, _ = own.shape
    tokens = width
    groups = rows // width
    half = cells // 2
    last = kept is not None
    tail = 0 if extra is None else extra.shape[1]
    operands = [gathered, own, near, far]
    operands += [kept] if last else []
    operands += [] if extra is None else [extra]
    blocks, deep = (2 * groups, tokens) if last else (groups, 2 * tokens)

    def body(s_ref, g_ref, own_ref, near_ref, far_ref, *refs):
        o_ref = refs[-1]
        x, core, b = s_ref[0], s_ref[1], s_ref[2]

        def piece(cell):
            return g_ref[cell // 2, (cell % 2) * tokens : (cell % 2 + 1) * tokens]

        def put(total, column, n):
            if last:
                mine = refs[0][column]
                total = total + jnp.where(n == b, mine, jnp.zeros_like(mine))
                o_ref[groups * column + n, :tokens] = total.astype(o_ref.dtype)
            else:
                start = pl.multiple_of(column * tokens, tokens)
                o_ref[n, pl.ds(start, tokens)] = total.astype(o_ref.dtype)

        for n in range(groups):
            cut = slice(n * width, (n + 1) * width)
            total = None
            for a in range(cells):
                term = lax.dot_general(
                    piece(a), own_ref[a, cut], NT, preferred_element_type=F32
                )
                total = term if total is None else total + term
            put(total, x, n)
        for n in range(groups):
            cut = slice(n * width, (n + 1) * width)
            total = None
            for ref, first in ((near_ref, core), (far_ref, 1 - core)):
                for i in range(half):
                    values = g_ref[
                        (half // 2) * first + i // 2, (i % 2) * tokens : (i % 2 + 1) * tokens
                    ]
                    term = lax.dot_general(
                        values, ref[i, cut], NT, preferred_element_type=F32
                    )
                    total = term if total is None else total + term
            put(total, 1 - x, n)
        if tail:
            for k in range(blocks):
                o_ref[k, deep:] = refs[-2][k % extra.shape[0]]

    return pl.pallas_call(
        body,
        in_specs=[SCALARS] + [WIDE] * len(operands),
        out_specs=WIDE,
        out_shape=jax.ShapeDtypeStruct((blocks, deep + tail, width), BF16),
        compiler_params=limit(16),
        cost_estimate=pl.CostEstimate(
            flops=4 * cells * width * rows * tokens,
            bytes_accessed=2 * (cells * width * (2 * rows + tokens) + 2 * rows * tokens),
            transcendentals=0,
        ),
    )(place, *operands)


def out_factors(grad, proj):
    def body(g_ref, p_ref, o_ref):
        total = lax.dot_general(p_ref[0], g_ref[0], NT, preferred_element_type=F32)
        total += lax.dot_general(p_ref[1], g_ref[1], NT, preferred_element_type=F32)
        o_ref[...] = total.astype(o_ref.dtype)

    return pl.pallas_call(
        body,
        in_specs=[WIDE, WIDE],
        out_specs=WIDE,
        out_shape=jax.ShapeDtypeStruct((proj.shape[1], grad.shape[1]), BF16),
        compiler_params=limit(8),
    )(grad, proj)


def block_parts(layer_of, outs, ins):
    layers, rank, tokens = outs.shape
    low = rank // 2

    def body(l_ref, a_ref, b_ref, o_ref):
        for o in range(layers):
            part = lax.dot_general(
                a_ref[l_ref[o]], b_ref[l_ref[o]], NT, preferred_element_type=F32
            ).astype(o_ref.dtype)
            side = jnp.concatenate([part[:low], part[low:]], axis=1)
            row, lane = low * (o // 2), 2 * rank * (o % 2)
            o_ref[row : row + low, lane : lane + 2 * rank] = side

    return pl.pallas_call(
        body,
        in_specs=[SCALARS, WIDE, WIDE],
        out_specs=WIDE,
        out_shape=jax.ShapeDtypeStruct((low * layers // 2, 4 * rank), BF16),
        compiler_params=limit(8),
    )(layer_of, outs, ins)


def exchange(blocks, axes, groups=None):
    return lax.all_to_all(blocks, axes, 0, 0, tiled=True, axis_index_groups=groups)


def spread(value, axes, peers, groups=None):
    return exchange(jnp.broadcast_to(value, (peers, *value.shape)), axes, groups)


def on_device(saved_inputs, output_grad, weights, proj_in, proj_out, query_grads, owner_map):
    layers, tokens, width = saved_inputs.shape
    rank = proj_in.shape[1]
    rows = weights.shape[1]
    n_dp, n_tensor, n_layer = (lax.axis_size(k) for k in ("dp", "tensor", "layer"))
    n_y = n_tensor // 2
    half = tokens // 2
    t, b = lax.axis_index("tensor"), lax.axis_index("layer")
    x, y = t % 2, t // 2
    core = lax.axis_index("dp") % 2
    place = jnp.stack([x, core, b]).astype(jnp.int32)
    along_y = [[2 * k + j for k in range(n_y)] for j in range(2)]
    along_xz = [[2 * n_layer * k + j for j in range(2 * n_layer)] for k in range(n_y)]
    within_y = [
        [
            (d * n_tensor + 2 * k + j) * n_layer + z
            for d in range(n_dp)
            for j in range(2)
            for z in range(n_layer)
        ]
        for k in range(n_y)
    ]
    across = [
        (d * n_tensor + k, (d ^ 2) * n_tensor + (k ^ 1)) for d in range(n_dp) for k in range(n_tensor)
    ]
    beside = [(k, k ^ 1) for k in range(n_tensor)]
    other_core = [(d, d ^ 1) for d in range(n_dp)]
    flat = pltpu.with_memory_space_constraint(
        weights.reshape(layers, rows, n_tensor, width), pltpu.HBM
    )
    top = layers - 1
    owners = jnp.arange(n_layer, dtype=jnp.int32)
    layer_of = jnp.sum(
        owners[None, :] * (owner_map[None, :] == owners[:, None]).astype(jnp.int32), axis=1
    )

    gathered = spread(output_grad, "tensor", n_tensor)
    own, passed, near, far = ([None] * layers for _ in range(4))
    for level in (2, 3, 1, 0):
        own[level], passed[level] = features_first(flat, level, core.astype(jnp.int32).reshape(1))
    near[2] = lax.ppermute(passed[2], ("dp", "tensor"), across)
    other_proj = lax.ppermute(proj_out, "tensor", beside)
    pair_proj = jnp.where(
        x == 0, jnp.stack([proj_out, other_proj], 1), jnp.stack([other_proj, proj_out], 1)
    )
    in_parts = jnp.stack(
        [
            lax.dot_general(proj_in[k], saved_inputs[k], NT, preferred_element_type=F32).astype(BF16)
            for k in range(layers)
        ]
    )
    in_parts = jnp.swapaxes(in_parts.reshape(layers, rank, 2, half), 1, 2)
    in_parts = jnp.swapaxes(in_parts, 0, 1).reshape(2 * layers, rank, half)

    partial = first_partial(gathered, own[top], in_parts)
    arrived = exchange(partial, ("tensor", "layer"), along_xz)
    arrived = arrived.reshape(2, n_layer, half + rank, width)
    start = lax.dynamic_slice(
        gathered.reshape(n_y, 2, 2, half, width), (y, 0, x, 0, 0), (1, 2, 1, half, width)
    ).reshape(2, half, width)
    total = start.astype(F32) + arrived[:, :, :half].astype(F32).sum(axis=1)
    in_mine = arrived[:, :, half:].astype(F32).sum(axis=(0, 1)).astype(BF16)
    grad = total.astype(BF16)
    outs = [None] * layers
    outs[3] = out_factors(start, pair_proj[3])

    outs[2] = out_factors(grad, pair_proj[2])
    grad, outs[2], outs[3] = after((grad, outs[2], outs[3]))
    passed[1], _ = after((passed[1], grad))
    near[1] = lax.ppermute(passed[1], "tensor", beside)
    near[2], _ = after((near[2], grad))
    far[2] = lax.ppermute(near[2], "dp", other_core)
    passed[0], _ = after((passed[0], near[2]))
    near[0] = lax.ppermute(passed[0], ("dp", "tensor"), across)
    gathered = spread(
        jnp.concatenate([grad.reshape(2 * half, width), in_mine]), "tensor", n_y, along_y
    )
    in_whole = gathered[:, 2 * half :].astype(F32).sum(axis=0).astype(BF16)
    partial = pair_partial(
        place, gathered, own[2], near[2], far[2], extra=in_whole.reshape(1, rank, half)
    )
    arrived = exchange(partial, "layer")
    ins = arrived[:, 2 * half :]
    total = total + arrived[:, : 2 * half].astype(F32).sum(axis=0).reshape(2, half, width)
    grad = total.astype(BF16)

    outs[1] = out_factors(grad, pair_proj[1])
    grad, outs[1] = after((grad, outs[1]))
    gathered = spread(grad.reshape(2 * half, width), "tensor", n_y, along_y)
    near[1], _ = after((near[1], gathered))
    far[1] = lax.ppermute(near[1], "dp", other_core)
    partial = pair_partial(place, gathered, own[1], near[1], far[1])
    near[0], _ = after((near[0], partial))
    far[0] = lax.ppermute(near[0], "dp", other_core)
    arrived = exchange(partial, "layer")
    total = total + arrived.astype(F32).sum(axis=0).reshape(2, half, width)
    grad = total.astype(BF16)

    outs[0] = out_factors(grad, pair_proj[0])
    blocks = block_parts(layer_of, jnp.stack(outs), ins)
    gathered = spread(
        jnp.concatenate([grad.reshape(2 * half, width), blocks]), "tensor", n_y, along_y
    )
    summed = gathered[:, 2 * half :].astype(F32).sum(axis=0).astype(BF16)
    summed = jnp.swapaxes(summed.reshape(2, rank // 2, 2, 2 * rank), 1, 2)
    summed = summed.reshape(n_layer, rank // 2, 2 * rank)
    every = exchange(
        jnp.broadcast_to(summed, (n_dp * 2, *summed.shape)).reshape(
            n_dp * 2 * n_layer, rank // 2, 2 * rank
        ),
        ("dp", "tensor", "layer"),
        within_y,
    )
    whole = every.reshape(n_dp, 2 * n_layer, rank // 2, 2, rank).astype(F32).sum(axis=1)
    whole = jnp.swapaxes(whole, 1, 2).reshape(n_dp, rank * rank).astype(BF16)
    scored = lax.dot_general(whole, query_grads[0], NT, preferred_element_type=F32)
    high = scored.astype(BF16)
    low = (scored - high.astype(F32)).astype(BF16)
    carried = jnp.concatenate([high, low], axis=1)[:, None, :]
    carried = jnp.broadcast_to(carried, (n_dp, 16, width))
    partial = pair_partial(place, gathered, own[0], near[0], far[0], kept=total, extra=carried)
    arrived = exchange(partial, ("tensor", "layer"), along_xz)
    arrived = arrived.reshape(2, n_layer, half + 16, width)
    input_grad = arrived[:, :, :half].astype(F32).sum(axis=1).astype(BF16).reshape(tokens, width)
    ends = lax.dynamic_index_in_dim(arrived[:, :, half], x, 0, keepdims=False).astype(F32).sum(axis=0)
    scores = (ends[: width // 2] + ends[width // 2 :])[None]
    return input_grad, scores


def solution(mesh):
    in_specs = (
        P(None, "dp", ("tensor", "layer")),
        P("dp", ("tensor", "layer")),
        P(None, "tensor", None, "layer", None),
        P(None, None, ("tensor", "layer")),
        P(None, None, ("tensor", "layer")),
        P("layer", ("dp", "tensor"), None),
        P(),
    )
    out_specs = (P("dp", ("tensor", "layer")), P("layer", ("dp", "tensor")))
    return jax.shard_map(
        on_device, mesh=mesh, in_specs=in_specs, out_specs=out_specs, check_vma=False
    )
```

time: 278 us -> 283 us (1.018)
  blocking collectives: 16.7 us -> 54.4 us
  starting transfers between devices: 54.3 us -> 34.8 us
  Pallas kernels: 52.4 us -> 34.5 us
  local copies, waits for them, and re-layouts: 10.4 us -> 26.5 us
  matrix products: 15 us -> 4.98 us
    all_to_all x10 -> x6, waiting for transfers between devices: 82.3 us -> 32.2 us  [exchange(): lax.all_to_all(blocks, axes, 0, 0, tiled=True, axis_index_groups=groups)]
    ppermute x7, waiting for transfers between devices: 34.3 us -> 83.4 us  [the longest x1 37.3 us: on_device(): near[0] = lax.ppermute(passed[0], ('dp', 'tensor'), across)]
    all_to_all x1 -> x3, blocking collectives: 16.7 us -> 54.4 us  [exchange(): lax.all_to_all(blocks, axes, 0, 0, tiled=True, axis_index_groups=groups)]
    all_to_all x10 -> x6, starting transfers between devices: 44.9 us -> 27.4 us  [exchange(): lax.all_to_all(blocks, axes, 0, 0, tiled=True, axis_index_groups=groups)]
    unnamed x24 -> x57, local copies, waits for them, and re-layouts: 1.74 us -> 18.9 us
    pallas_call x4 -> x9, Pallas kernels: 33 us -> 18.1 us  [the longest x3 14.2 us: pair_partial(): pl.pallas_call(body, in_specs=[SCALARS] + [WIDE] * len(operands), out_spe...]
    dot_general x12 -> x4, matrix products: 14 us -> 4.61 us  [on_device(): lax.dot_general(proj_in[k], saved_inputs[k], NT, preferred_element_type=F32)]
    reduce_sum x7 -> x9, other arithmetic: 3.61 us -> 6.96 us  [the longest x1 1.46 us: on_device(): total = start.astype(F32) + arrived[:, :, :half].astype(F32).sum(axis=1)]
  transfers between devices with their start and end apart: 17 -> 13, of which waited for: 9 -> 6; matrix products, arithmetic and copies ran while one was open for 11% -> 7% of each run, Pallas kernels for 19% -> 9%
where the time goes in v2:
time: 283 us; the launch traced here: 282 us
  waiting for transfers between devices  116 us (41%)
  blocking collectives  54.4 us (19%)
  starting transfers between devices  34.8 us (12%)
  Pallas kernels  34.5 us (12%)
  local copies, waits for them, and re-layouts  26.5 us (9%)
  other arithmetic  10.1 us (4%)
  matrix products  4.98 us (2%)
    all_to_all x3, blocking collectives, exchange(): lax.all_to_all(blocks, axes, 0, 0, tiled=True, axis_index_groups=groups)  54.4 us
    ppermute x1, waiting for transfers between devices, on_device(): near[0] = lax.ppermute(passed[0], ('dp', 'tensor'), across)  37.3 us
    all_to_all x6, waiting for transfers between devices, exchange(): lax.all_to_all(blocks, axes, 0, 0, tiled=True, axis_index_groups=groups)  32.2 us
    ppermute x1, waiting for transfers between devices, on_device(): near[1] = lax.ppermute(passed[1], 'tensor', beside)  30 us
    all_to_all x6, starting transfers between devices, exchange(): lax.all_to_all(blocks, axes, 0, 0, tiled=True, axis_index_groups=groups)  27.4 us
    unnamed x57, local copies, waits for them, and re-layouts  18.9 us
    pallas_call x4, Pallas kernels, features_first(): pl.pallas_call(body, grid_spec=pltpu.PrefetchScalarGridSpec(num_scalar_pr...  16.4 us
    ppermute x1, waiting for transfers between devices, on_device(): other_proj = lax.ppermute(proj_out, 'tensor', beside)  16 us
  transfers between devices with their start and end apart: 13, of which 6 were waited for; matrix products, arithmetic and copies ran while one was open for 7% of the time, Pallas kernels for 9%

profile of v2, /device:TPU:0, one launch (start us, length us, event | category | flops | bytes accessed | tf_op | source)
XLA Modules:
  0.0 282.0 jit_solution(14623754974844123959)
XLA Ops:
  0.6 2.5 broadcast_in_dim.27
  3.1 5.5 %all-to-all-start = ((bf16[8,512,256]{2,1,0:T(8,128)(2,1)}), bf16[8,512,256]{2,1,0:T(8,128)(2,1)S(1)}, u32[]{:S(2)}, u32[]{:S(2)}) async-start(bf16[8,512,256]{2,1,0:T(8,128)(2,1)} %broadcast_in_dim.27), calls=%async_computation | async-start | bytes 4194304 | tf_op jit(solution)/shard_map/all_to_all | solution.py:191
  8.6 4.0 %shard_map.90 = (bf16[8,1024,256]{2,1,0:T(8,128)(2,1)S(1)}, bf16[4,1024,256]{2,1,0:T(8,128)(2,1)}) custom-call(s32[1]{0:T(128)} %bitcast.1.core_ref, bf16[4,1024,8,256]{3,2,1,0:T(8,128)(2,1)} %bitcast.93), custom_call_target="tpu_custom_call" | custom-call | bytes 10485760 | tf_op jit(solution)/shard_map/pallas_call | solution.py:28
  12.6 1.9 copy-done.2
  14.6 3.3 %collective-permute-start.1 = (bf16[4,1024,256]{2,1,0:T(8,128)(2,1)}, bf16[4,1024,256]{2,1,0:T(8,128)(2,1)}, u32[]{:S(2)}, u32[]{:S(2)}) collective-permute-start(bf16[4,1024,256]{2,1,0:T(8,128)(2,1)} %get-tuple-element.22), channel_id=1, source_target_pairs={{0,68},{4,64},{8,76},{12,72},{16,84},{20,80},{24,92},{28,88},{32,1... | collective-permute-start | bytes 6291464 | tf_op jit(solution)/shard_map/ppermute | solution.py:238
  17.8 4.0 %shard_map.86 = (bf16[8,1024,256]{2,1,0:T(8,128)(2,1)S(1)}, bf16[4,1024,256]{2,1,0:T(8,128)(2,1)}) custom-call(s32[1]{0:T(128)} %bitcast.1.core_ref, bf16[4,1024,8,256]{3,2,1,0:T(8,128)(2,1)} %bitcast.94), custom_call_target="tpu_custom_call" | custom-call | bytes 10485760 | tf_op jit(solution)/shard_map/pallas_call | solution.py:28
  21.9 2.0 copy-done.17
  23.9 1.2 convolution_convert_fusion.3
  25.1 1.2 convolution_convert_fusion.2
  26.3 1.2 convolution_convert_fusion.1
  28.1 1.1 convolution_convert_fusion
  30.2 5.4 %all-to-all-done.g_ref = bf16[8,512,256]{2,1,0:T(8,128)(2,1)S(1)} async-done(((bf16[8,512,256]{2,1,0:T(8,128)(2,1)}), bf16[8,512,256]{2,1,0:T(8,128)(2,1)S(1)}, u32[]{:S(2)}, u32[]{:S(2)}) %all-to-all-start) | async-done | bytes 2097184 | tf_op jit(solution)/shard_map/all_to_all | solution.py:191
  35.6 2.2 copy-done.18
  37.8 2.4 shard_map.87
  40.2 1.1 copy-done.8
  41.2 5.7 %all-to-all-start.1 = ((bf16[8,320,256]{2,1,0:T(8,128)(2,1)}), bf16[8,320,256]{2,1,0:T(8,128)(2,1)}, u32[]{:S(2)}, u32[]{:S(2)}) async-start(bf16[8,320,256]{2,1,0:T(8,128)(2,1)} %copy-done.8), calls=%async_computation.1 | async-start | bytes 2621440 | tf_op jit(solution)/shard_map/all_to_all | solution.py:191
  47.0 2.0 collective-permute-start
  49.0 16.0 %collective-permute-done = bf16[4,64,256]{2,1,0:T(8,128)(2,1)S(1)} collective-permute-done((bf16[4,64,256]{2,1,0:T(8,128)(2,1)S(1)}, bf16[4,64,256]{2,1,0:T(8,128)(2,1)S(1)}, u32[]{:S(2)}, u32[]{:S(2)}) %collective-permute-start) | collective-permute-done | bytes 131104 | tf_op jit(solution)/shard_map/ppermute | solution.py:239
  65.7 1.0 maximum_select_fusion
  67.3 1.5 convert_reduce_fusion.2
  70.4 1.0 slice_reduce_fusion.1
  71.4 1.1 broadcast_in_dim.28
  72.5 3.8 %all-to-all-start.2 = ((bf16[4,576,256]{2,1,0:T(8,128)(2,1)}), bf16[4,576,256]{2,1,0:T(8,128)(2,1)S(1)}, u32[]{:S(2)}, u32[]{:S(2)}) async-start(bf16[4,576,256]{2,1,0:T(8,128)(2,1)} %broadcast_in_dim.28), calls=%async_computation.2 | async-start | bytes 2359296 | tf_op jit(solution)/shard_map/all_to_all | solution.py:191
  76.4 17.1 %all-to-all-done.2.g_ref = bf16[4,576,256]{2,1,0:T(8,128)(2,1)S(1)} async-done(((bf16[4,576,256]{2,1,0:T(8,128)(2,1)}), bf16[4,576,256]{2,1,0:T(8,128)(2,1)S(1)}, u32[]{:S(2)}, u32[]{:S(2)}) %all-to-all-start.2) | async-done | bytes 1179680 | tf_op jit(solution)/shard_map/all_to_all | solution.py:191
  93.5 2.2 copy-done.3
  95.7 4.6 %shard_map.91 = bf16[4,576,256]{2,1,0:T(8,128)(2,1)S(1)} custom-call(s32[3]{0:T(128)S(1)} %pad_add_fusion.s_ref, bf16[4,576,256]{2,1,0:T(8,128)(2,1)S(1)} %all-to-all-done.2.g_ref, bf16[8,1024,256]{2,1,0:T(8,128)(2,1)S(1)} %copy-done.3, bf16[4,1024,256]{2,1,0:T(8,128)(2,1)} %collective-permute-done.1.near_ref, ...), custom_call_target="tpu_custom_call" | custom-call | flops 2147483648 | bytes 10485760 | tf_op jit(solution)/shard_map/pallas_call | solution.py:139
  100.3 1.0 copy-done.1
  101.4 4.3 %all-to-all-start.3 = ((bf16[4,576,256]{2,1,0:T(8,128)(2,1)}), bf16[4,576,256]{2,1,0:T(8,128)(2,1)}, u32[]{:S(2)}, u32[]{:S(2)}) async-start(bf16[4,576,256]{2,1,0:T(8,128)(2,1)} %copy-done.1), calls=%async_computation.3 | async-start | bytes 2359296 | tf_op jit(solution)/shard_map/all_to_all | solution.py:191
  105.7 4.1 %shard_map.93 = (bf16[8,1024,256]{2,1,0:T(8,128)(2,1)S(1)}, bf16[4,1024,256]{2,1,0:T(8,128)(2,1)}) custom-call(s32[1]{0:T(128)} %bitcast.1.core_ref, bf16[4,1024,8,256]{3,2,1,0:T(8,128)(2,1)} %bitcast.95), custom_call_target="tpu_custom_call" | custom-call | bytes 10485760 | tf_op jit(solution)/shard_map/pallas_call | solution.py:28
  109.8 2.0 copy-done.6
  112.3 9.8 %all-to-all-done.3 = bf16[4,576,256]{2,1,0:T(8,128)(2,1)} async-done(((bf16[4,576,256]{2,1,0:T(8,128)(2,1)}), bf16[4,576,256]{2,1,0:T(8,128)(2,1)}, u32[]{:S(2)}, u32[]{:S(2)}) %all-to-all-start.3) | async-done | bytes 1179680 | tf_op jit(solution)/shard_map/all_to_all | solution.py:191
  122.1 1.4 convert_reduce_fusion.1
  124.4 1.1 broadcast_in_dim.29
  125.6 3.5 %all-to-all-start.4 = ((bf16[4,512,256]{2,1,0:T(8,128)(2,1)}), bf16[4,512,256]{2,1,0:T(8,128)(2,1)S(1)}, u32[]{:S(2)}, u32[]{:S(2)}) async-start(bf16[4,512,256]{2,1,0:T(8,128)(2,1)} %broadcast_in_dim.29), calls=%async_computation.4 | async-start | bytes 2097152 | tf_op jit(solution)/shard_map/all_to_all | solution.py:191
  129.1 30.0 %collective-permute-done.3.near_ref = bf16[4,1024,256]{2,1,0:T(8,128)(2,1)} collective-permute-done((bf16[4,1024,256]{2,1,0:T(8,128)(2,1)}, bf16[4,1024,256]{2,1,0:T(8,128)(2,1)}, u32[]{:S(2)}, u32[]{:S(2)}) %collective-permute-start.3) | collective-permute-done | bytes 2097184 | tf_op jit(solution)/shard_map/ppermute | solution.py:267
  159.1 4.2 %shard_map.97 = (bf16[8,1024,256]{2,1,0:T(8,128)(2,1)S(1)}, bf16[4,1024,256]{2,1,0:T(8,128)(2,1)}) custom-call(s32[1]{0:T(128)} %bitcast.1.core_ref, bf16[4,1024,8,256]{3,2,1,0:T(8,128)(2,1)} %bitcast.96), custom_call_target="tpu_custom_call" | custom-call | bytes 10485760 | tf_op jit(solution)/shard_map/pallas_call | solution.py:28
  163.3 1.9 copy-done.4
  165.2 1.6 collective-permute-start.5
  166.8 4.9 %shard_map.94 = bf16[4,512,256]{2,1,0:T(8,128)(2,1)} custom-call(s32[3]{0:T(128)S(1)} %pad_add_fusion.s_ref, bf16[4,512,256]{2,1,0:T(8,128)(2,1)S(1)} %all-to-all-done.4.g_ref, bf16[8,1024,256]{2,1,0:T(8,128)(2,1)S(1)} %copy-done.7, bf16[4,1024,256]{2,1,0:T(8,128)(2,1)} %collective-permute-done.3.near_ref, ...), custom_call_target="tpu_custom_call" | custom-call | flops 2147483648 | bytes 10485760 | tf_op jit(solution)/shard_map/pallas_call | solution.py:139
  171.7 4.6 %all-to-all-start.5 = ((bf16[4,512,256]{2,1,0:T(8,128)(2,1)}), bf16[4,512,256]{2,1,0:T(8,128)(2,1)}, u32[]{:S(2)}, u32[]{:S(2)}) async-start(bf16[4,512,256]{2,1,0:T(8,128)(2,1)} %shard_map.94), calls=%async_computation.5 | async-start | bytes 2097152 | tf_op jit(solution)/shard_map/all_to_all | solution.py:191
  176.5 0.9 slice.96.b_ref
  177.4 37.3 %collective-permute-done.5.near_ref = bf16[4,1024,256]{2,1,0:T(8,128)(2,1)} collective-permute-done((bf16[4,1024,256]{2,1,0:T(8,128)(2,1)}, bf16[4,1024,256]{2,1,0:T(8,128)(2,1)}, u32[]{:S(2)}, u32[]{:S(2)}) %collective-permute-start.5) | collective-permute-done | bytes 2097184 | tf_op jit(solution)/shard_map/ppermute | solution.py:271
  214.8 1.4 convert_reduce_fusion
  217.7 19.9 %all_to_all.45.g_ref = bf16[4,576,256]{2,1,0:T(8,128)(2,1)S(1)} all-to-all(bf16[4,576,256]{2,1,0:T(8,128)(2,1)S(1)} %broadcast_in_dim.30), channel_id=1, replica_groups={{0,8,16,24},{4,12,20,28},{1,9,17,25},{5,13,21,29},{2,10,18,26},{6,14,22..., dimensions={0} | all-to-all | bytes 2359296 | tf_op jit(solution)/shard_map/all_to_all | solution.py:191
  237.7 15.0 %all_to_all.46 = bf16[32,32,128]{2,1,0:T(8,128)(2,1)S(1)} all-to-all(bf16[32,32,128]{2,1,0:T(8,128)(2,1)S(1)} %bitcast.102), channel_id=1, replica_groups={{0,1,2,3,4,5,6,7,32,33,34,35,36,37,38,39,64,65,66,67,68,69,70,71,96,97,..., dimensions={0} | all-to-all | bytes 524288 | tf_op jit(solution)/shard_map/all_to_all | solution.py:191
  254.3 2.2 copy-done.5
  256.5 4.6 %shard_map.98 = bf16[8,272,256]{2,1,0:T(8,128)(2,1)S(1)} custom-call(s32[3]{0:T(128)S(1)} %pad_add_fusion.s_ref, bf16[4,576,256]{2,1,0:T(8,128)(2,1)S(1)} %all_to_all.45.g_ref, bf16[8,1024,256]{2,1,0:T(8,128)(2,1)S(1)} %copy-done.5, bf16[4,1024,256]{2,1,0:T(8,128)(2,1)} %collective-permute-done.5.near_ref, ...), custom_call_target="tpu_custom_call" | custom-call | flops 2147483648 | bytes 10485760 | tf_op jit(solution)/shard_map/pallas_call | solution.py:139
  261.1 19.5 %all_to_all.47 = bf16[8,272,256]{2,1,0:T(8,128)(2,1)S(1)} all-to-all(bf16[8,272,256]{2,1,0:T(8,128)(2,1)S(1)} %shard_map.98), channel_id=1, replica_groups={{0,1,2,3,4,5,6,7},{8,9,10,11,12,13,14,15},{16,17,18,19,20,21,22,23},{24..., dimensions={0} | all-to-all | bytes 2228224 | tf_op jit(solution)/shard_map/all_to_all | solution.py:191
  (99 shorter events, 10.6 us)
Async XLA Ops:
  0.6 253.2 %copy-start = (bf16[1,128,4096]{2,1,0:T(8,128)(2,1)S(1)}, bf16[1,128,4096]{2,1,0:T(8,128)(2,1)}, u32[]{:S(2)}) copy-start(bf16[1,128,4096]{2,1,0:T(8,128)(2,1)} %param.12) | copy-start | bytes 3145732
  3.1 32.5 %all-to-all-start = ((bf16[8,512,256]{2,1,0:T(8,128)(2,1)}), bf16[8,512,256]{2,1,0:T(8,128)(2,1)S(1)}, u32[]{:S(2)}, u32[]{:S(2)}) async-start(bf16[8,512,256]{2,1,0:T(8,128)(2,1)} %broadcast_in_dim.27), calls=%async_computation | async-start | bytes 4194304 | tf_op jit(solution)/shard_map/all_to_all | solution.py:191
  12.6 1.9 copy-start.2
  14.6 9.3 %copy-start.26 = (bf16[4,64,256]{2,1,0:T(8,128)(2,1)S(1)}, bf16[4,64,256]{2,1,0:T(8,128)(2,1)}, u32[]{:S(2)}) copy-start(bf16[4,64,256]{2,1,0:T(8,128)(2,1)} %param.10) | copy-start | bytes 393220
  14.6 55.8 %collective-permute-start.1 = (bf16[4,1024,256]{2,1,0:T(8,128)(2,1)}, bf16[4,1024,256]{2,1,0:T(8,128)(2,1)}, u32[]{:S(2)}, u32[]{:S(2)}) collective-permute-start(bf16[4,1024,256]{2,1,0:T(8,128)(2,1)} %get-tuple-element.22), channel_id=1, source_target_pairs={{0,68},{4,64},{8,76},{12,72},{16,84},{20,80},{24,92},{28,88},{32,1... | collective-permute-start | bytes 6291464 | tf_op jit(solution)/shard_map/ppermute | solution.py:238
  21.9 2.0 copy-start.17
  35.6 2.2 copy-start.18
  40.1 1.1 copy-start.8
  41.2 5.7 %copy-start.24 = (bf16[4,64,256]{2,1,0:T(8,128)(2,1)S(1)}, bf16[4,64,256]{2,1,0:T(8,128)(2,1)}, u32[]{:S(2)}) copy-start(bf16[4,64,256]{2,1,0:T(8,128)(2,1)} %param.11) | copy-start | bytes 393220
  41.2 26.1 %all-to-all-start.1 = ((bf16[8,320,256]{2,1,0:T(8,128)(2,1)}), bf16[8,320,256]{2,1,0:T(8,128)(2,1)}, u32[]{:S(2)}, u32[]{:S(2)}) async-start(bf16[8,320,256]{2,1,0:T(8,128)(2,1)} %copy-done.8), calls=%async_computation.1 | async-start | bytes 2621440 | tf_op jit(solution)/shard_map/all_to_all | solution.py:191
  47.0 18.1 %collective-permute-start = (bf16[4,64,256]{2,1,0:T(8,128)(2,1)S(1)}, bf16[4,64,256]{2,1,0:T(8,128)(2,1)S(1)}, u32[]{:S(2)}, u32[]{:S(2)}) collective-permute-start(bf16[4,64,256]{2,1,0:T(8,128)(2,1)S(1)} %copy-done.24), channel_id=1, source_target_pairs={{0,4},{4,0},{8,12},{12,8},{16,20},{20,16},{24,28},{28,24},{1,5},{5... | collective-permute-start | bytes 393224 | tf_op jit(solution)/shard_map/ppermute | solution.py:239
  65.0 0.7 copy-start.25
  67.3 1.6 copy-start.10
  67.3 1.8 copy-start.9
  68.8 2.6 copy-start.19
  69.1 0.6 copy-start.11
  69.7 0.6 copy-start.13
  70.3 23.2 %collective-permute-start.2 = (bf16[4,1024,256]{2,1,0:T(8,128)(2,1)}, bf16[4,1024,256]{2,1,0:T(8,128)(2,1)}, u32[]{:S(2)}, u32[]{:S(2)}) collective-permute-start(bf16[4,1024,256]{2,1,0:T(8,128)(2,1)} %collective-permute-done.1.near_ref), channel_id=1, source_target_pairs={{0,32},{32,0},{64,96},{96,64},{1,33},{33,1},{65,97},{97,65},{2,34}... | collective-permute-start | bytes 6291464 | tf_op jit(solution)/shard_map/ppermute | solution.py:269
  72.5 21.0 %all-to-all-start.2 = ((bf16[4,576,256]{2,1,0:T(8,128)(2,1)}), bf16[4,576,256]{2,1,0:T(8,128)(2,1)S(1)}, u32[]{:S(2)}, u32[]{:S(2)}) async-start(bf16[4,576,256]{2,1,0:T(8,128)(2,1)} %broadcast_in_dim.28), calls=%async_computation.2 | async-start | bytes 2359296 | tf_op jit(solution)/shard_map/all_to_all | solution.py:191
  93.5 2.2 copy-start.3
  100.3 1.1 copy-start.1
  101.4 20.7 %all-to-all-start.3 = ((bf16[4,576,256]{2,1,0:T(8,128)(2,1)}), bf16[4,576,256]{2,1,0:T(8,128)(2,1)}, u32[]{:S(2)}, u32[]{:S(2)}) async-start(bf16[4,576,256]{2,1,0:T(8,128)(2,1)} %copy-done.1), calls=%async_computation.3 | async-start | bytes 2359296 | tf_op jit(solution)/shard_map/all_to_all | solution.py:191
  105.7 17.9 %copy-start.20 = (f32[2,256,256]{2,1,0:T(8,128)S(1)}, f32[2,256,256]{2,1,0:T(8,128)}, u32[]{:S(2)}) copy-start(f32[2,256,256]{2,1,0:T(8,128)} %copy-done.19) | copy-start | bytes 1572868
  109.8 2.0 copy-start.6
  111.8 47.3 %collective-permute-start.3 = (bf16[4,1024,256]{2,1,0:T(8,128)(2,1)}, bf16[4,1024,256]{2,1,0:T(8,128)(2,1)}, u32[]{:S(2)}, u32[]{:S(2)}) collective-permute-start(bf16[4,1024,256]{2,1,0:T(8,128)(2,1)} %get-tuple-element.27), channel_id=1, source_target_pairs={{0,4},{4,0},{8,12},{12,8},{16,20},{20,16},{24,28},{28,24},{1,5},{5... | collective-permute-start | bytes 6291464 | tf_op jit(solution)/shard_map/ppermute | solution.py:267
  123.5 2.1 copy-start.22
  123.8 0.6 copy-start.15
  125.6 33.5 %all-to-all-start.4 = ((bf16[4,512,256]{2,1,0:T(8,128)(2,1)}), bf16[4,512,256]{2,1,0:T(8,128)(2,1)S(1)}, u32[]{:S(2)}, u32[]{:S(2)}) async-start(bf16[4,512,256]{2,1,0:T(8,128)(2,1)} %broadcast_in_dim.29), calls=%async_computation.4 | async-start | bytes 2097152 | tf_op jit(solution)/shard_map/all_to_all | solution.py:191
  159.1 7.7 %collective-permute-start.4 = (bf16[4,1024,256]{2,1,0:T(8,128)(2,1)}, bf16[4,1024,256]{2,1,0:T(8,128)(2,1)S(1)}, u32[]{:S(2)}, u32[]{:S(2)}) collective-permute-start(bf16[4,1024,256]{2,1,0:T(8,128)(2,1)} %collective-permute-done.3.near_ref), channel_id=1, source_target_pairs={{0,32},{32,0},{64,96},{96,64},{1,33},{33,1},{65,97},{97,65},{2,34}... | collective-permute-start | bytes 6291464 | tf_op jit(solution)/shard_map/ppermute | solution.py:288
  159.1 7.7 %copy-start.7 = (bf16[8,1024,256]{2,1,0:T(8,128)(2,1)S(1)}, bf16[8,1024,256]{2,1,0:T(8,128)(2,1)}, u32[]{:S(2)}) copy-start(bf16[8,1024,256]{2,1,0:T(8,128)(2,1)} %copy-done.6) | copy-start | bytes 12582916
  163.3 1.9 copy-start.4
  165.2 49.6 %collective-permute-start.5 = (bf16[4,1024,256]{2,1,0:T(8,128)(2,1)}, bf16[4,1024,256]{2,1,0:T(8,128)(2,1)}, u32[]{:S(2)}, u32[]{:S(2)}) collective-permute-start(bf16[4,1024,256]{2,1,0:T(8,128)(2,1)} %get-tuple-element.34), channel_id=1, source_target_pairs={{0,68},{4,64},{8,76},{12,72},{16,84},{20,80},{24,92},{28,88},{32,1... | collective-permute-start | bytes 6291464 | tf_op jit(solution)/shard_map/ppermute | solution.py:271
  171.7 4.6 %copy-start.27 = (s32[4]{0:T(128)S(1)}, s32[4]{0:T(128)}, u32[]{:S(2)}) copy-start(s32[4]{0:T(128)} %param.13) | copy-start | bytes 52
  171.7 44.5 %copy-start.21 = (f32[2,256,256]{2,1,0:T(8,128)S(1)}, f32[2,256,256]{2,1,0:T(8,128)}, u32[]{:S(2)}) copy-start(f32[2,256,256]{2,1,0:T(8,128)} %copy-done.19) | copy-start | bytes 1572868
  171.7 44.5 %copy-start.23 = (f32[512,256]{1,0:T(8,128)S(1)}, f32[512,256]{1,0:T(8,128)}, u32[]{:S(2)}) copy-start(f32[512,256]{1,0:T(8,128)} %copy-done.22) | copy-start | bytes 1572868
  171.7 43.1 %all-to-all-start.5 = ((bf16[4,512,256]{2,1,0:T(8,128)(2,1)}), bf16[4,512,256]{2,1,0:T(8,128)(2,1)}, u32[]{:S(2)}, u32[]{:S(2)}) async-start(bf16[4,512,256]{2,1,0:T(8,128)(2,1)} %shard_map.94), calls=%async_computation.5 | async-start | bytes 2097152 | tf_op jit(solution)/shard_map/all_to_all | solution.py:191
  177.4 39.2 %copy-start.12 = (bf16[64,256]{1,0:T(8,128)(2,1)S(1)}, bf16[64,256]{1,0:T(8,128)(2,1)}, u32[]{:S(2)}) copy-start(bf16[64,256]{1,0:T(8,128)(2,1)} %copy-done.11) | copy-start | bytes 98308
  177.4 39.2 %copy-start.14 = (bf16[64,256]{1,0:T(8,128)(2,1)S(1)}, bf16[64,256]{1,0:T(8,128)(2,1)}, u32[]{:S(2)}) copy-start(bf16[64,256]{1,0:T(8,128)(2,1)} %copy-done.13) | copy-start | bytes 98308
  177.4 39.2 %copy-start.16 = (bf16[64,256]{1,0:T(8,128)(2,1)S(1)}, bf16[64,256]{1,0:T(8,128)(2,1)}, u32[]{:S(2)}) copy-start(bf16[64,256]{1,0:T(8,128)(2,1)} %copy-done.15) | copy-start | bytes 98308
  214.8 39.5 %collective-permute-start.6 = (bf16[4,1024,256]{2,1,0:T(8,128)(2,1)}, bf16[4,1024,256]{2,1,0:T(8,128)(2,1)}, u32[]{:S(2)}, u32[]{:S(2)}) collective-permute-start(bf16[4,1024,256]{2,1,0:T(8,128)(2,1)} %collective-permute-done.5.near_ref), channel_id=1, source_target_pairs={{0,32},{32,0},{64,96},{96,64},{1,33},{33,1},{65,97},{97,65},{2,34}... | collective-permute-start | bytes 6291464 | tf_op jit(solution)/shard_map/ppermute | solution.py:291
  254.3 2.2 copy-start.5

commit v3 on v0

v3 whole, which is shorter than its diff:
```python
import jax
import jax.numpy as jnp
from jax import lax
from jax.experimental import pallas as pl
from jax.experimental.pallas import tpu as pltpu
from jax.sharding import PartitionSpec as P

NT = (((1,), (1,)), ((), ()))
NN = (((1,), (0,)), ((), ()))
F32 = jnp.float32
BF16 = jnp.bfloat16
WIDE = pl.BlockSpec(memory_space=pltpu.VMEM)
SCALARS = pl.BlockSpec(memory_space=pltpu.SMEM)
after = lax.optimization_barrier


def limit(mib):
    return pltpu.CompilerParams(vmem_limit_bytes=mib << 20)


def dot(left, right, dims=NN):
    return lax.dot_general(left, right, dims, preferred_element_type=F32)


def sum_of(terms):
    total = None
    for term in terms:
        total = term if total is None else total + term
    return total


def local_call(body, outs, operands, scalars=(), cost=None):
    return pl.pallas_call(
        body,
        in_specs=[SCALARS] * len(scalars) + [WIDE] * len(operands),
        out_specs=[WIDE] * len(outs),
        out_shape=[jax.ShapeDtypeStruct(*out) for out in outs],
        compiler_params=limit(8),
        cost_estimate=cost,
    )(*scalars, *operands)


def features_first(weights, levels, core, pieces):
    _, rows, cells, width = weights.shape
    step, half = 512, cells // 2
    steps = rows // step
    count = len(levels)
    deep = half // max(pieces, 1)

    def body(core_ref, w_ref, *refs):
        own_refs, s_refs = refs[:count], refs[count:]
        for k, o_ref in enumerate(own_refs):

            @pl.when(pl.program_id(0) == k)
            def _(o_ref=o_ref):
                o_ref[...] = jnp.swapaxes(w_ref[0], 0, 1)
                for i, s_ref in enumerate(s_refs):
                    s_ref[0] = o_ref[pl.ds(half * core_ref[0] + deep * i, deep)]

    def own_map(k):
        def index(m, n, c):
            return (0, jnp.where(m < k, 0, jnp.where(m > k, steps - 1, n)), 0)

        return index

    return pl.pallas_call(
        body,
        grid_spec=pltpu.PrefetchScalarGridSpec(
            num_scalar_prefetch=1,
            grid=(count, steps),
            in_specs=[
                pl.BlockSpec(
                    (1, step, cells, width), lambda m, n, c: (levels[0] - m, n, 0, 0)
                )
            ],
            out_specs=[pl.BlockSpec((cells, step, width), own_map(k)) for k in range(count)]
            + [pl.BlockSpec((1, deep, step, width), lambda m, n, c: (m, 0, n, 0))] * pieces,
        ),
        out_shape=[jax.ShapeDtypeStruct((cells, rows, width), weights.dtype)] * count
        + [jax.ShapeDtypeStruct((count, deep, rows, width), weights.dtype)] * pieces,
        compiler_params=limit(14 + 6 * (count - 1)),
        cost_estimate=pl.CostEstimate(
            flops=0, bytes_accessed=5 * count * rows * cells * width, transcendentals=0
        ),
    )(core, weights)


def first_partial(gathered, weight, extra):
    cells, tokens, width = gathered.shape
    rows = weight.shape[1]
    groups = rows // width
    half = tokens // 2
    tail = extra.shape[1]

    def body(g_ref, w_ref, e_ref, o_ref):
        for h in range(2):
            for n in range(groups):
                total = sum_of(
                    dot(
                        w_ref[a, n * width : (n + 1) * width],
                        g_ref[a, h * half : (h + 1) * half],
                        NT,
                    )
                    for a in range(cells)
                )
                o_ref[h * groups + n, :width] = total.astype(o_ref.dtype)
        o_ref[:, width:] = e_ref[...]

    return local_call(
        body,
        [((2 * groups, width + tail, half), BF16)],
        [gathered, weight, extra],
        cost=pl.CostEstimate(
            flops=2 * cells * width * rows * tokens,
            bytes_accessed=2 * (cells * width * (rows + tokens) + rows * tokens),
            transcendentals=0,
        ),
    )[0]


def pair_totals(s_ref, g_ref, w_refs, slot, groups):
    own_ref, *others = w_refs
    cells, _, width = own_ref.shape
    half = cells // 2
    deep = others[0].shape[1]
    pieces = half // deep
    x, core = s_ref[0], s_ref[1]
    for n in range(groups):
        cut = slice(n * width, (n + 1) * width)
        yield x, n, sum_of(
            dot(own_ref[a, cut], g_ref[a // 2, (a % 2) * width : (a % 2 + 1) * width])
            for a in range(cells)
        )
    for n in range(groups):
        cut = slice(n * width, (n + 1) * width)
        yield 1 - x, n, sum_of(
            dot(
                refs[i // deep][slot, i % deep, cut],
                g_ref[(half // 2) * first + i // 2, (i % 2) * width : (i % 2 + 1) * width],
            )
            for first, refs in ((core, others[:pieces]), (1 - core, others[pieces:]))
            for i in range(half)
        )


def pair_cost(own, tokens):
    cells, rows, width = own.shape
    return pl.CostEstimate(
        flops=4 * cells * width * rows * tokens,
        bytes_accessed=4 * cells * width * rows,
        transcendentals=0,
    )


def pair_partial(place, gathered, held, slot, extra):
    own = held[0]
    width = own.shape[2]
    groups = own.shape[1] // width

    def body(s_ref, g_ref, *refs):
        *w_refs, e_ref, o_ref = refs
        for column, n, total in pair_totals(s_ref, g_ref, w_refs, slot, groups):
            start = pl.multiple_of(column * width, width)
            o_ref[n, pl.ds(start, width)] = total.astype(o_ref.dtype)
        for n in range(groups):
            o_ref[n, 2 * width :] = e_ref[...]

    return local_call(
        body,
        [((groups, 2 * width + extra.shape[0], gathered.shape[2]), BF16)],
        [gathered, *held, extra],
        [place],
        pair_cost(own, gathered.shape[2]),
    )[0]


def pair_partial_scored(place, layer_of, gathered, held, slot, outs, kept_out, proj, ins):
    own = held[0]
    width = own.shape[2]
    groups = own.shape[1] // width
    rank = ins.shape[1]
    quarter = rank // 4

    def body(s_ref, l_ref, g_ref, *refs):
        *w_refs, a_ref, k_ref, p_ref, i_ref, o_ref, f_ref = refs
        f_ref[1:] = a_ref[...]
        final = k_ref[...]
        for column, n, total in pair_totals(s_ref, g_ref, w_refs, slot, groups):
            start = pl.multiple_of(column * width, width)
            rounded = total.astype(o_ref.dtype)
            o_ref[n, pl.ds(start, width)] = rounded
            final = final + dot(p_ref[n, column], rounded)
        f_ref[0] = final.astype(f_ref.dtype)
        for o in range(groups):
            block = dot(f_ref[l_ref[o]], i_ref[l_ref[o]], NT).astype(o_ref.dtype)
            o_ref[o, 2 * width :] = jnp.concatenate(
                [block[quarter * j : quarter * (j + 1)] for j in range(4)], axis=1
            )

    tokens = gathered.shape[2]
    return local_call(
        body,
        [((groups, 2 * width + quarter, tokens), BF16), ((outs.shape[0] + 1, rank, tokens), BF16)],
        [gathered, *held, outs, kept_out, proj, ins],
        [place, layer_of],
        pair_cost(own, tokens),
    )[0]


def last_partial(place, gathered, held, slot, kept, extra):
    own = held[0]
    width = own.shape[2]
    groups = own.shape[1] // width

    def body(s_ref, g_ref, *refs):
        *w_refs, t_ref, e_ref, o_ref = refs
        for column, n, total in pair_totals(s_ref, g_ref, w_refs, slot, groups):
            start = pl.multiple_of(column * width, width)
            mine = t_ref[pl.ds(start, width)]
            total = total + jnp.where(n == s_ref[2], mine, jnp.zeros_like(mine))
            o_ref[groups * column + n, :width] = total.astype(o_ref.dtype)
        for k in range(2 * groups):
            o_ref[k, width:] = e_ref[k % groups]

    return local_call(
        body,
        [((2 * groups, width + extra.shape[1], gathered.shape[2]), BF16)],
        [gathered, *held, kept, extra],
        [place],
        pair_cost(own, gathered.shape[2]),
    )[0]


def settle_first(place, arrived, gathered, proj_top, proj_next):
    blocks, deep, half = arrived.shape
    width = gathered.shape[2]
    groups = blocks // 2
    rank = proj_top.shape[1]

    def body(s_ref, r_ref, g_ref, p_ref, q_ref, t_ref, c_ref, o_ref):
        x, y = s_ref[0], s_ref[3]
        outs = [None, None]
        for k in range(2):
            start = g_ref[2 * y + k, pl.ds(pl.multiple_of(x * half, half), half)].astype(F32).T
            outs[0] = sum_of([*([outs[0]] if k else []), dot(p_ref[k], start.astype(BF16))])
            total = start + sum_of(r_ref[groups * k + z, :width].astype(F32) for z in range(groups))
            t_ref[k * width : (k + 1) * width] = total
            rounded = total.astype(BF16)
            outs[1] = sum_of([*([outs[1]] if k else []), dot(q_ref[k], rounded)])
            for j in range(c_ref.shape[0]):
                c_ref[j, k * width : (k + 1) * width] = rounded
        ins = sum_of(r_ref[k, width:].astype(F32) for k in range(blocks)).astype(BF16)
        for j in range(c_ref.shape[0]):
            c_ref[j, 2 * width :] = ins
        o_ref[0] = outs[0].astype(BF16)
        o_ref[1] = outs[1].astype(BF16)

    return local_call(
        body,
        [
            ((2 * width, half), F32),
            ((gathered.shape[0] // 2, 2 * width + deep - width, half), BF16),
            ((2, rank, half), BF16),
        ],
        [arrived, gathered, proj_top, proj_next],
        [place],
    )


def settle(arrived, total, projs):
    groups, _, half = arrived.shape
    depth = total.shape[0]
    width = depth // 2
    count, _, rank, _ = projs.shape

    def body(r_ref, t_ref, p_ref, o_ref, c_ref, f_ref):
        value = t_ref[...] + sum_of(r_ref[z, :depth].astype(F32) for z in range(groups))
        o_ref[...] = value
        rounded = value.astype(BF16)
        for j in range(c_ref.shape[0]):
            c_ref[j] = rounded
        for i in range(count):
            f_ref[i] = dot(p_ref[i, 0], rounded[:width]) + dot(p_ref[i, 1], rounded[width:])

    return local_call(
        body,
        [(total.shape, F32), ((groups, depth, half), BF16), ((count, rank, half), F32)],
        [arrived, total, projs],
    )


def settle_scored(arrived, total):
    groups, deep, half = arrived.shape
    depth = total.shape[0]

    def body(r_ref, t_ref, o_ref, c_ref):
        value = t_ref[...] + sum_of(r_ref[z, :depth].astype(F32) for z in range(groups))
        o_ref[...] = value
        rounded = value.astype(BF16)
        blocks = sum_of(r_ref[z, depth:].astype(F32) for z in range(groups)).astype(BF16)
        for j in range(c_ref.shape[0]):
            c_ref[j, :depth] = rounded
            c_ref[j, depth:] = blocks

    return local_call(
        body, [(total.shape, F32), ((groups, deep, half), BF16)], [arrived, total]
    )


def finish(arrived):
    blocks, _, half = arrived.shape
    groups = blocks // 2
    width = half

    def body(r_ref, o_ref):
        for k in range(2):
            value = sum_of(r_ref[groups * k + z, :width].astype(F32) for z in range(groups))
            o_ref[k * half : (k + 1) * half] = value.T.astype(o_ref.dtype)

    return local_call(body, [((2 * half, width), BF16)], [arrived])[0]


def exchange(blocks, axes, groups=None):
    return lax.all_to_all(blocks, axes, 0, 0, tiled=True, axis_index_groups=groups)


def on_device(saved_inputs, output_grad, weights, proj_in, proj_out, query_grads, owner_map):
    layers, tokens, width = saved_inputs.shape
    rank = proj_in.shape[1]
    rows = weights.shape[1]
    n_dp, n_tensor, n_layer = (lax.axis_size(k) for k in ("dp", "tensor", "layer"))
    n_y = n_tensor // 2
    half = tokens // 2
    t, b = lax.axis_index("tensor"), lax.axis_index("layer")
    x, y = t & 1, t >> 1
    core = lax.axis_index("dp") & 1
    place = jnp.stack([x, core, b, y]).astype(jnp.int32)
    along_y = [[2 * k + j for k in range(n_y)] for j in range(2)]
    along_xz = [[2 * n_layer * k + j for j in range(2 * n_layer)] for k in range(n_y)]
    along_dp_x = [
        [d * n_tensor + 2 * k + j for d in range(n_dp) for j in range(2)] for k in range(n_y)
    ]
    across = [
        (d * n_tensor + k, (d ^ 2) * n_tensor + (k ^ 1)) for d in range(n_dp) for k in range(n_tensor)
    ]
    beside = [(k, k ^ 1) for k in range(n_tensor)]
    to_other_core = [(d, d ^ 1) for d in range(n_dp)]
    flat = pltpu.with_memory_space_constraint(
        weights.reshape(layers, rows, n_tensor, width), pltpu.HBM
    )
    owners = jnp.arange(n_layer, dtype=jnp.int32)
    layer_of = jnp.sum(
        owners[None, :] * (owner_map[None, :] == owners[:, None]).astype(jnp.int32), axis=1
    )

    gathered = exchange(
        jnp.broadcast_to(output_grad, (n_tensor, *output_grad.shape)), "tensor"
    )
    one = core.astype(jnp.int32).reshape(1)
    own = [None] * layers
    own[2], passed_first = features_first(flat, [2], one, 1)
    near_first = lax.ppermute(passed_first, ("dp", "tensor"), across)
    (own[3],) = features_first(flat, [3], one, 0)
    own[1], own[0], *passed = features_first(flat, [1, 0], one, 2)
    other_proj = lax.ppermute(proj_out, "tensor", beside)
    pair_proj = jnp.where(
        x == 0, jnp.stack([proj_out, other_proj], 1), jnp.stack([other_proj, proj_out], 1)
    )
    shifted = [pair_proj[0]] + [
        lax.ppermute(pair_proj[0], "layer", [(z, z ^ k) for z in range(n_layer)])
        for k in range(1, n_layer)
    ]
    last_proj = jnp.stack(
        [
            sum_of(jnp.where((b ^ k) == z, shifted[k], 0) for k in range(n_layer))
            for z in range(n_layer)
        ]
    ).astype(BF16)
    in_parts = jnp.stack(
        [dot(proj_in[k], saved_inputs[k], NT).astype(BF16) for k in range(layers)]
    )
    in_parts = jnp.stack([in_parts[:, :, :half], in_parts[:, :, half:]])
    in_parts = in_parts.reshape(2 * layers, rank, half)
    gathered, own, passed, pair_proj, last_proj, in_parts = after(
        (gathered, own, passed, pair_proj, last_proj, in_parts)
    )

    partial = first_partial(gathered, own[3], in_parts)
    arrived = exchange(partial, ("tensor", "layer"), along_xz)
    total, copies, outs_top = settle_first(place, arrived, gathered, pair_proj[3], pair_proj[2])

    passed, _ = after((passed, total))
    near = [
        lax.ppermute(passed[0], ("dp", "tensor"), across),
        lax.ppermute(passed[1], "tensor", beside),
    ]
    near_first, _ = after((near_first, total))
    far_first = lax.ppermute(near_first, "dp", to_other_core)
    gathered = exchange(copies, "tensor", along_y)
    in_whole = gathered[:, 2 * width :].astype(F32).sum(axis=0).astype(BF16)
    partial = pair_partial(place, gathered, [own[2], near_first, far_first], 0, in_whole)
    arrived = exchange(partial, "layer")
    ins = arrived[:, 2 * width :]
    total, copies, outs_low = settle(arrived, total, jnp.stack([pair_proj[1], pair_proj[0]]))
    outs = jnp.stack([outs_low[0].astype(BF16), outs_top[1], outs_top[0]])
    copies, outs, ins = after((copies, outs, ins))

    gathered = exchange(copies, "tensor", along_y)
    near, _ = after((near, copies))
    far = [lax.ppermute(v, "dp", to_other_core) for v in near]
    partial = pair_partial_scored(
        place, layer_of, gathered, [own[1], *near, *far], 0, outs, outs_low[1], last_proj, ins
    )
    arrived = exchange(partial, "layer")
    total, copies = settle_scored(arrived, total)

    gathered = exchange(copies, "tensor", along_y)
    summed = gathered[:, 2 * width :].astype(F32).sum(axis=0).astype(BF16)
    every = exchange(
        jnp.broadcast_to(summed, (2 * n_dp, *summed.shape)), ("dp", "tensor"), along_dp_x
    )
    whole = every.reshape(n_dp, 2, rank // 4, 4, rank).astype(F32).sum(axis=1)
    whole = jnp.swapaxes(whole, 1, 2).reshape(n_dp, rank * rank).astype(BF16)
    scored = dot(whole, query_grads[0], NT)
    high = scored.astype(BF16)
    low = (scored - high.astype(F32)).astype(BF16)
    carried = jnp.concatenate([high, low], axis=1)[:, None, :]
    carried = jnp.broadcast_to(carried, (n_dp, 16, carried.shape[2]))
    partial = last_partial(place, gathered, [own[0], *near, *far], 1, total, carried)
    arrived = exchange(partial, ("tensor", "layer"), along_xz)
    input_grad = finish(arrived)
    ends = arrived.reshape(2, n_layer, *arrived.shape[1:])[:, :, width]
    ends = lax.dynamic_index_in_dim(ends, x, 0, keepdims=False).astype(F32).sum(axis=0)
    scores = (ends[: ends.shape[0] // 2] + ends[ends.shape[0] // 2 :])[None]
    return input_grad, scores


def solution(mesh):
    in_specs = (
        P(None, "dp", ("tensor", "layer")),
        P("dp", ("tensor", "layer")),
        P(None, "tensor", None, "layer", None),
        P(None, None, ("tensor", "layer")),
        P(None, None, ("tensor", "layer")),
        P("layer", ("dp", "tensor"), None),
        P(),
    )
    out_specs = (P("dp", ("tensor", "layer")), P("layer", ("dp", "tensor")))
    return jax.shard_map(
        on_device, mesh=mesh, in_specs=in_specs, out_specs=out_specs, check_vma=False
    )
```

time: 276 us -> 250 us (0.906)
  waiting for transfers between devices: 116 us -> 78.3 us
  Pallas kernels: 0 us -> 37.3 us
  matrix products: 32.1 us -> 5.11 us
  blocking collectives: 28.7 us -> 42.4 us
  starting transfers between devices: 45.1 us -> 37.7 us
  local copies, waits for them, and re-layouts: 45.1 us -> 42 us
    all_to_all x10 -> x6, waiting for transfers between devices: 116 us -> 73.6 us  [exchange(): lax.all_to_all(blocks, axes, 0, 0, tiled=True, axis_index_groups=groups)]
    pallas_call x0 -> x11, Pallas kernels: none -> 37.3 us  [the longest x8 24.3 us: local_call(): pl.pallas_call(body, in_specs=[SCALARS] * len(scalars) + [WIDE] * len(ope...]
    dot_general x14 -> x5, matrix products: 32.1 us -> 5.11 us  [dot(): return lax.dot_general(left, right, dims, preferred_element_type=F32)]
    all_to_all x10 -> x6, starting transfers between devices: 45.1 us -> 25.3 us  [exchange(): lax.all_to_all(blocks, axes, 0, 0, tiled=True, axis_index_groups=groups)]
    all_to_all x2 -> x3, blocking collectives: 28.7 us -> 42.4 us  [exchange(): lax.all_to_all(blocks, axes, 0, 0, tiled=True, axis_index_groups=groups)]
    ppermute x0 -> x10, starting transfers between devices: none -> 12.4 us  [the longest x3 4.98 us: on_device(): lax.ppermute(pair_proj[0], 'layer', [(z, z ^ k) for z in range(n_layer)])]
    unnamed x25 -> x69, local copies, waits for them, and re-layouts: 22.2 us -> 33.7 us
    slice x1 -> x5, local copies, waits for them, and re-layouts: 10.8 us -> 4.1 us  [the longest x1 1.6 us: on_device(): pair_proj[1]]
  transfers between devices with their start and end apart: 10 -> 16, of which waited for: 9 -> 8; matrix products, arithmetic and copies ran while one was open for 19% -> 7% of each run, Pallas kernels for 0% -> 9%
where the time goes in v3:
time: 250 us; the launch traced here: 248 us
  waiting for transfers between devices  78.3 us (31%)
  blocking collectives  42.4 us (17%)
  local copies, waits for them, and re-layouts  42 us (17%)
  starting transfers between devices  37.7 us (15%)
  Pallas kernels  37.3 us (15%)
  matrix products  5.11 us (2%)
  other arithmetic  4.23 us (2%)
    all_to_all x6, waiting for transfers between devices, exchange(): lax.all_to_all(blocks, axes, 0, 0, tiled=True, axis_index_groups=groups)  73.6 us
    all_to_all x3, blocking collectives, exchange(): lax.all_to_all(blocks, axes, 0, 0, tiled=True, axis_index_groups=groups)  42.4 us
    unnamed x69, local copies, waits for them, and re-layouts  33.7 us
    all_to_all x6, starting transfers between devices, exchange(): lax.all_to_all(blocks, axes, 0, 0, tiled=True, axis_index_groups=groups)  25.3 us
    pallas_call x8, Pallas kernels, local_call(): pl.pallas_call(body, in_specs=[SCALARS] * len(scalars) + [WIDE] * len(ope...  24.3 us
    pallas_call x3, Pallas kernels, features_first(): pl.pallas_call(body, grid_spec=pltpu.PrefetchScalarGridSpec(num_scalar_pr...  13 us
    dot_general x5, matrix products, dot(): return lax.dot_general(left, right, dims, preferred_element_type=F32)  5.11 us
  transfers between devices with their start and end apart: 16, of which 8 were waited for; matrix products, arithmetic and copies ran while one was open for 7% of the time, Pallas kernels for 9%

profile of v3, /device:TPU:0, one launch (start us, length us, event | category | flops | bytes accessed | tf_op | source)
XLA Modules:
  0.0 248.2 jit_solution(14994651813695320761)
XLA Ops:
  0.6 1.7 collective-permute-start
  2.3 2.4 broadcast_in_dim.37
  4.7 4.5 %all-to-all-start = ((bf16[8,512,256]{2,1,0:T(8,128)(2,1)}), bf16[8,512,256]{2,1,0:T(8,128)(2,1)S(1)}, u32[]{:S(2)}, u32[]{:S(2)}) async-start(bf16[8,512,256]{2,1,0:T(8,128)(2,1)} %broadcast_in_dim.37), calls=%async_computation | async-start | bytes 4194304 | tf_op jit(solution)/shard_map/all_to_all | solution.py:324
  9.2 4.1 %shard_map.87 = (bf16[8,1024,256]{2,1,0:T(8,128)(2,1)S(1)}, bf16[1,4,1024,256]{3,2,1,0:T(8,128)(2,1)}) custom-call(s32[1]{0:T(128)} %bitcast.1.core_ref, bf16[4,1024,8,256]{3,2,1,0:T(8,128)(2,1)} %bitcast.84), custom_call_target="tpu_custom_call" | custom-call | bytes 10485760 | tf_op jit(solution)/shard_map/pallas_call | solution.py:66
  13.2 2.0 copy-done.9
  15.3 3.5 %collective-permute-start.4 = (bf16[1,4,1024,256]{3,2,1,0:T(8,128)(2,1)}, bf16[1,4,1024,256]{3,2,1,0:T(8,128)(2,1)}, u32[]{:S(2)}, u32[]{:S(2)}) collective-permute-start(bf16[1,4,1024,256]{3,2,1,0:T(8,128)(2,1)} %get-tuple-element.46), channel_id=1, source_target_pairs={{0,68},{4,64},{8,76},{12,72},{16,84},{20,80},{24,92},{28,88},{32,1... | collective-permute-start | bytes 6291464 | tf_op jit(solution)/shard_map/ppermute | solution.py:362
  18.8 1.2 fusion.1
  20.0 3.1 %shard_map.88.w_ref = bf16[8,1024,256]{2,1,0:T(8,128)(2,1)S(1)} custom-call(s32[1]{0:T(128)} %bitcast.1.core_ref, bf16[4,1024,8,256]{3,2,1,0:T(8,128)(2,1)} %bitcast.85), custom_call_target="tpu_custom_call" | custom-call | bytes 10485760 | tf_op jit(solution)/shard_map/pallas_call | solution.py:66
  23.2 1.9 copy-done.11
  25.1 5.8 %shard_map.86 = (bf16[8,1024,256]{2,1,0:T(8,128)(2,1)S(1)}, bf16[8,1024,256]{2,1,0:T(8,128)(2,1)S(1)}, bf16[2,2,1024,256]{3,2,1,0:T(8,128)(2,1)S(1)}, bf16[2,2,1024,256]{3,2,1,0:T(8,128)(2,1)S(1)}) custom-call(s32[1]{0:T(128)} %bitcast.1.core_ref, bf16[4,1024,8,256]{3,2,1,0:T(8,128)(2,1)} %bitcast.86), custom_call_target="tpu_custom_call" | custom-call | bytes 20971520 | tf_op jit(solution)/shard_map/pallas_call | solution.py:66
  31.0 2.0 copy-done.5
  32.9 2.0 copy-done.7
  35.0 1.3 copy-done.27
  36.3 1.3 copy-done.28
  37.6 1.2 fusion
  38.8 1.2 fusion.3
  40.0 1.2 fusion.2
  41.3 4.0 %collective-permute-start.2 = (bf16[2,64,256]{2,1,0:T(8,128)(2,1)S(1)}, bf16[2,64,256]{2,1,0:T(8,128)(2,1)S(1)}, u32[]{:S(2)}, u32[]{:S(2)}) collective-permute-start(bf16[2,64,256]{2,1,0:T(8,128)(2,1)S(1)} %slice_bitcast_fusion.2), channel_id=1, source_target_pairs={{0,2},{1,3},{2,0},{3,1},{4,6},{5,7},{6,4},{7,5},{8,10},{9,11},{10,... | collective-permute-start | bytes 196616 | tf_op jit(solution)/shard_map/ppermute | solution.py:370
  47.9 1.7 collective-permute-done.1
  49.6 2.2 collective-permute-done.3
  52.0 2.2 copy-done.12
  55.1 2.4 shard_map.89
  58.5 4.3 %all-to-all-start.1 = ((bf16[8,320,256]{2,1,0:T(8,128)(2,1)}), bf16[8,320,256]{2,1,0:T(8,128)(2,1)}, u32[]{:S(2)}, u32[]{:S(2)}) async-start(bf16[8,320,256]{2,1,0:T(8,128)(2,1)} %copy-done.13), calls=%async_computation.1 | async-start | bytes 2621440 | tf_op jit(solution)/shard_map/all_to_all | solution.py:324
  62.9 1.6 fusion.22
  64.5 13.8 %all-to-all-done.1.r_ref = bf16[8,320,256]{2,1,0:T(8,128)(2,1)} async-done(((bf16[8,320,256]{2,1,0:T(8,128)(2,1)}), bf16[8,320,256]{2,1,0:T(8,128)(2,1)}, u32[]{:S(2)}, u32[]{:S(2)}) %all-to-all-start.1) | async-done | bytes 1310752 | tf_op jit(solution)/shard_map/all_to_all | solution.py:324
  78.3 1.7 shard_map.90
  82.4 4.3 %all-to-all-start.2 = ((bf16[4,576,256]{2,1,0:T(8,128)(2,1)}), bf16[4,576,256]{2,1,0:T(8,128)(2,1)}, u32[]{:S(2)}, u32[]{:S(2)}) async-start(bf16[4,576,256]{2,1,0:T(8,128)(2,1)} %copy-done.14), calls=%async_computation.2 | async-start | bytes 2359296 | tf_op jit(solution)/shard_map/all_to_all | solution.py:324
  87.0 1.4 collective-permute-start.7
  88.4 15.8 %all-to-all-done.2.g_ref = bf16[4,576,256]{2,1,0:T(8,128)(2,1)} async-done(((bf16[4,576,256]{2,1,0:T(8,128)(2,1)}), bf16[4,576,256]{2,1,0:T(8,128)(2,1)}, u32[]{:S(2)}, u32[]{:S(2)}) %all-to-all-start.2) | async-done | bytes 1179680 | tf_op jit(solution)/shard_map/all_to_all | solution.py:324
  105.2 2.2 copy-done.10
  107.4 4.9 %shard_map.91 = bf16[4,576,256]{2,1,0:T(8,128)(2,1)S(1)} custom-call(s32[4]{0:T(128)S(1)} %pad_add_fusion.s_ref, bf16[4,576,256]{2,1,0:T(8,128)(2,1)} %all-to-all-done.2.g_ref, bf16[8,1024,256]{2,1,0:T(8,128)(2,1)S(1)} %copy-done.10, bf16[1,4,1024,256]{3,2,1,0:T(8,128)(2,1)} %collective-permute-done.4.refs_1_, ...), custom_call_target="tpu_custom_call" | custom-call | flops 2147483648 | bytes 8388608 | tf_op jit(solution)/shard_map/pallas_call | solution.py:33
  113.3 4.3 %all-to-all-start.3 = ((bf16[4,576,256]{2,1,0:T(8,128)(2,1)}), bf16[4,576,256]{2,1,0:T(8,128)(2,1)}, u32[]{:S(2)}, u32[]{:S(2)}) async-start(bf16[4,576,256]{2,1,0:T(8,128)(2,1)} %copy-done.1), calls=%async_computation.3 | async-start | bytes 2359296 | tf_op jit(solution)/shard_map/all_to_all | solution.py:324
  118.5 1.4 fusion.23
  119.9 14.4 %all-to-all-done.3.r_ref = bf16[4,576,256]{2,1,0:T(8,128)(2,1)} async-done(((bf16[4,576,256]{2,1,0:T(8,128)(2,1)}), bf16[4,576,256]{2,1,0:T(8,128)(2,1)}, u32[]{:S(2)}, u32[]{:S(2)}) %all-to-all-start.3) | async-done | bytes 1179680 | tf_op jit(solution)/shard_map/all_to_all | solution.py:324
  135.4 1.6 shard_map.92
  140.3 4.4 %all-to-all-start.4 = ((bf16[4,512,256]{2,1,0:T(8,128)(2,1)}), bf16[4,512,256]{2,1,0:T(8,128)(2,1)}, u32[]{:S(2)}, u32[]{:S(2)}) async-start(bf16[4,512,256]{2,1,0:T(8,128)(2,1)} %copy-done.15), calls=%async_computation.4 | async-start | bytes 2097152 | tf_op jit(solution)/shard_map/all_to_all | solution.py:324
  144.9 1.5 slice_bitcast_fusion.3.refs_6_
  146.3 13.9 %all-to-all-done.4.g_ref = bf16[4,512,256]{2,1,0:T(8,128)(2,1)} async-done(((bf16[4,512,256]{2,1,0:T(8,128)(2,1)}), bf16[4,512,256]{2,1,0:T(8,128)(2,1)}, u32[]{:S(2)}, u32[]{:S(2)}) %all-to-all-start.4) | async-done | bytes 1048608 | tf_op jit(solution)/shard_map/all_to_all | solution.py:324
  160.3 2.2 copy-done.8
  164.2 7.5 %shard_map.93 = (bf16[4,528,256]{2,1,0:T(8,128)(2,1)S(1)}, bf16[4,64,256]{2,1,0:T(8,128)(2,1)}) custom-call(s32[4]{0:T(128)S(1)} %pad_add_fusion.s_ref, s32[4]{0:T(128)S(1)} %select_reduce_fusion.l_ref, bf16[4,512,256]{2,1,0:T(8,128)(2,1)} %all-to-all-done.4.g_ref, bf16[8,1024,256]{2,1,0:T(8,128)(2,1)S(1)} %copy-done.8, ...), custom_call_target="tpu_custom_call" | custom-call | flops 2147483648 | bytes 8388608 | tf_op jit(solution)/shard_map/pallas_call | solution.py:33
  171.7 17.7 %all_to_all.45.r_ref = bf16[4,528,256]{2,1,0:T(8,128)(2,1)S(1)} all-to-all(bf16[4,528,256]{2,1,0:T(8,128)(2,1)S(1)} %get-tuple-element.63), channel_id=1, replica_groups=mesh['dp'=4,'tensor'=8,'layer'=4] {'layer'}, dimensions={0} | all-to-all | bytes 2162688 | tf_op jit(solution)/shard_map/all_to_all | solution.py:324
  190.3 16.6 %all_to_all.46.g_ref = bf16[4,528,256]{2,1,0:T(8,128)(2,1)S(1)} all-to-all(bf16[4,528,256]{2,1,0:T(8,128)(2,1)S(1)} %get-tuple-element.65), channel_id=1, replica_groups={{0,8,16,24},{4,12,20,28},{1,9,17,25},{5,13,21,29},{2,10,18,26},{6,14,22..., dimensions={0} | all-to-all | bytes 2162688 | tf_op jit(solution)/shard_map/all_to_all | solution.py:324
  207.9 8.2 %all_to_all.47 = bf16[8,16,256]{2,1,0:T(8,128)(2,1)S(1)} all-to-all(bf16[8,16,256]{2,1,0:T(8,128)(2,1)S(1)} %broadcast_in_dim.39), channel_id=1, replica_groups={{0,4,32,36,64,68,96,100},{8,12,40,44,72,76,104,108},{16,20,48,52,80,84,..., dimensions={0} | all-to-all | bytes 131072 | tf_op jit(solution)/shard_map/all_to_all | solution.py:324
  216.9 1.2 copy-done.3
  218.1 2.2 copy-done.6
  221.4 5.2 %shard_map.95 = bf16[8,272,256]{2,1,0:T(8,128)(2,1)S(1)} custom-call(s32[4]{0:T(128)S(1)} %pad_add_fusion.s_ref, bf16[4,528,256]{2,1,0:T(8,128)(2,1)S(1)} %copy-done.3, bf16[8,1024,256]{2,1,0:T(8,128)(2,1)S(1)} %copy-done.6, bf16[2,2,1024,256]{3,2,1,0:T(8,128)(2,1)S(1)} %collective-permute-done.6.refs_1_, ...), custom_call_target="tpu_custom_call" | custom-call | flops 2147483648 | bytes 8388608 | tf_op jit(solution)/shard_map/pallas_call | solution.py:33
  227.6 3.6 %all-to-all-start.8 = ((bf16[8,272,256]{2,1,0:T(8,128)(2,1)}), bf16[8,272,256]{2,1,0:T(8,128)(2,1)S(1)}, u32[]{:S(2)}, u32[]{:S(2)}) async-start(bf16[8,272,256]{2,1,0:T(8,128)(2,1)} %copy-done.4), calls=%async_computation.8 | async-start | bytes 2228224 | tf_op jit(solution)/shard_map/all_to_all | solution.py:324
  231.1 15.6 %all-to-all-done.8.r_ref = bf16[8,272,256]{2,1,0:T(8,128)(2,1)S(1)} async-done(((bf16[8,272,256]{2,1,0:T(8,128)(2,1)}), bf16[8,272,256]{2,1,0:T(8,128)(2,1)S(1)}, u32[]{:S(2)}, u32[]{:S(2)}) %all-to-all-start.8) | async-done | bytes 1114144 | tf_op jit(solution)/shard_map/all_to_all | solution.py:324
  (101 shorter events, 22.9 us)
Async XLA Ops:
  0.6 215.8 %copy-start = (bf16[1,128,4096]{2,1,0:T(8,128)(2,1)S(1)}, bf16[1,128,4096]{2,1,0:T(8,128)(2,1)}, u32[]{:S(2)}) copy-start(bf16[1,128,4096]{2,1,0:T(8,128)(2,1)} %param.12) | copy-start | bytes 3145732
  0.6 40.6 %collective-permute-start = (bf16[4,64,256]{2,1,0:T(8,128)(2,1)}, bf16[4,64,256]{2,1,0:T(8,128)(2,1)S(1)}, u32[]{:S(2)}, u32[]{:S(2)}) collective-permute-start(bf16[4,64,256]{2,1,0:T(8,128)(2,1)} %param.11), channel_id=1, source_target_pairs={{0,4},{4,0},{8,12},{12,8},{16,20},{20,16},{24,28},{28,24},{1,5},{5... | collective-permute-start | bytes 393224 | tf_op jit(solution)/shard_map/ppermute | solution.py:365
  4.7 47.2 %all-to-all-start = ((bf16[8,512,256]{2,1,0:T(8,128)(2,1)}), bf16[8,512,256]{2,1,0:T(8,128)(2,1)S(1)}, u32[]{:S(2)}, u32[]{:S(2)}) async-start(bf16[8,512,256]{2,1,0:T(8,128)(2,1)} %broadcast_in_dim.37), calls=%async_computation | async-start | bytes 4194304 | tf_op jit(solution)/shard_map/all_to_all | solution.py:324
  13.2 2.1 copy-start.9
  15.3 67.1 %collective-permute-start.4 = (bf16[1,4,1024,256]{3,2,1,0:T(8,128)(2,1)}, bf16[1,4,1024,256]{3,2,1,0:T(8,128)(2,1)}, u32[]{:S(2)}, u32[]{:S(2)}) collective-permute-start(bf16[1,4,1024,256]{3,2,1,0:T(8,128)(2,1)} %get-tuple-element.46), channel_id=1, source_target_pairs={{0,68},{4,64},{8,76},{12,72},{16,84},{20,80},{24,92},{28,88},{32,1... | collective-permute-start | bytes 6291464 | tf_op jit(solution)/shard_map/ppermute | solution.py:362
  23.2 1.9 copy-start.11
  31.0 2.0 copy-start.5
  32.9 2.0 copy-start.7
  34.9 1.3 copy-start.27
  36.3 1.3 copy-start.28
  37.6 3.7 %copy-start.30 = (bf16[4,64,256]{2,1,0:T(8,128)(2,1)S(1)}, bf16[4,64,256]{2,1,0:T(8,128)(2,1)}, u32[]{:S(2)}) copy-start(bf16[4,64,256]{2,1,0:T(8,128)(2,1)} %param.11) | copy-start | bytes 393220
  41.3 10.6 %copy-start.29 = (bf16[4,2,64,256]{3,2,1,0:T(8,128)(2,1)}, bf16[4,2,64,256]{3,2,1,0:T(8,128)(2,1)S(1)}, u32[]{:S(2)}) copy-start(bf16[4,2,64,256]{3,2,1,0:T(8,128)(2,1)S(1)} %maximum_select_fusion) | copy-start | bytes 786436
  41.3 6.5 %collective-permute-start.2 = (bf16[2,64,256]{2,1,0:T(8,128)(2,1)S(1)}, bf16[2,64,256]{2,1,0:T(8,128)(2,1)S(1)}, u32[]{:S(2)}, u32[]{:S(2)}) collective-permute-start(bf16[2,64,256]{2,1,0:T(8,128)(2,1)S(1)} %slice_bitcast_fusion.2), channel_id=1, source_target_pairs={{0,2},{1,3},{2,0},{3,1},{4,6},{5,7},{6,4},{7,5},{8,10},{9,11},{10,... | collective-permute-start | bytes 196616 | tf_op jit(solution)/shard_map/ppermute | solution.py:370
  45.3 4.3 %collective-permute-start.1 = (bf16[2,64,256]{2,1,0:T(8,128)(2,1)S(1)}, bf16[2,64,256]{2,1,0:T(8,128)(2,1)S(1)}, u32[]{:S(2)}, u32[]{:S(2)}) collective-permute-start(bf16[2,64,256]{2,1,0:T(8,128)(2,1)S(1)} %slice_bitcast_fusion.2), channel_id=1, source_target_pairs={{0,1},{1,0},{2,3},{3,2},{4,5},{5,4},{6,7},{7,6},{8,9},{9,8},{10,11... | collective-permute-start | bytes 196616 | tf_op jit(solution)/shard_map/ppermute | solution.py:370
  46.3 5.5 %collective-permute-start.3 = (bf16[2,64,256]{2,1,0:T(8,128)(2,1)S(1)}, bf16[2,64,256]{2,1,0:T(8,128)(2,1)S(1)}, u32[]{:S(2)}, u32[]{:S(2)}) collective-permute-start(bf16[2,64,256]{2,1,0:T(8,128)(2,1)S(1)} %slice_bitcast_fusion.2), channel_id=1, source_target_pairs={{0,3},{1,2},{2,1},{3,0},{4,7},{5,6},{6,5},{7,4},{8,11},{9,10},{10,... | collective-permute-start | bytes 196616 | tf_op jit(solution)/shard_map/ppermute | solution.py:370
  52.0 2.2 copy-start.12
  54.1 0.9 copy-start.24
  57.4 1.1 copy-start.13
  58.5 19.7 %all-to-all-start.1 = ((bf16[8,320,256]{2,1,0:T(8,128)(2,1)}), bf16[8,320,256]{2,1,0:T(8,128)(2,1)}, u32[]{:S(2)}, u32[]{:S(2)}) async-start(bf16[8,320,256]{2,1,0:T(8,128)(2,1)} %copy-done.13), calls=%async_computation.1 | async-start | bytes 2621440 | tf_op jit(solution)/shard_map/all_to_all | solution.py:324
  80.0 1.0 copy-start.14
  81.0 0.8 copy-start.16
  82.4 22.7 %collective-permute-start.5 = (bf16[1,4,1024,256]{3,2,1,0:T(8,128)(2,1)}, bf16[1,4,1024,256]{3,2,1,0:T(8,128)(2,1)}, u32[]{:S(2)}, u32[]{:S(2)}) collective-permute-start(bf16[1,4,1024,256]{3,2,1,0:T(8,128)(2,1)} %collective-permute-done.4.refs_1_), channel_id=1, source_target_pairs={{0,32},{32,0},{64,96},{96,64},{1,33},{33,1},{65,97},{97,65},{2,34}... | collective-permute-start | bytes 6291464 | tf_op jit(solution)/shard_map/ppermute | solution.py:398
  82.4 21.8 %all-to-all-start.2 = ((bf16[4,576,256]{2,1,0:T(8,128)(2,1)}), bf16[4,576,256]{2,1,0:T(8,128)(2,1)}, u32[]{:S(2)}, u32[]{:S(2)}) async-start(bf16[4,576,256]{2,1,0:T(8,128)(2,1)} %copy-done.14), calls=%async_computation.2 | async-start | bytes 2359296 | tf_op jit(solution)/shard_map/all_to_all | solution.py:324
  86.7 53.0 %collective-permute-start.6 = (bf16[2,2,1024,256]{3,2,1,0:T(8,128)(2,1)}, bf16[2,2,1024,256]{3,2,1,0:T(8,128)(2,1)S(1)}, u32[]{:S(2)}, u32[]{:S(2)}) collective-permute-start(bf16[2,2,1024,256]{3,2,1,0:T(8,128)(2,1)} %copy-done.28), channel_id=1, source_target_pairs={{0,68},{4,64},{8,76},{12,72},{16,84},{20,80},{24,92},{28,88},{32,1... | collective-permute-start | bytes 6291464 | tf_op jit(solution)/shard_map/ppermute | solution.py:394
  87.0 52.7 %collective-permute-start.7 = (bf16[2,2,1024,256]{3,2,1,0:T(8,128)(2,1)}, bf16[2,2,1024,256]{3,2,1,0:T(8,128)(2,1)}, u32[]{:S(2)}, u32[]{:S(2)}) collective-permute-start(bf16[2,2,1024,256]{3,2,1,0:T(8,128)(2,1)} %copy-done.27), channel_id=1, source_target_pairs={{0,4},{4,0},{8,12},{12,8},{16,20},{20,16},{24,28},{28,24},{1,5},{5... | collective-permute-start | bytes 6291464 | tf_op jit(solution)/shard_map/ppermute | solution.py:395
  105.2 2.2 copy-start.10
  112.3 1.0 copy-start.1
  113.3 21.0 %all-to-all-start.3 = ((bf16[4,576,256]{2,1,0:T(8,128)(2,1)}), bf16[4,576,256]{2,1,0:T(8,128)(2,1)}, u32[]{:S(2)}, u32[]{:S(2)}) async-start(bf16[4,576,256]{2,1,0:T(8,128)(2,1)} %copy-done.1), calls=%async_computation.3 | async-start | bytes 2359296 | tf_op jit(solution)/shard_map/all_to_all | solution.py:324
  134.3 1.0 copy-start.17
  135.3 3.7 %copy-start.31 = (bf16[1,64,256]{2,1,0:T(8,128)(2,1)S(1)}, bf16[1,64,256]{2,1,0:T(8,128)(2,1)}, u32[]{:S(2)}) copy-start(bf16[1,64,256]{2,1,0:T(8,128)(2,1)} %get-tuple-element.79) | copy-start | bytes 98308
  135.4 3.7 %copy-start.32 = (bf16[1,64,256]{2,1,0:T(8,128)(2,1)S(1)}, bf16[1,64,256]{2,1,0:T(8,128)(2,1)}, u32[]{:S(2)}) copy-start(bf16[1,64,256]{2,1,0:T(8,128)(2,1)} %get-tuple-element.80) | copy-start | bytes 98308
  135.4 9.4 %copy-start.33 = (s32[4]{0:T(128)S(1)}, s32[4]{0:T(128)}, u32[]{:S(2)}) copy-start(s32[4]{0:T(128)} %param.13) | copy-start | bytes 52
  136.9 1.0 copy-start.15
  137.9 1.8 copy-start.18
  137.9 1.8 copy-start.25
  139.7 20.5 %collective-permute-start.8 = (bf16[2,2,1024,256]{3,2,1,0:T(8,128)(2,1)S(1)}, bf16[2,2,1024,256]{3,2,1,0:T(8,128)(2,1)}, u32[]{:S(2)}, u32[]{:S(2)}) collective-permute-start(bf16[2,2,1024,256]{3,2,1,0:T(8,128)(2,1)S(1)} %collective-permute-done.6.refs_1_), channel_id=1, source_target_pairs={{0,32},{32,0},{64,96},{96,64},{1,33},{33,1},{65,97},{97,65},{2,34}... | collective-permute-start | bytes 6291464 | tf_op jit(solution)/shard_map/ppermute | solution.py:410
  139.8 20.4 %collective-permute-start.9 = (bf16[2,2,1024,256]{3,2,1,0:T(8,128)(2,1)}, bf16[2,2,1024,256]{3,2,1,0:T(8,128)(2,1)}, u32[]{:S(2)}, u32[]{:S(2)}) collective-permute-start(bf16[2,2,1024,256]{3,2,1,0:T(8,128)(2,1)} %collective-permute-done.7.refs_2_), channel_id=1, source_target_pairs={{0,32},{32,0},{64,96},{96,64},{1,33},{33,1},{65,97},{97,65},{2,34}... | collective-permute-start | bytes 6291464 | tf_op jit(solution)/shard_map/ppermute | solution.py:410
  140.3 19.9 %all-to-all-start.4 = ((bf16[4,512,256]{2,1,0:T(8,128)(2,1)}), bf16[4,512,256]{2,1,0:T(8,128)(2,1)}, u32[]{:S(2)}, u32[]{:S(2)}) async-start(bf16[4,512,256]{2,1,0:T(8,128)(2,1)} %copy-done.15), calls=%async_computation.4 | async-start | bytes 2097152 | tf_op jit(solution)/shard_map/all_to_all | solution.py:324
  160.3 2.2 copy-start.8
  162.5 0.9 copy-start.22
  163.4 0.8 copy-start.23
  171.7 17.7 %copy-start.19 = (f32[512,256]{1,0:T(8,128)S(1)}, f32[512,256]{1,0:T(8,128)}, u32[]{:S(2)}) copy-start(f32[512,256]{1,0:T(8,128)} %copy-done.18) | copy-start | bytes 1572868
  206.9 1.0 copy-start.2
  216.9 1.2 copy-start.3
  218.1 2.2 copy-start.6
  220.3 1.0 copy-start.21
  226.6 1.0 copy-start.4
  227.6 19.2 %all-to-all-start.8 = ((bf16[8,272,256]{2,1,0:T(8,128)(2,1)}), bf16[8,272,256]{2,1,0:T(8,128)(2,1)S(1)}, u32[]{:S(2)}, u32[]{:S(2)}) async-start(bf16[8,272,256]{2,1,0:T(8,128)(2,1)} %copy-done.4), calls=%async_computation.8 | async-start | bytes 2228224 | tf_op jit(solution)/shard_map/all_to_all | solution.py:324
  (2 other events, 1.4 us)

commit v4 on v3

v4 whole, which is shorter than its diff:
```python
import jax
import jax.numpy as jnp
from jax import lax
from jax.experimental import pallas as pl
from jax.experimental.pallas import tpu as pltpu
from jax.sharding import PartitionSpec as P

NT = (((1,), (1,)), ((), ()))
NN = (((1,), (0,)), ((), ()))
F32 = jnp.float32
BF16 = jnp.bfloat16
WIDE = pl.BlockSpec(memory_space=pltpu.VMEM)
SCALARS = pl.BlockSpec(memory_space=pltpu.SMEM)
after = lax.optimization_barrier


def limit(mib):
    return pltpu.CompilerParams(vmem_limit_bytes=mib << 20)


def dot(left, right, dims=NN):
    return lax.dot_general(left, right, dims, preferred_element_type=F32)


def sum_of(terms):
    total = None
    for term in terms:
        total = term if total is None else total + term
    return total


def in_hbm(value):
    return pltpu.with_memory_space_constraint(value, pltpu.HBM)


def local_call(body, outs, operands, scalars=(), cost=None):
    return pl.pallas_call(
        body,
        in_specs=[SCALARS] * len(scalars) + [WIDE] * len(operands),
        out_specs=[WIDE] * len(outs),
        out_shape=[jax.ShapeDtypeStruct(*out) for out in outs],
        compiler_params=limit(8),
        cost_estimate=cost,
    )(*scalars, *operands)


def streamed_call(body, outs, weights, operands, scalars, scratch=()):
    rows, width = weights[0].shape[1:]
    tokens = operands[0].shape[-1]
    cells = sum(w.shape[0] for w in weights)
    return pl.pallas_call(
        body,
        grid=(rows // width,),
        in_specs=[SCALARS] * len(scalars)
        + [pl.BlockSpec((w.shape[0], width, width), lambda n: (0, n, 0)) for w in weights]
        + [WIDE] * len(operands),
        out_specs=[WIDE] * len(outs),
        out_shape=[jax.ShapeDtypeStruct(*out) for out in outs],
        scratch_shapes=list(scratch),
        compiler_params=limit(24),
        cost_estimate=pl.CostEstimate(
            flops=2 * cells * width * rows * tokens,
            bytes_accessed=2 * cells * width * rows,
            transcendentals=0,
        ),
    )(*scalars, *weights, *operands)


def features_first(weights, level, core, pieces):
    _, rows, cells, width = weights.shape
    step, half = 512, cells // 2
    deep = half // max(pieces, 1)

    def body(core_ref, w_ref, o_ref, *s_refs):
        o_ref[...] = jnp.swapaxes(w_ref[0], 0, 1)
        for i, s_ref in enumerate(s_refs):
            s_ref[...] = o_ref[pl.ds(half * core_ref[0] + deep * i, deep)]

    depths = [cells] + [deep] * pieces
    parts = pl.pallas_call(
        body,
        grid_spec=pltpu.PrefetchScalarGridSpec(
            num_scalar_prefetch=1,
            grid=(rows // step,),
            in_specs=[pl.BlockSpec((1, step, cells, width), lambda n, c: (level, n, 0, 0))],
            out_specs=[pl.BlockSpec((k, step, width), lambda n, c: (0, n, 0)) for k in depths],
        ),
        out_shape=[pltpu.HBM((k, rows, width), weights.dtype) for k in depths],
        compiler_params=limit(16),
        cost_estimate=pl.CostEstimate(
            flops=0, bytes_accessed=5 * rows * cells * width, transcendentals=0
        ),
    )(core, weights)
    return in_hbm(parts[0]), [in_hbm(part) for part in parts[1:]]


def in_factor_parts(saved_inputs, proj_in):
    layers, tokens, width = saved_inputs.shape
    rank = proj_in.shape[1]
    half = tokens // 2

    def body(x_ref, p_ref, o_ref):
        for h in range(2):
            part = dot(p_ref[0], x_ref[0, h * half : (h + 1) * half], NT)
            o_ref[h, 0] = part.astype(o_ref.dtype)

    return pl.pallas_call(
        body,
        grid=(layers,),
        in_specs=[
            pl.BlockSpec((1, tokens, width), lambda k: (k, 0, 0)),
            pl.BlockSpec((1, rank, width), lambda k: (k, 0, 0)),
        ],
        out_specs=pl.BlockSpec((2, 1, rank, half), lambda k: (0, k, 0, 0)),
        out_shape=jax.ShapeDtypeStruct((2, layers, rank, half), BF16),
        compiler_params=limit(8),
        cost_estimate=pl.CostEstimate(
            flops=2 * layers * tokens * width * rank,
            bytes_accessed=2 * layers * tokens * width,
            transcendentals=0,
        ),
    )(saved_inputs, proj_in).reshape(2 * layers, rank, half)


def first_partial(gathered, weight, extra):
    cells, tokens, width = gathered.shape
    groups = weight.shape[1] // width
    half = tokens // 2

    def body(w_ref, g_ref, e_ref, o_ref):
        n = pl.program_id(0)
        for h in range(2):
            total = sum_of(
                dot(w_ref[a], g_ref[a, h * half : (h + 1) * half], NT) for a in range(cells)
            )
            o_ref[h * groups + n, :width] = total.astype(o_ref.dtype)

        @pl.when(n == 0)
        def _():
            o_ref[:, width:] = e_ref[...]

    return streamed_call(
        body,
        [((2 * groups, width + extra.shape[1], half), BF16)],
        [weight],
        [gathered, extra],
        [],
    )[0]


def pair_totals(s_ref, g_ref, w_refs):
    own_ref, *others = w_refs
    cells, _, width = own_ref.shape
    half = cells // 2
    deep = others[0].shape[0]
    pieces = half // deep
    x, core = s_ref[0], s_ref[1]
    yield x, sum_of(
        dot(own_ref[a], g_ref[a // 2, (a % 2) * width : (a % 2 + 1) * width]) for a in range(cells)
    )
    yield 1 - x, sum_of(
        dot(
            refs[i // deep][i % deep],
            g_ref[(half // 2) * first + i // 2, (i % 2) * width : (i % 2 + 1) * width],
        )
        for first, refs in ((core, others[:pieces]), (1 - core, others[pieces:]))
        for i in range(half)
    )


def pair_partial(place, gathered, held):
    width = held[0].shape[2]
    groups = held[0].shape[1] // width

    def body(s_ref, *refs):
        *w_refs, g_ref, o_ref = refs
        n = pl.program_id(0)
        for column, total in pair_totals(s_ref, g_ref, w_refs):
            start = pl.multiple_of(column * width, width)
            o_ref[n, pl.ds(start, width)] = total.astype(o_ref.dtype)

        @pl.when(n == 0)
        def _():
            whole = sum_of(g_ref[k, 2 * width :].astype(F32) for k in range(g_ref.shape[0]))
            for k in range(groups):
                o_ref[k, 2 * width :] = whole.astype(o_ref.dtype)

    return streamed_call(
        body, [((groups, *gathered.shape[1:]), BF16)], held, [gathered], [place]
    )[0]


def pair_partial_scored(place, layer_of, gathered, held, outs_top, outs_low, proj, ins):
    width = held[0].shape[2]
    groups = held[0].shape[1] // width
    layers, rank, tokens = ins.shape
    quarter = rank // 4

    def body(s_ref, l_ref, *refs):
        *w_refs, g_ref, a_ref, k_ref, p_ref, i_ref, o_ref, f_ref, last_ref = refs
        n = pl.program_id(0)

        @pl.when(n == 0)
        def _():
            f_ref[3] = a_ref[0]
            f_ref[2] = a_ref[1]
            f_ref[1] = k_ref[0].astype(f_ref.dtype)
            last_ref[...] = k_ref[1]

        for column, total in pair_totals(s_ref, g_ref, w_refs):
            start = pl.multiple_of(column * width, width)
            rounded = total.astype(o_ref.dtype)
            o_ref[n, pl.ds(start, width)] = rounded
            last_ref[...] += dot(p_ref[n, column], rounded)

        @pl.when(n == groups - 1)
        def _():
            f_ref[0] = last_ref[...].astype(f_ref.dtype)
            for o in range(layers):
                block = dot(f_ref[l_ref[o]], i_ref[l_ref[o]], NT).astype(o_ref.dtype)
                o_ref[o, 2 * width :] = jnp.concatenate(
                    [block[quarter * j : quarter * (j + 1)] for j in range(4)], axis=1
                )

    return streamed_call(
        body,
        [((groups, 2 * width + quarter, tokens), BF16)],
        held,
        [gathered, outs_top, outs_low, proj, ins],
        [place, layer_of],
        [pltpu.VMEM((layers, rank, tokens), BF16), pltpu.VMEM((rank, tokens), F32)],
    )[0]


def last_partial(place, gathered, held, kept, extra):
    width = held[0].shape[2]
    groups = held[0].shape[1] // width

    def body(s_ref, *refs):
        *w_refs, g_ref, t_ref, e_ref, o_ref = refs
        n = pl.program_id(0)
        for column, total in pair_totals(s_ref, g_ref, w_refs):
            start = pl.multiple_of(column * width, width)
            mine = t_ref[pl.ds(start, width)]
            total = total + jnp.where(n == s_ref[2], mine, jnp.zeros_like(mine))
            o_ref[groups * column + n, :width] = total.astype(o_ref.dtype)

        @pl.when(n == 0)
        def _():
            for k in range(2 * groups):
                o_ref[k, width:] = e_ref[k % groups]

    return streamed_call(
        body,
        [((2 * groups, width + extra.shape[1], gathered.shape[2]), BF16)],
        held,
        [gathered, kept, extra],
        [place],
    )[0]


def settle_first(place, arrived, gathered, proj_top, proj_next):
    blocks, deep, half = arrived.shape
    width = gathered.shape[2]
    groups = blocks // 2
    rank = proj_top.shape[1]

    def body(s_ref, r_ref, g_ref, p_ref, q_ref, t_ref, c_ref, o_ref):
        x, y = s_ref[0], s_ref[3]
        outs = [None, None]
        for k in range(2):
            start = g_ref[2 * y + k, pl.ds(pl.multiple_of(x * half, half), half)].astype(F32).T
            outs[0] = sum_of([*([outs[0]] if k else []), dot(p_ref[k], start.astype(BF16))])
            total = start + sum_of(r_ref[groups * k + z, :width].astype(F32) for z in range(groups))
            t_ref[k * width : (k + 1) * width] = total
            rounded = total.astype(BF16)
            outs[1] = sum_of([*([outs[1]] if k else []), dot(q_ref[k], rounded)])
            for j in range(c_ref.shape[0]):
                c_ref[j, k * width : (k + 1) * width] = rounded
        ins = sum_of(r_ref[k, width:].astype(F32) for k in range(blocks)).astype(BF16)
        for j in range(c_ref.shape[0]):
            c_ref[j, 2 * width :] = ins
        o_ref[0] = outs[0].astype(BF16)
        o_ref[1] = outs[1].astype(BF16)

    return local_call(
        body,
        [
            ((2 * width, half), F32),
            ((gathered.shape[0] // 2, 2 * width + deep - width, half), BF16),
            ((2, rank, half), BF16),
        ],
        [arrived, gathered, proj_top, proj_next],
        [place],
    )


def settle(arrived, total, proj_next, proj_last):
    groups, deep, half = arrived.shape
    depth = total.shape[0]
    width = depth // 2
    rank = proj_next.shape[1]

    def body(r_ref, t_ref, p_ref, q_ref, o_ref, c_ref, f_ref, i_ref):
        value = t_ref[...] + sum_of(r_ref[z, :depth].astype(F32) for z in range(groups))
        o_ref[...] = value
        rounded = value.astype(BF16)
        for j in range(c_ref.shape[0]):
            c_ref[j] = rounded
        for i, ref in enumerate((p_ref, q_ref)):
            f_ref[i] = dot(ref[0], rounded[:width]) + dot(ref[1], rounded[width:])
        i_ref[...] = r_ref[:, depth:]

    return local_call(
        body,
        [
            (total.shape, F32),
            ((groups, depth, half), BF16),
            ((2, rank, half), F32),
            ((groups, deep - depth, half), BF16),
        ],
        [arrived, total, proj_next, proj_last],
    )


def settle_scored(arrived, total):
    groups, deep, half = arrived.shape
    depth = total.shape[0]

    def body(r_ref, t_ref, o_ref, c_ref):
        value = t_ref[...] + sum_of(r_ref[z, :depth].astype(F32) for z in range(groups))
        o_ref[...] = value
        rounded = value.astype(BF16)
        blocks = sum_of(r_ref[z, depth:].astype(F32) for z in range(groups)).astype(BF16)
        for j in range(c_ref.shape[0]):
            c_ref[j, :depth] = rounded
            c_ref[j, depth:] = blocks

    return local_call(
        body, [(total.shape, F32), ((groups, deep, half), BF16)], [arrived, total]
    )


def finish(place, arrived):
    blocks, _, half = arrived.shape
    groups = blocks // 2
    width = half

    def body(s_ref, r_ref, o_ref, e_ref):
        for k in range(2):
            value = sum_of(r_ref[groups * k + z, :width].astype(F32) for z in range(groups))
            o_ref[k * half : (k + 1) * half] = value.T.astype(o_ref.dtype)
        ends = sum_of(r_ref[groups * s_ref[0] + z, width:].astype(F32) for z in range(groups))
        e_ref[...] = ends[:1, : half // 2] + ends[:1, half // 2 :]

    return local_call(
        body, [((2 * half, width), BF16), ((1, half // 2), F32)], [arrived], [place]
    )


def exchange(blocks, axes, groups=None):
    return lax.all_to_all(blocks, axes, 0, 0, tiled=True, axis_index_groups=groups)


def on_device(saved_inputs, output_grad, weights, proj_in, proj_out, query_grads, owner_map):
    layers, tokens, width = saved_inputs.shape
    rank = proj_in.shape[1]
    rows = weights.shape[1]
    n_dp, n_tensor, n_layer = (lax.axis_size(k) for k in ("dp", "tensor", "layer"))
    n_y = n_tensor // 2
    half = tokens // 2
    t, b = lax.axis_index("tensor"), lax.axis_index("layer")
    x, y = t & 1, t >> 1
    core = lax.axis_index("dp") & 1
    place = jnp.stack([x, core, b, y]).astype(jnp.int32)
    along_y = [[2 * k + j for k in range(n_y)] for j in range(2)]
    along_xz = [[2 * n_layer * k + j for j in range(2 * n_layer)] for k in range(n_y)]
    along_dp_x = [
        [d * n_tensor + 2 * k + j for d in range(n_dp) for j in range(2)] for k in range(n_y)
    ]
    across = [
        (d * n_tensor + k, (d ^ 2) * n_tensor + (k ^ 1)) for d in range(n_dp) for k in range(n_tensor)
    ]
    beside = [(k, k ^ 1) for k in range(n_tensor)]
    flat = pltpu.with_memory_space_constraint(
        weights.reshape(layers, rows, n_tensor, width), pltpu.HBM
    )
    owners = jnp.arange(n_layer, dtype=jnp.int32)
    layer_of = jnp.sum(
        owners[None, :] * (owner_map[None, :] == owners[:, None]).astype(jnp.int32), axis=1
    )

    gathered = exchange(
        jnp.broadcast_to(output_grad, (n_tensor, *output_grad.shape)), "tensor"
    )
    one = core.astype(jnp.int32).reshape(1)
    own, passed, near, far = ([None] * layers for _ in range(4))
    for level, pieces in ((2, 1), (3, 0), (1, 2), (0, 2)):
        own[level], passed[level] = features_first(flat, level, one, pieces)

    def over_both(values):
        return [
            in_hbm(lax.ppermute(values[0], ("dp", "tensor"), across)),
            in_hbm(lax.ppermute(values[1], "tensor", beside)),
        ]

    def to_other_core(values):
        return [in_hbm(lax.ppermute(v, "dp", [(d, d ^ 1) for d in range(n_dp)])) for v in values]

    near[2] = [in_hbm(lax.ppermute(passed[2][0], ("dp", "tensor"), across))]
    other_proj = lax.ppermute(proj_out, "tensor", beside)
    pair_proj = [
        jnp.where(x == 0, jnp.stack([p, q]), jnp.stack([q, p])) for p, q in zip(proj_out, other_proj)
    ]
    shifted = [pair_proj[0]] + [
        lax.ppermute(pair_proj[0], "layer", [(z, z ^ k) for z in range(n_layer)])
        for k in range(1, n_layer)
    ]
    last_proj = jnp.stack(
        [
            sum_of(jnp.where((b ^ k) == z, shifted[k], 0) for k in range(n_layer))
            for z in range(n_layer)
        ]
    ).astype(BF16)
    in_parts = in_factor_parts(saved_inputs, proj_in)
    gathered, own, passed, pair_proj, last_proj, in_parts, place, layer_of = after(
        (gathered, own, passed, pair_proj, last_proj, in_parts, place, layer_of)
    )

    partial = first_partial(gathered, own[3], in_parts)
    arrived = exchange(partial, ("tensor", "layer"), along_xz)
    total, copies, outs_top = settle_first(place, arrived, gathered, pair_proj[3], pair_proj[2])

    passed[1], _ = after((passed[1], total))
    near[1] = over_both(passed[1])
    near[2], _ = after((near[2], total))
    far[2] = to_other_core(near[2])
    gathered = exchange(copies, "tensor", along_y)
    partial = pair_partial(place, gathered, [own[2], *near[2], *far[2]])
    arrived = exchange(partial, "layer")
    total, copies, outs_low, ins = settle(arrived, total, pair_proj[1], pair_proj[0])

    near[1], _ = after((near[1], total))
    far[1] = to_other_core(near[1])
    passed[0], _ = after((passed[0], near[1]))
    near[0] = over_both(passed[0])
    gathered = exchange(copies, "tensor", along_y)
    far[1], gathered = after((far[1], gathered))
    partial = pair_partial_scored(
        place, layer_of, gathered, [own[1], *near[1], *far[1]], outs_top, outs_low, last_proj, ins
    )
    partial, near[0] = after((partial, near[0]))
    far[0] = to_other_core(near[0])
    arrived = exchange(partial, "layer")
    total, copies = settle_scored(arrived, total)

    gathered = exchange(copies, "tensor", along_y)
    summed = gathered[:, 2 * width :].astype(F32).sum(axis=0).astype(BF16)
    every = exchange(
        jnp.broadcast_to(summed, (2 * n_dp, *summed.shape)), ("dp", "tensor"), along_dp_x
    )
    whole = every.reshape(n_dp, 2, rank // 4, 4, rank).astype(F32).sum(axis=1)
    whole = jnp.swapaxes(whole, 1, 2).reshape(n_dp, rank * rank).astype(BF16)
    scored = dot(whole, query_grads[0], NT)
    high = scored.astype(BF16)
    low = (scored - high.astype(F32)).astype(BF16)
    carried = jnp.concatenate([high, low], axis=1)[:, None, :]
    carried = jnp.broadcast_to(carried, (n_dp, 16, carried.shape[2]))
    partial = last_partial(place, gathered, [own[0], *near[0], *far[0]], total, carried)
    arrived = exchange(partial, ("tensor", "layer"), along_xz)
    input_grad, scores = finish(place, arrived)
    return input_grad, scores


def solution(mesh):
    in_specs = (
        P(None, "dp", ("tensor", "layer")),
        P("dp", ("tensor", "layer")),
        P(None, "tensor", None, "layer", None),
        P(None, None, ("tensor", "layer")),
        P(None, None, ("tensor", "layer")),
        P("layer", ("dp", "tensor"), None),
        P(),
    )
    out_specs = (P("dp", ("tensor", "layer")), P("layer", ("dp", "tensor")))
    return jax.shard_map(
        on_device, mesh=mesh, in_specs=in_specs, out_specs=out_specs, check_vma=False
    )
```

time: 250 us -> 222 us (0.89)
  blocking collectives: 42.4 us -> 101 us
  waiting for transfers between devices: 78.3 us -> 34.9 us
  local copies, waits for them, and re-layouts: 42 us -> 9.93 us
  starting transfers between devices: 37.7 us -> 28.1 us
  Pallas kernels: 37.3 us -> 44.3 us
  matrix products: 5.11 us -> 0.37 us
  other arithmetic: 4.23 us -> 1.71 us
    all_to_all x3 -> x6, blocking collectives: 42.4 us -> 101 us  [exchange(): lax.all_to_all(blocks, axes, 0, 0, tiled=True, axis_index_groups=groups)]
    all_to_all x6 -> x3, waiting for transfers between devices: 73.6 us -> 27.4 us  [exchange(): lax.all_to_all(blocks, axes, 0, 0, tiled=True, axis_index_groups=groups)]
    unnamed x69 -> x49, local copies, waits for them, and re-layouts: 33.7 us -> 6.49 us
    pallas_call x0 -> x5, Pallas kernels: none -> 22.6 us  [the longest x4 21.8 us: streamed_call(): pl.pallas_call(body, grid=(rows // width,), in_specs=[SCALARS] * len(scal...]
    pallas_call x8 -> x4, Pallas kernels: 24.3 us -> 2.82 us  [local_call(): pl.pallas_call(body, in_specs=[SCALARS] * len(scalars) + [WIDE] * len(ope...]
    all_to_all x6 -> x3, starting transfers between devices: 25.3 us -> 13.1 us  [exchange(): lax.all_to_all(blocks, axes, 0, 0, tiled=True, axis_index_groups=groups)]
    pallas_call x3 -> x4, Pallas kernels: 13 us -> 18.8 us  [features_first(): pl.pallas_call(body, grid_spec=pltpu.PrefetchScalarGridSpec(num_scalar_pr...]
    dot_general x5 -> x1, matrix products: 5.11 us -> 0.37 us  [dot(): return lax.dot_general(left, right, dims, preferred_element_type=F32)]
  transfers between devices with their start and end apart: 16 -> 17, of which waited for: 8 -> 5; matrix products, arithmetic and copies ran while one was open for 7% -> 1% of each run, Pallas kernels for 9% -> 17%
where the time goes in v4:
time: 222 us; the launch traced here: 221 us
  blocking collectives  101 us (45%)
  Pallas kernels  44.3 us (20%)
  waiting for transfers between devices  34.9 us (16%)
  starting transfers between devices  28.1 us (13%)
  local copies, waits for them, and re-layouts  9.93 us (4%)
    all_to_all x6, blocking collectives, exchange(): lax.all_to_all(blocks, axes, 0, 0, tiled=True, axis_index_groups=groups)  101 us
    all_to_all x3, waiting for transfers between devices, exchange(): lax.all_to_all(blocks, axes, 0, 0, tiled=True, axis_index_groups=groups)  27.4 us
    pallas_call x4, Pallas kernels, streamed_call(): pl.pallas_call(body, grid=(rows // width,), in_specs=[SCALARS] * len(scal...  21.8 us
    pallas_call x4, Pallas kernels, features_first(): pl.pallas_call(body, grid_spec=pltpu.PrefetchScalarGridSpec(num_scalar_pr...  18.8 us
    all_to_all x3, starting transfers between devices, exchange(): lax.all_to_all(blocks, axes, 0, 0, tiled=True, axis_index_groups=groups)  13.1 us
    unnamed x49, local copies, waits for them, and re-layouts  6.49 us
    ppermute x3, starting transfers between devices, on_device(): lax.ppermute(pair_proj[0], 'layer', [(z, z ^ k) for z in range(n_layer)])  5.07 us
  transfers between devices with their start and end apart: 17, of which 5 were waited for; matrix products, arithmetic and copies ran while one was open for 1% of the time, Pallas kernels for 17%

profile of v4, /device:TPU:0, one launch (start us, length us, event | category | flops | bytes accessed | tf_op | source)
XLA Modules:
  0.0 220.8 jit_solution(3561514650839331946)
XLA Ops:
  0.6 2.5 %broadcast_in_dim.34 = bf16[8,512,256]{2,1,0:T(8,128)(2,1)} broadcast(bf16[512,256]{1,0:T(8,128)(2,1)} %param.8), dimensions={1,2} | broadcast | bytes 2359296 | tf_op jit(solution)/shard_map/broadcast_in_dim | solution.py:394
  3.2 5.6 %all-to-all-start = ((bf16[8,512,256]{2,1,0:T(8,128)(2,1)}), bf16[8,512,256]{2,1,0:T(8,128)(2,1)S(1)}, u32[]{:S(2)}, u32[]{:S(2)}) async-start(bf16[8,512,256]{2,1,0:T(8,128)(2,1)} %broadcast_in_dim.34), calls=%async_computation | async-start | bytes 4194304 | tf_op jit(solution)/shard_map/all_to_all | solution.py:362
  8.8 2.0 collective-permute-start
  10.8 4.8 %shard_map.88 = (bf16[8,1024,256]{2,1,0:T(8,128)(2,1)}, bf16[4,1024,256]{2,1,0:T(8,128)(2,1)}) custom-call(s32[1]{0:T(128)} %bitcast.core_ref, bf16[4,1024,8,256]{3,2,1,0:T(8,128)(2,1)} %bitcast.26), custom_call_target="tpu_custom_call" | custom-call | bytes 10485760 | tf_op jit(solution)/shard_map/pallas_call | solution.py:80
  15.6 1.4 collective-permute-start.6
  17.0 0.6 fusion.2
  17.7 4.2 %shard_map.89.w_ref = bf16[8,1024,256]{2,1,0:T(8,128)(2,1)} custom-call(s32[1]{0:T(128)} %bitcast.core_ref, bf16[4,1024,8,256]{3,2,1,0:T(8,128)(2,1)} %bitcast.27), custom_call_target="tpu_custom_call" | custom-call | bytes 10485760 | tf_op jit(solution)/shard_map/pallas_call | solution.py:80
  21.9 4.9 %shard_map.87 = (bf16[8,1024,256]{2,1,0:T(8,128)(2,1)}, bf16[2,1024,256]{2,1,0:T(8,128)(2,1)}, bf16[2,1024,256]{2,1,0:T(8,128)(2,1)}) custom-call(s32[1]{0:T(128)} %bitcast.core_ref, bf16[4,1024,8,256]{3,2,1,0:T(8,128)(2,1)} %bitcast.28), custom_call_target="tpu_custom_call" | custom-call | bytes 10485760 | tf_op jit(solution)/shard_map/pallas_call | solution.py:80
  26.8 5.0 %shard_map.86 = (bf16[8,1024,256]{2,1,0:T(8,128)(2,1)}, bf16[2,1024,256]{2,1,0:T(8,128)(2,1)}, bf16[2,1024,256]{2,1,0:T(8,128)(2,1)}) custom-call(s32[1]{0:T(128)} %bitcast.core_ref, bf16[4,1024,8,256]{3,2,1,0:T(8,128)(2,1)} %bitcast.29), custom_call_target="tpu_custom_call" | custom-call | bytes 10485760 | tf_op jit(solution)/shard_map/pallas_call | solution.py:80
  31.8 0.9 shard_map.90
  32.7 0.7 copy-done.4
  33.5 3.9 %collective-permute-done = bf16[4,64,256]{2,1,0:T(8,128)(2,1)S(1)} collective-permute-done((bf16[4,64,256]{2,1,0:T(8,128)(2,1)S(1)}, bf16[4,64,256]{2,1,0:T(8,128)(2,1)S(1)}, u32[]{:S(2)}, u32[]{:S(2)}) %collective-permute-start) | collective-permute-done | bytes 131104 | tf_op jit(solution)/shard_map/ppermute | solution.py:411
  37.4 4.1 %collective-permute-start.3 = (bf16[2,64,256]{2,1,0:T(8,128)(2,1)S(1)}, bf16[2,64,256]{2,1,0:T(8,128)(2,1)S(1)}, u32[]{:S(2)}, u32[]{:S(2)}) collective-permute-start(bf16[2,64,256]{2,1,0:T(8,128)(2,1)S(1)} %maximum_select_fusion.q_ref), channel_id=1, source_target_pairs={{0,3},{1,2},{2,1},{3,0},{4,7},{5,6},{6,5},{7,4},{8,11},{9,10},{10,... | collective-permute-start | bytes 196616 | tf_op jit(solution)/shard_map/ppermute | solution.py:416
  41.5 0.9 collective-permute-start.1
  42.5 0.6 maximum_select_fusion.1
  43.1 0.6 maximum_select_fusion.3.p_ref
  43.7 0.3 collective-permute-done.3
  44.0 3.3 %collective-permute-done.2 = bf16[2,64,256]{2,1,0:T(8,128)(2,1)S(1)} collective-permute-done((bf16[2,64,256]{2,1,0:T(8,128)(2,1)S(1)}, bf16[2,64,256]{2,1,0:T(8,128)(2,1)S(1)}, u32[]{:S(2)}, u32[]{:S(2)}) %collective-permute-start.2) | collective-permute-done | bytes 65568 | tf_op jit(solution)/shard_map/ppermute | solution.py:416
  47.5 0.9 copy-done.5
  48.4 4.8 %shard_map.91 = bf16[8,320,256]{2,1,0:T(8,128)(2,1)S(1)} custom-call(bf16[8,1024,256]{2,1,0:T(8,128)(2,1)} %shard_map.89.w_ref, bf16[8,512,256]{2,1,0:T(8,128)(2,1)S(1)} %all-to-all-done.g_ref, bf16[8,64,256]{2,1,0:T(8,128)(2,1)S(1)} %bitcast.25), custom_call_target="tpu_custom_call" | custom-call | flops 1073741824 | bytes 4194304 | tf_op jit(solution)/shard_map/pallas_call | solution.py:51
  53.3 19.3 %all_to_all.45.r_ref = bf16[8,320,256]{2,1,0:T(8,128)(2,1)S(1)} all-to-all(bf16[8,320,256]{2,1,0:T(8,128)(2,1)S(1)} %shard_map.91), channel_id=1, replica_groups={{0,1,2,3,4,5,6,7},{8,9,10,11,12,13,14,15},{16,17,18,19,20,21,22,23},{24..., dimensions={0} | all-to-all | bytes 2621440 | tf_op jit(solution)/shard_map/all_to_all | solution.py:362
  72.5 0.9 shard_map.92
  73.5 1.0 copy-done.1
  74.5 0.8 copy-done.6
  75.3 0.6 copy-done.11
  75.9 4.0 %all-to-all-start.2 = ((bf16[4,576,256]{2,1,0:T(8,128)(2,1)}), bf16[4,576,256]{2,1,0:T(8,128)(2,1)S(1)}, u32[]{:S(2)}, u32[]{:S(2)}) async-start(bf16[4,576,256]{2,1,0:T(8,128)(2,1)} %copy-done.1), calls=%async_computation.2 | async-start | bytes 2359296 | tf_op jit(solution)/shard_map/all_to_all | solution.py:362
  79.9 1.9 collective-permute-start.4
  81.8 0.8 collective-permute-start.5
  82.6 14.5 %all-to-all-done.2.refs_3_ = bf16[4,576,256]{2,1,0:T(8,128)(2,1)S(1)} async-done(((bf16[4,576,256]{2,1,0:T(8,128)(2,1)}), bf16[4,576,256]{2,1,0:T(8,128)(2,1)S(1)}, u32[]{:S(2)}, u32[]{:S(2)}) %all-to-all-start.2) | async-done | bytes 1179680 | tf_op jit(solution)/shard_map/all_to_all | solution.py:362
  97.1 5.4 %shard_map.93 = bf16[4,576,256]{2,1,0:T(8,128)(2,1)S(1)} custom-call(s32[4]{0:T(128)S(1)} %pad_add_fusion.s_ref, bf16[8,1024,256]{2,1,0:T(8,128)(2,1)} %get-tuple-element.71.refs_0_, bf16[4,1024,256]{2,1,0:T(8,128)(2,1)} %collective-permute-done.6.refs_1_, bf16[4,1024,256]{2,1,0:T(8,128)(2,1)} %collective-permute-done.7.refs_2_, ...), custom_call_target="tpu_custom_call" | custom-call | flops 2147483648 | bytes 8388608 | tf_op jit(solution)/shard_map/pallas_call | solution.py:51
  102.5 18.9 %all_to_all.46.r_ref = bf16[4,576,256]{2,1,0:T(8,128)(2,1)S(1)} all-to-all(bf16[4,576,256]{2,1,0:T(8,128)(2,1)S(1)} %shard_map.93), channel_id=1, replica_groups=mesh['dp'=4,'tensor'=8,'layer'=4] {'layer'}, dimensions={0} | all-to-all | bytes 2359296 | tf_op jit(solution)/shard_map/all_to_all | solution.py:362
  121.9 0.5 collective-permute-start.9
  122.4 1.9 collective-permute-start.10
  124.3 0.8 collective-permute-start.11
  125.1 17.5 %all_to_all.47.refs_5_ = bf16[4,512,256]{2,1,0:T(8,128)(2,1)S(1)} all-to-all(bf16[4,512,256]{2,1,0:T(8,128)(2,1)S(1)} %get-tuple-element.79), channel_id=1, replica_groups={{0,8,16,24},{4,12,20,28},{1,9,17,25},{5,13,21,29},{2,10,18,26},{6,14,22..., dimensions={0} | all-to-all | bytes 2097152 | tf_op jit(solution)/shard_map/all_to_all | solution.py:362
  142.6 1.0 copy-done.13
  143.5 0.3 copy-done.14
  143.9 6.1 %shard_map.95 = bf16[4,528,256]{2,1,0:T(8,128)(2,1)S(1)} custom-call(s32[4]{0:T(128)S(1)} %pad_add_fusion.s_ref, s32[4]{0:T(128)S(1)} %select_reduce_fusion.l_ref, bf16[8,1024,256]{2,1,0:T(8,128)(2,1)} %get-tuple-element.60.refs_0_, bf16[2,1024,256]{2,1,0:T(8,128)(2,1)} %collective-permute-done.4.refs_1_, ...), custom_call_target="tpu_custom_call" | custom-call | flops 2147483648 | bytes 8388608 | tf_op jit(solution)/shard_map/pallas_call | solution.py:51
  150.0 16.9 %all_to_all.48.r_ref = bf16[4,528,256]{2,1,0:T(8,128)(2,1)S(1)} all-to-all(bf16[4,528,256]{2,1,0:T(8,128)(2,1)S(1)} %shard_map.95), channel_id=1, replica_groups=mesh['dp'=4,'tensor'=8,'layer'=4] {'layer'}, dimensions={0} | all-to-all | bytes 2162688 | tf_op jit(solution)/shard_map/all_to_all | solution.py:362
  167.1 1.0 copy-done.2
  168.1 3.5 %all-to-all-start.6 = ((bf16[4,528,256]{2,1,0:T(8,128)(2,1)}), bf16[4,528,256]{2,1,0:T(8,128)(2,1)S(1)}, u32[]{:S(2)}, u32[]{:S(2)}) async-start(bf16[4,528,256]{2,1,0:T(8,128)(2,1)} %copy-done.2), calls=%async_computation.6 | async-start | bytes 2162688 | tf_op jit(solution)/shard_map/all_to_all | solution.py:362
  171.7 0.5 collective-permute-start.13
  172.2 13.0 %all-to-all-done.6.refs_5_ = bf16[4,528,256]{2,1,0:T(8,128)(2,1)S(1)} async-done(((bf16[4,528,256]{2,1,0:T(8,128)(2,1)}), bf16[4,528,256]{2,1,0:T(8,128)(2,1)S(1)}, u32[]{:S(2)}, u32[]{:S(2)}) %all-to-all-start.6) | async-done | bytes 1081376 | tf_op jit(solution)/shard_map/all_to_all | solution.py:362
  185.2 8.7 %all_to_all.49 = bf16[8,16,256]{2,1,0:T(8,128)(2,1)S(1)} all-to-all(bf16[8,16,256]{2,1,0:T(8,128)(2,1)S(1)} %broadcast_in_dim.36), channel_id=1, replica_groups={{0,4,32,36,64,68,96,100},{8,12,40,44,72,76,104,108},{16,20,48,52,80,84,..., dimensions={0} | all-to-all | bytes 131072 | tf_op jit(solution)/shard_map/all_to_all | solution.py:362
  194.3 0.4 subtract_convert_fusion
  194.7 5.5 %shard_map.97 = bf16[8,272,256]{2,1,0:T(8,128)(2,1)S(1)} custom-call(s32[4]{0:T(128)S(1)} %pad_add_fusion.s_ref, bf16[8,1024,256]{2,1,0:T(8,128)(2,1)} %get-tuple-element.58.refs_0_, bf16[2,1024,256]{2,1,0:T(8,128)(2,1)} %copy-done.15, bf16[2,1024,256]{2,1,0:T(8,128)(2,1)} %copy-done.16, bf16[2,1024,256]{2,1,0:T(8,128)(2,1)} %collective-permute-done.12.refs_3_, ...), custom_call_target="tpu_custom_call" | custom-call | flops 2147483648 | bytes 8388608 | tf_op jit(solution)/shard_map/pallas_call | solution.py:51
  200.1 19.2 %all_to_all.50.r_ref = bf16[8,272,256]{2,1,0:T(8,128)(2,1)S(1)} all-to-all(bf16[8,272,256]{2,1,0:T(8,128)(2,1)S(1)} %shard_map.97), channel_id=1, replica_groups={{0,1,2,3,4,5,6,7},{8,9,10,11,12,13,14,15},{16,17,18,19,20,21,22,23},{24..., dimensions={0} | all-to-all | bytes 2228224 | tf_op jit(solution)/shard_map/all_to_all | solution.py:362
  219.4 1.4 shard_map.98
  (73 shorter events, 1.5 us)
Async XLA Ops:
  0.6 193.6 %copy-start = (bf16[1,128,4096]{2,1,0:T(8,128)(2,1)S(1)}, bf16[1,128,4096]{2,1,0:T(8,128)(2,1)}, u32[]{:S(2)}) copy-start(bf16[1,128,4096]{2,1,0:T(8,128)(2,1)} %param.12) | copy-start | bytes 3145732
  3.2 5.6 %copy-start.17 = (bf16[4,64,256]{2,1,0:T(8,128)(2,1)S(1)}, bf16[4,64,256]{2,1,0:T(8,128)(2,1)}, u32[]{:S(2)}) copy-start(bf16[4,64,256]{2,1,0:T(8,128)(2,1)} %param.11) | copy-start | bytes 393220
  3.2 44.3 %all-to-all-start = ((bf16[8,512,256]{2,1,0:T(8,128)(2,1)}), bf16[8,512,256]{2,1,0:T(8,128)(2,1)S(1)}, u32[]{:S(2)}, u32[]{:S(2)}) async-start(bf16[8,512,256]{2,1,0:T(8,128)(2,1)} %broadcast_in_dim.34), calls=%async_computation | async-start | bytes 4194304 | tf_op jit(solution)/shard_map/all_to_all | solution.py:362
  8.8 28.6 %collective-permute-start = (bf16[4,64,256]{2,1,0:T(8,128)(2,1)S(1)}, bf16[4,64,256]{2,1,0:T(8,128)(2,1)S(1)}, u32[]{:S(2)}, u32[]{:S(2)}) collective-permute-start(bf16[4,64,256]{2,1,0:T(8,128)(2,1)S(1)} %copy-done.17), channel_id=1, source_target_pairs={{0,4},{4,0},{8,12},{12,8},{16,20},{20,16},{24,28},{28,24},{1,5},{5... | collective-permute-start | bytes 393224 | tf_op jit(solution)/shard_map/ppermute | solution.py:411
  15.6 60.3 %collective-permute-start.6 = (bf16[4,1024,256]{2,1,0:T(8,128)(2,1)}, bf16[4,1024,256]{2,1,0:T(8,128)(2,1)}, u32[]{:S(2)}, u32[]{:S(2)}) collective-permute-start(bf16[4,1024,256]{2,1,0:T(8,128)(2,1)} %get-tuple-element.56), channel_id=1, source_target_pairs={{0,68},{4,64},{8,76},{12,72},{16,84},{20,80},{24,92},{28,88},{32,1... | collective-permute-start | bytes 6291464 | tf_op jit(solution)/shard_map/ppermute | solution.py:410
  26.8 5.0 %copy-start.3 = (bf16[4,512,256]{2,1,0:T(8,128)(2,1)S(1)}, bf16[4,512,256]{2,1,0:T(8,128)(2,1)}, u32[]{:S(2)}) copy-start(bf16[4,512,256]{2,1,0:T(8,128)(2,1)} %x_ref.1) | copy-start | bytes 3145732
  26.8 5.0 %copy-start.10 = (bf16[4,64,256]{2,1,0:T(8,128)(2,1)S(1)}, bf16[4,64,256]{2,1,0:T(8,128)(2,1)}, u32[]{:S(2)}) copy-start(bf16[4,64,256]{2,1,0:T(8,128)(2,1)} %p_ref.1) | copy-start | bytes 393220
  31.8 1.6 copy-start.23
  31.8 10.7 %copy-start.19 = (bf16[1,64,256]{2,1,0:T(8,128)(2,1)S(1)}, bf16[1,64,256]{2,1,0:T(8,128)(2,1)}, u32[]{:S(2)}) copy-start(bf16[1,64,256]{2,1,0:T(8,128)(2,1)} %get-tuple-element.102) | copy-start | bytes 98308
  31.8 10.7 %copy-start.20 = (bf16[1,64,256]{2,1,0:T(8,128)(2,1)S(1)}, bf16[1,64,256]{2,1,0:T(8,128)(2,1)}, u32[]{:S(2)}) copy-start(bf16[1,64,256]{2,1,0:T(8,128)(2,1)} %get-tuple-element.104) | copy-start | bytes 98308
  31.8 11.3 %copy-start.18 = (bf16[1,64,256]{2,1,0:T(8,128)(2,1)S(1)}, bf16[1,64,256]{2,1,0:T(8,128)(2,1)}, u32[]{:S(2)}) copy-start(bf16[1,64,256]{2,1,0:T(8,128)(2,1)} %get-tuple-element.101) | copy-start | bytes 98308
  32.7 0.7 copy-start.4
  37.4 6.6 %collective-permute-start.3 = (bf16[2,64,256]{2,1,0:T(8,128)(2,1)S(1)}, bf16[2,64,256]{2,1,0:T(8,128)(2,1)S(1)}, u32[]{:S(2)}, u32[]{:S(2)}) collective-permute-start(bf16[2,64,256]{2,1,0:T(8,128)(2,1)S(1)} %maximum_select_fusion.q_ref), channel_id=1, source_target_pairs={{0,3},{1,2},{2,1},{3,0},{4,7},{5,6},{6,5},{7,4},{8,11},{9,10},{10,... | collective-permute-start | bytes 196616 | tf_op jit(solution)/shard_map/ppermute | solution.py:416
  41.5 5.8 %collective-permute-start.2 = (bf16[2,64,256]{2,1,0:T(8,128)(2,1)S(1)}, bf16[2,64,256]{2,1,0:T(8,128)(2,1)S(1)}, u32[]{:S(2)}, u32[]{:S(2)}) collective-permute-start(bf16[2,64,256]{2,1,0:T(8,128)(2,1)S(1)} %maximum_select_fusion.q_ref), channel_id=1, source_target_pairs={{0,2},{1,3},{2,0},{3,1},{4,6},{5,7},{6,4},{7,5},{8,10},{9,11},{10,... | collective-permute-start | bytes 196616 | tf_op jit(solution)/shard_map/ppermute | solution.py:416
  41.5 5.8 %collective-permute-start.1 = (bf16[2,64,256]{2,1,0:T(8,128)(2,1)S(1)}, bf16[2,64,256]{2,1,0:T(8,128)(2,1)S(1)}, u32[]{:S(2)}, u32[]{:S(2)}) collective-permute-start(bf16[2,64,256]{2,1,0:T(8,128)(2,1)S(1)} %maximum_select_fusion.q_ref), channel_id=1, source_target_pairs={{0,1},{1,0},{2,3},{3,2},{4,5},{5,4},{6,7},{7,6},{8,9},{9,8},{10,11... | collective-permute-start | bytes 196616 | tf_op jit(solution)/shard_map/ppermute | solution.py:416
  47.5 1.0 copy-start.5
  53.2 19.3 %copy-start.8 = (bf16[2,64,256]{2,1,0:T(8,128)(2,1)S(1)}, bf16[2,64,256]{2,1,0:T(8,128)(2,1)}, u32[]{:S(2)}) copy-start(bf16[2,64,256]{2,1,0:T(8,128)(2,1)} %maximum_select_fusion.3.p_ref) | copy-start | bytes 196612
  53.2 19.3 %copy-start.9 = (bf16[2,64,256]{2,1,0:T(8,128)(2,1)S(1)}, bf16[2,64,256]{2,1,0:T(8,128)(2,1)}, u32[]{:S(2)}) copy-start(bf16[2,64,256]{2,1,0:T(8,128)(2,1)} %get-tuple-element.67.q_ref) | copy-start | bytes 196612
  73.5 1.0 copy-start.1
  74.5 0.8 copy-start.6
  75.3 0.6 copy-start.11
  75.9 21.1 %collective-permute-start.7 = (bf16[4,1024,256]{2,1,0:T(8,128)(2,1)}, bf16[4,1024,256]{2,1,0:T(8,128)(2,1)}, u32[]{:S(2)}, u32[]{:S(2)}) collective-permute-start(bf16[4,1024,256]{2,1,0:T(8,128)(2,1)} %collective-permute-done.6.refs_1_), channel_id=1, source_target_pairs={{0,32},{32,0},{64,96},{96,64},{1,33},{33,1},{65,97},{97,65},{2,34}... | collective-permute-start | bytes 6291464 | tf_op jit(solution)/shard_map/ppermute | solution.py:408
  75.9 21.1 %all-to-all-start.2 = ((bf16[4,576,256]{2,1,0:T(8,128)(2,1)}), bf16[4,576,256]{2,1,0:T(8,128)(2,1)S(1)}, u32[]{:S(2)}, u32[]{:S(2)}) async-start(bf16[4,576,256]{2,1,0:T(8,128)(2,1)} %copy-done.1), calls=%async_computation.2 | async-start | bytes 2359296 | tf_op jit(solution)/shard_map/all_to_all | solution.py:362
  79.9 41.9 %collective-permute-start.4 = (bf16[2,1024,256]{2,1,0:T(8,128)(2,1)}, bf16[2,1024,256]{2,1,0:T(8,128)(2,1)}, u32[]{:S(2)}, u32[]{:S(2)}) collective-permute-start(bf16[2,1024,256]{2,1,0:T(8,128)(2,1)} %get-tuple-element.69), channel_id=1, source_target_pairs={{0,68},{4,64},{8,76},{12,72},{16,84},{20,80},{24,92},{28,88},{32,1... | collective-permute-start | bytes 3145736 | tf_op jit(solution)/shard_map/ppermute | solution.py:403
  81.8 40.0 %collective-permute-start.5 = (bf16[2,1024,256]{2,1,0:T(8,128)(2,1)}, bf16[2,1024,256]{2,1,0:T(8,128)(2,1)}, u32[]{:S(2)}, u32[]{:S(2)}) collective-permute-start(bf16[2,1024,256]{2,1,0:T(8,128)(2,1)} %get-tuple-element.70), channel_id=1, source_target_pairs={{0,4},{4,0},{8,12},{12,8},{16,20},{20,16},{24,28},{28,24},{1,5},{5... | collective-permute-start | bytes 3145736 | tf_op jit(solution)/shard_map/ppermute | solution.py:404
  102.5 18.9 %copy-start.7 = (f32[512,256]{1,0:T(8,128)S(1)}, f32[512,256]{1,0:T(8,128)}, u32[]{:S(2)}) copy-start(f32[512,256]{1,0:T(8,128)} %copy-done.6) | copy-start | bytes 1572868
  102.5 19.9 %copy-start.22 = (bf16[2,1024,256]{2,1,0:T(8,128)(2,1)S(1)}, bf16[2,1024,256]{2,1,0:T(8,128)(2,1)}, u32[]{:S(2)}) copy-start(bf16[2,1024,256]{2,1,0:T(8,128)(2,1)} %get-tuple-element.89) | copy-start | bytes 3145732
  121.4 2.8 %copy-start.21 = (bf16[2,1024,256]{2,1,0:T(8,128)(2,1)S(1)}, bf16[2,1024,256]{2,1,0:T(8,128)(2,1)}, u32[]{:S(2)}) copy-start(bf16[2,1024,256]{2,1,0:T(8,128)(2,1)} %get-tuple-element.90) | copy-start | bytes 3145732
  121.7 22.1 %copy-start.12 = (bf16[2,64,256]{2,1,0:T(8,128)(2,1)S(1)}, bf16[2,64,256]{2,1,0:T(8,128)(2,1)}, u32[]{:S(2)}) copy-start(bf16[2,64,256]{2,1,0:T(8,128)(2,1)} %copy-done.11) | copy-start | bytes 196612
  121.8 20.8 %collective-permute-start.8 = (bf16[2,1024,256]{2,1,0:T(8,128)(2,1)}, bf16[2,1024,256]{2,1,0:T(8,128)(2,1)S(1)}, u32[]{:S(2)}, u32[]{:S(2)}) collective-permute-start(bf16[2,1024,256]{2,1,0:T(8,128)(2,1)} %collective-permute-done.4.refs_1_), channel_id=1, source_target_pairs={{0,32},{32,0},{64,96},{96,64},{1,33},{33,1},{65,97},{97,65},{2,34}... | collective-permute-start | bytes 3145736 | tf_op jit(solution)/shard_map/ppermute | solution.py:408
  121.9 20.7 %collective-permute-start.9 = (bf16[2,1024,256]{2,1,0:T(8,128)(2,1)}, bf16[2,1024,256]{2,1,0:T(8,128)(2,1)S(1)}, u32[]{:S(2)}, u32[]{:S(2)}) collective-permute-start(bf16[2,1024,256]{2,1,0:T(8,128)(2,1)} %collective-permute-done.5.refs_2_), channel_id=1, source_target_pairs={{0,32},{32,0},{64,96},{96,64},{1,33},{33,1},{65,97},{97,65},{2,34}... | collective-permute-start | bytes 3145736 | tf_op jit(solution)/shard_map/ppermute | solution.py:408
  122.4 27.6 %collective-permute-start.10 = (bf16[2,1024,256]{2,1,0:T(8,128)(2,1)S(1)}, bf16[2,1024,256]{2,1,0:T(8,128)(2,1)S(1)}, u32[]{:S(2)}, u32[]{:S(2)}) collective-permute-start(bf16[2,1024,256]{2,1,0:T(8,128)(2,1)S(1)} %copy-done.22), channel_id=1, source_target_pairs={{0,68},{4,64},{8,76},{12,72},{16,84},{20,80},{24,92},{28,88},{32,1... | collective-permute-start | bytes 3145736 | tf_op jit(solution)/shard_map/ppermute | solution.py:403
  124.3 25.7 %collective-permute-start.11 = (bf16[2,1024,256]{2,1,0:T(8,128)(2,1)S(1)}, bf16[2,1024,256]{2,1,0:T(8,128)(2,1)S(1)}, u32[]{:S(2)}, u32[]{:S(2)}) collective-permute-start(bf16[2,1024,256]{2,1,0:T(8,128)(2,1)S(1)} %copy-done.21), channel_id=1, source_target_pairs={{0,4},{4,0},{8,12},{12,8},{16,20},{20,16},{24,28},{28,24},{1,5},{5... | collective-permute-start | bytes 3145736 | tf_op jit(solution)/shard_map/ppermute | solution.py:404
  142.5 1.0 copy-start.13
  142.6 1.3 copy-start.14
  149.9 17.1 %copy-start.15 = (bf16[2,1024,256]{2,1,0:T(8,128)(2,1)}, bf16[2,1024,256]{2,1,0:T(8,128)(2,1)S(1)}, u32[]{:S(2)}) copy-start(bf16[2,1024,256]{2,1,0:T(8,128)(2,1)S(1)} %collective-permute-done.10.refs_1_) | copy-start | bytes 3145732
  150.0 17.1 %copy-start.16 = (bf16[2,1024,256]{2,1,0:T(8,128)(2,1)}, bf16[2,1024,256]{2,1,0:T(8,128)(2,1)S(1)}, u32[]{:S(2)}) copy-start(bf16[2,1024,256]{2,1,0:T(8,128)(2,1)S(1)} %collective-permute-done.11.refs_2_) | copy-start | bytes 3145732
  167.1 1.0 copy-start.2
  168.1 17.1 %all-to-all-start.6 = ((bf16[4,528,256]{2,1,0:T(8,128)(2,1)}), bf16[4,528,256]{2,1,0:T(8,128)(2,1)S(1)}, u32[]{:S(2)}, u32[]{:S(2)}) async-start(bf16[4,528,256]{2,1,0:T(8,128)(2,1)} %copy-done.2), calls=%async_computation.6 | async-start | bytes 2162688 | tf_op jit(solution)/shard_map/all_to_all | solution.py:362
  171.6 23.1 %collective-permute-start.12 = (bf16[2,1024,256]{2,1,0:T(8,128)(2,1)}, bf16[2,1024,256]{2,1,0:T(8,128)(2,1)}, u32[]{:S(2)}, u32[]{:S(2)}) collective-permute-start(bf16[2,1024,256]{2,1,0:T(8,128)(2,1)} %copy-done.15), channel_id=1, source_target_pairs={{0,32},{32,0},{64,96},{96,64},{1,33},{33,1},{65,97},{97,65},{2,34}... | collective-permute-start | bytes 3145736 | tf_op jit(solution)/shard_map/ppermute | solution.py:408
  171.7 23.0 %collective-permute-start.13 = (bf16[2,1024,256]{2,1,0:T(8,128)(2,1)}, bf16[2,1024,256]{2,1,0:T(8,128)(2,1)}, u32[]{:S(2)}, u32[]{:S(2)}) collective-permute-start(bf16[2,1024,256]{2,1,0:T(8,128)(2,1)} %copy-done.16), channel_id=1, source_target_pairs={{0,32},{32,0},{64,96},{96,64},{1,33},{33,1},{65,97},{97,65},{2,34}... | collective-permute-start | bytes 3145736 | tf_op jit(solution)/shard_map/ppermute | solution.py:408

commit v5 on v4

--- a/solution.py
+++ b/solution.py
@@ -48,16 +48,44 @@
     rows, width = weights[0].shape[1:]
     tokens = operands[0].shape[-1]
     cells = sum(w.shape[0] for w in weights)
+    groups = rows // width
+    sizes = [len(scalars), len(weights), len(operands), len(outs), len(weights), len(scratch)]
+
+    def kernel(*refs):
+        parts, at = [], 0
+        for size in sizes:
+            parts.append(refs[at : at + size])
+            at += size
+        scalar_refs, far_refs, operand_refs, out_refs, held_refs, scratch_refs = parts
+        sems = refs[-1]
+
+        def copy(k, n):
+            rows_of = pl.ds(n * width, width)
+            return pltpu.make_async_copy(
+                far_refs[k].at[:, rows_of], held_refs[k].at[:, rows_of], sems.at[k, n]
+            )
+
+        for n in range(groups):
+            for k in range(len(weights)):
+                copy(k, n).start()
+
+        def fetch(n):
+            for k in range(len(weights)):
+                copy(k, n).wait()
+
+        body(fetch, scalar_refs, held_refs, operand_refs, out_refs, scratch_refs)
+
     return pl.pallas_call(
-        body,
-        grid=(rows // width,),
+        kernel,
         in_specs=[SCALARS] * len(scalars)
-        + [pl.BlockSpec((w.shape[0], width, width), lambda n: (0, n, 0)) for w in weights]
+        + [pl.BlockSpec(memory_space=pltpu.HBM)] * len(weights)
         + [WIDE] * len(operands),
         out_specs=[WIDE] * len(outs),
         out_shape=[jax.ShapeDtypeStruct(*out) for out in outs],
-        scratch_shapes=list(scratch),
-        compiler_params=limit(24),
+        scratch_shapes=[pltpu.VMEM(w.shape, w.dtype) for w in weights]
+        + list(scratch)
+        + [pltpu.SemaphoreType.DMA((len(weights), groups))],
+        compiler_params=limit(20),
         cost_estimate=pl.CostEstimate(
             flops=2 * cells * width * rows * tokens,
             bytes_accessed=2 * cells * width * rows,
@@ -127,17 +155,21 @@
     groups = weight.shape[1] // width
     half = tokens // 2
 
-    def body(w_ref, g_ref, e_ref, o_ref):
-        n = pl.program_id(0)
-        for h in range(2):
-            total = sum_of(
-                dot(w_ref[a], g_ref[a, h * half : (h + 1) * half], NT) for a in range(cells)
-            )
-            o_ref[h * groups + n, :width] = total.astype(o_ref.dtype)
-
-        @pl.when(n == 0)
-        def _():
-            o_ref[:, width:] = e_ref[...]
+    def body(fetch, _, weight_refs, operand_refs, out_refs, __):
+        (w_ref,), (g_ref, e_ref), (o_ref,) = weight_refs, operand_refs, out_refs
+        o_ref[:, width:] = e_ref[...]
+        for n in range(groups):
+            fetch(n)
+            for h in range(2):
+                total = sum_of(
+                    dot(
+                        w_ref[a, n * width : (n + 1) * width],
+                        g_ref[a, h * half : (h + 1) * half],
+                        NT,
+                    )
+                    for a in range(cells)
+                )
+                o_ref[h * groups + n, :width] = total.astype(o_ref.dtype)
 
     return streamed_call(
         body,
@@ -148,19 +180,21 @@
     )[0]
 
 
-def pair_totals(s_ref, g_ref, w_refs):
+def pair_totals(s_ref, g_ref, w_refs, n):
     own_ref, *others = w_refs
     cells, _, width = own_ref.shape
     half = cells // 2
     deep = others[0].shape[0]
     pieces = half // deep
     x, core = s_ref[0], s_ref[1]
+    cut = slice(n * width, (n + 1) * width)
     yield x, sum_of(
-        dot(own_ref[a], g_ref[a // 2, (a % 2) * width : (a % 2 + 1) * width]) for a in range(cells)
+        dot(own_ref[a, cut], g_ref[a // 2, (a % 2) * width : (a % 2 + 1) * width])
+        for a in range(cells)
     )
     yield 1 - x, sum_of(
         dot(
-            refs[i // deep][i % deep],
+            refs[i // deep][i % deep, cut],
             g_ref[(half // 2) * first + i // 2, (i % 2) * width : (i % 2 + 1) * width],
         )
         for first, refs in ((core, others[:pieces]), (1 - core, others[pieces:]))
@@ -172,63 +206,59 @@
     width = held[0].shape[2]
     groups = held[0].shape[1] // width
 
-    def body(s_ref, *refs):
-        *w_refs, g_ref, o_ref = refs
-        n = pl.program_id(0)
-        for column, total in pair_totals(s_ref, g_ref, w_refs):
-            start = pl.multiple_of(column * width, width)
-            o_ref[n, pl.ds(start, width)] = total.astype(o_ref.dtype)
-
-        @pl.when(n == 0)
-        def _():
-            whole = sum_of(g_ref[k, 2 * width :].astype(F32) for k in range(g_ref.shape[0]))
-            for k in range(groups):
-                o_ref[k, 2 * width :] = whole.astype(o_ref.dtype)
+    def body(fetch, scalar_refs, w_refs, operand_refs, out_refs, _):
+        (s_ref,), (g_ref,), (o_ref,) = scalar_refs, operand_refs, out_refs
+        whole = sum_of(g_ref[k, 2 * width :].astype(F32) for k in range(g_ref.shape[0]))
+        for n in range(groups):
+            o_ref[n, 2 * width :] = whole.astype(o_ref.dtype)
+            fetch(n)
+            for column, total in pair_totals(s_ref, g_ref, w_refs, n):
+                start = pl.multiple_of(column * width, width)
+                o_ref[n, pl.ds(start, width)] = total.astype(o_ref.dtype)
 
     return streamed_call(
         body, [((groups, *gathered.shape[1:]), BF16)], held, [gathered], [place]
     )[0]
 
 
-def pair_partial_scored(place, layer_of, gathered, held, outs_top, outs_low, proj, ins):
+def pair_partial_scored(place, layer_of, gathered, held, grads, proj, last_proj, ins):
     width = held[0].shape[2]
     groups = held[0].shape[1] // width
     layers, rank, tokens = ins.shape
     quarter = rank // 4
 
-    def body(s_ref, l_ref, *refs):
-        *w_refs, g_ref, a_ref, k_ref, p_ref, i_ref, o_ref, f_ref, last_ref = refs
-        n = pl.program_id(0)
-
-        @pl.when(n == 0)
-        def _():
-            f_ref[3] = a_ref[0]
-            f_ref[2] = a_ref[1]
-            f_ref[1] = k_ref[0].astype(f_ref.dtype)
-            last_ref[...] = k_ref[1]
-
-        for column, total in pair_totals(s_ref, g_ref, w_refs):
-            start = pl.multiple_of(column * width, width)
-            rounded = total.astype(o_ref.dtype)
-            o_ref[n, pl.ds(start, width)] = rounded
-            last_ref[...] += dot(p_ref[n, column], rounded)
-
-        @pl.when(n == groups - 1)
-        def _():
-            f_ref[0] = last_ref[...].astype(f_ref.dtype)
-            for o in range(layers):
-                block = dot(f_ref[l_ref[o]], i_ref[l_ref[o]], NT).astype(o_ref.dtype)
-                o_ref[o, 2 * width :] = jnp.concatenate(
-                    [block[quarter * j : quarter * (j + 1)] for j in range(4)], axis=1
-                )
+    def body(fetch, scalar_refs, w_refs, operand_refs, out_refs, scratch_refs):
+        s_ref, l_ref = scalar_refs
+        g_ref, *grad_refs, p_ref, q_ref, i_ref = operand_refs
+        (o_ref,), (f_ref,) = out_refs, scratch_refs
+
+        def factor(level, ref):
+            return dot(p_ref[level, 0], ref[:width]) + dot(p_ref[level, 1], ref[width : 2 * width])
+
+        for k, ref in enumerate(grad_refs):
+            f_ref[layers - 1 - k] = factor(layers - 1 - k, ref).astype(f_ref.dtype)
+        final = factor(0, grad_refs[-1])
+        for n in range(groups):
+            fetch(n)
+            for column, total in pair_totals(s_ref, g_ref, w_refs, n):
+                start = pl.multiple_of(column * width, width)
+                rounded = total.astype(o_ref.dtype)
+                o_ref[n, pl.ds(start, width)] = rounded
+                final = final + dot(q_ref[n, column], rounded)
+        f_ref[0] = final.astype(f_ref.dtype)
+        for o in range(layers):
+            block = dot(f_ref[l_ref[o]], i_ref[l_ref[o]], NT).astype(o_ref.dtype)
+            o_ref[o, 2 * width :] = jnp.concatenate(
+                [block[quarter * j : quarter * (j + 1)] for j in range(4)], axis=1
+            )
 
     return streamed_call(
         body,
         [((groups, 2 * width + quarter, tokens), BF16)],
         held,
-        [gathered, outs_top, outs_low, proj, ins],
+        [gathered, *grads, proj, last_proj, ins],
         [place, layer_of],
-        [pltpu.VMEM((layers, rank, tokens), BF16), pltpu.VMEM((rank, tokens), F32)],
+        [pltpu.VMEM((layers, rank, tokens), BF16)],
     )[0]
 
 
@@ -236,19 +266,17 @@
     width = held[0].shape[2]
     groups = held[0].shape[1] // width
 
-    def body(s_ref, *refs):
-        *w_refs, g_ref, t_ref, e_ref, o_ref = refs
-        n = pl.program_id(0)
-        for column, total in pair_totals(s_ref, g_ref, w_refs):
-            start = pl.multiple_of(column * width, width)
-            mine = t_ref[pl.ds(start, width)]
-            total = total + jnp.where(n == s_ref[2], mine, jnp.zeros_like(mine))
-            o_ref[groups * column + n, :width] = total.astype(o_ref.dtype)
-
-        @pl.when(n == 0)
-        def _():
-            for k in range(2 * groups):
-                o_ref[k, width:] = e_ref[k % groups]
+    def body(fetch, scalar_refs, w_refs, operand_refs, out_refs, _):
+        (s_ref,), (g_ref, t_ref, e_ref), (o_ref,) = scalar_refs, operand_refs, out_refs
+        for k in range(2 * groups):
+            o_ref[k, width:] = e_ref[k % groups]
+        for n in range(groups):
+            fetch(n)
+            for column, total in pair_totals(s_ref, g_ref, w_refs, n):
+                start = pl.multiple_of(column * width, width)
+                mine = t_ref[pl.ds(start, width)]
+                total = total + jnp.where(n == s_ref[2], mine, jnp.zeros_like(mine))
+                o_ref[groups * column + n, :width] = total.astype(o_ref.dtype)
 
     return streamed_call(
         body,
@@ -259,56 +287,51 @@
     )[0]
 
 
-def settle_first(place, arrived, gathered, proj_top, proj_next):
+def settle_first(place, arrived, gathered):
     blocks, deep, half = arrived.shape
     width = gathered.shape[2]
     groups = blocks // 2
-    rank = proj_top.shape[1]
-
-    def body(s_ref, r_ref, g_ref, p_ref, q_ref, t_ref, c_ref, o_ref):
+
+    def body(s_ref, r_ref, g_ref, t_ref, c_ref, b_ref, m_ref):
         x, y = s_ref[0], s_ref[3]
-        outs = [None, None]
         for k in range(2):
+            rows_of = slice(k * width, (k + 1) * width)
             start = g_ref[2 * y + k, pl.ds(pl.multiple_of(x * half, half), half)].astype(F32).T
-            outs[0] = sum_of([*([outs[0]] if k else []), dot(p_ref[k], start.astype(BF16))])
+            b_ref[rows_of] = start.astype(BF16)
             total = start + sum_of(r_ref[groups * k + z, :width].astype(F32) for z in range(groups))
-            t_ref[k * width : (k + 1) * width] = total
+            t_ref[rows_of] = total
             rounded = total.astype(BF16)
-            outs[1] = sum_of([*([outs[1]] if k else []), dot(q_ref[k], rounded)])
+            m_ref[rows_of] = rounded
             for j in range(c_ref.shape[0]):
-                c_ref[j, k * width : (k + 1) * width] = rounded
+                c_ref[j, rows_of] = rounded
         ins = sum_of(r_ref[k, width:].astype(F32) for k in range(blocks)).astype(BF16)
         for j in range(c_ref.shape[0]):
             c_ref[j, 2 * width :] = ins
-        o_ref[0] = outs[0].astype(BF16)
-        o_ref[1] = outs[1].astype(BF16)
 
     return local_call(
         body,
         [
             ((2 * width, half), F32),
             ((gathered.shape[0] // 2, 2 * width + deep - width, half), BF16),
-            ((2, rank, half), BF16),
+            ((2 * width, half), BF16),
+            ((2 * width, half), BF16),
         ],
-        [arrived, gathered, proj_top, proj_next],
+        [arrived, gathered],
         [place],
     )
 
 
-def settle(arrived, total, proj_next, proj_last):
+def settle(arrived, total):
     groups, deep, half = arrived.shape
     depth = total.shape[0]
-    width = depth // 2
-    rank = proj_next.shape[1]
-
-    def body(r_ref, t_ref, p_ref, q_ref, o_ref, c_ref, f_ref, i_ref):
+
+    def body(r_ref, t_ref, o_ref, c_ref, m_ref, i_ref):
         value = t_ref[...] + sum_of(r_ref[z, :depth].astype(F32) for z in range(groups))
         o_ref[...] = value
         rounded = value.astype(BF16)
+        m_ref[...] = rounded
         for j in range(c_ref.shape[0]):
             c_ref[j] = rounded
-        for i, ref in enumerate((p_ref, q_ref)):
-            f_ref[i] = dot(ref[0], rounded[:width]) + dot(ref[1], rounded[width:])
         i_ref[...] = r_ref[:, depth:]
 
     return local_call(
@@ -316,10 +339,10 @@
         [
             (total.shape, F32),
             ((groups, depth, half), BF16),
-            ((2, rank, half), F32),
+            (total.shape, BF16),
             ((groups, deep - depth, half), BF16),
         ],
-        [arrived, total, proj_next, proj_last],
+        [arrived, total],
     )
 
 
@@ -408,10 +431,20 @@
         return [in_hbm(lax.ppermute(v, "dp", [(d, d ^ 1) for d in range(n_dp)])) for v in values]
 
     near[2] = [in_hbm(lax.ppermute(passed[2][0], ("dp", "tensor"), across))]
+    in_parts = in_factor_parts(saved_inputs, proj_in)
+    gathered, own[3], own[2], own[1], passed[1], in_parts, place, layer_of = after(
+        (gathered, own[3], own[2], own[1], passed[1], in_parts, place, layer_of)
+    )
+
+    partial = first_partial(gathered, own[3], in_parts)
+    arrived = exchange(partial, ("tensor", "layer"), along_xz)
+    total, copies, above_3, above_2 = settle_first(place, arrived, gathered)
+
+    passed[1], proj_out, _ = after((passed[1], proj_out, total))
     other_proj = lax.ppermute(proj_out, "tensor", beside)
-    pair_proj = [
-        jnp.where(x == 0, jnp.stack([p, q]), jnp.stack([q, p])) for p, q in zip(proj_out, other_proj)
-    ]
+    pair_proj = jnp.where(
+        x == 0, jnp.stack([proj_out, other_proj], 1), jnp.stack([other_proj, proj_out], 1)
+    )
     shifted = [pair_proj[0]] + [
         lax.ppermute(pair_proj[0], "layer", [(z, z ^ k) for z in range(n_layer)])
         for k in range(1, n_layer)
@@ -422,23 +455,16 @@
             for z in range(n_layer)
         ]
     ).astype(BF16)
-    in_parts = in_factor_parts(saved_inputs, proj_in)
-    gathered, own, passed, pair_proj, last_proj, in_parts, place, layer_of = after(
-        (gathered, own, passed, pair_proj, last_proj, in_parts, place, layer_of)
-    )
-
-    partial = first_partial(gathered, own[3], in_parts)
-    arrived = exchange(partial, ("tensor", "layer"), along_xz)
-    total, copies, outs_top = settle_first(place, arrived, gathered, pair_proj[3], pair_proj[2])
-
-    passed[1], _ = after((passed[1], total))
     near[1] = over_both(passed[1])
     near[2], _ = after((near[2], total))
     far[2] = to_other_core(near[2])
     gathered = exchange(copies, "tensor", along_y)
+    gathered, own[0], passed[0], pair_proj, last_proj = after(
+        (gathered, own[0], passed[0], pair_proj, last_proj)
+    )
     partial = pair_partial(place, gathered, [own[2], *near[2], *far[2]])
     arrived = exchange(partial, "layer")
-    total, copies, outs_low, ins = settle(arrived, total, pair_proj[1], pair_proj[0])
+    total, copies, above_1, ins = settle(arrived, total)
 
     near[1], _ = after((near[1], total))
     far[1] = to_other_core(near[1])
@@ -447,11 +473,19 @@
     gathered = exchange(copies, "tensor", along_y)
     far[1], gathered = after((far[1], gathered))
     partial = pair_partial_scored(
-        place, layer_of, gathered, [own[1], *near[1], *far[1]], outs_top, outs_low, last_proj, ins
+        place,
+        layer_of,
+        gathered,
+        [own[1], *near[1], *far[1]],
+        [above_3, above_2, above_1],
+        pair_proj,
+        last_proj,
+        ins,
     )
     partial, near[0] = after((partial, near[0]))
     far[0] = to_other_core(near[0])
     arrived = exchange(partial, "layer")
+    arrived, far[0] = after((arrived, far[0]))
     total, copies = settle_scored(arrived, total)
 
     gathered = exchange(copies, "tensor", along_y)

time: 222 us -> 214 us (0.964)
  waiting for transfers between devices: 34.9 us -> 12.4 us
  blocking collectives: 101 us -> 123 us
  starting transfers between devices: 28.1 us -> 24 us
    all_to_all x6 -> x7, blocking collectives: 101 us -> 123 us  [exchange(): lax.all_to_all(blocks, axes, 0, 0, tiled=True, axis_index_groups=groups)]
    all_to_all x3 -> x2, waiting for transfers between devices: 27.4 us -> 11 us  [exchange(): lax.all_to_all(blocks, axes, 0, 0, tiled=True, axis_index_groups=groups)]
    all_to_all x3 -> x2, starting transfers between devices: 13.1 us -> 9.33 us  [exchange(): lax.all_to_all(blocks, axes, 0, 0, tiled=True, axis_index_groups=groups)]
    ppermute x3, waiting for transfers between devices: 3.55 us -> 0.01 us  [on_device(): lax.ppermute(pair_proj[0], 'layer', [(z, z ^ k) for z in range(n_layer)])]
    ppermute x1, waiting for transfers between devices: 3.87 us -> 1.39 us  [on_device(): other_proj = lax.ppermute(proj_out, 'tensor', beside)]
    unnamed x49 -> x37, local copies, waits for them, and re-layouts: 6.49 us -> 5.2 us
  transfers between devices with their start and end apart: 17 -> 16, of which waited for: 5 -> 3; matrix products, arithmetic and copies ran while one was open for 1% -> 0% of each run, Pallas kernels for 17% -> 18%
where the time goes in v5:
time: 214 us; the launch traced here: 213 us
  blocking collectives  123 us (57%)
  Pallas kernels  44.3 us (21%)
  starting transfers between devices  24 us (11%)
  waiting for transfers between devices  12.4 us (6%)
  local copies, waits for them, and re-layouts  8.02 us (4%)
    all_to_all x7, blocking collectives, exchange(): lax.all_to_all(blocks, axes, 0, 0, tiled=True, axis_index_groups=groups)  123 us
    pallas_call x4, Pallas kernels, streamed_call(): pl.pallas_call(kernel, in_specs=[SCALARS] * len(scalars) + [pl.BlockSpec(...  22.1 us
    pallas_call x4, Pallas kernels, features_first(): pl.pallas_call(body, grid_spec=pltpu.PrefetchScalarGridSpec(num_scalar_pr...  18.8 us
    all_to_all x2, waiting for transfers between devices, exchange(): lax.all_to_all(blocks, axes, 0, 0, tiled=True, axis_index_groups=groups)  11 us
    all_to_all x2, starting transfers between devices, exchange(): lax.all_to_all(blocks, axes, 0, 0, tiled=True, axis_index_groups=groups)  9.33 us
    unnamed x37, local copies, waits for them, and re-layouts  5.2 us
    ppermute x2, starting transfers between devices, over_both(): lax.ppermute(values[0], ('dp', 'tensor'), across)  4.57 us
  transfers between devices with their start and end apart: 16, of which 3 were waited for; matrix products, arithmetic and copies ran while one was open for 0% of the time, Pallas kernels for 18%

profile of v5, /device:TPU:0, one launch (start us, length us, event | category | flops | bytes accessed | tf_op | source)
XLA Modules:
  0.0 213.1 jit_solution(5657046194932104585)
XLA Ops:
  0.6 2.6 %broadcast_in_dim.34 = bf16[8,512,256]{2,1,0:T(8,128)(2,1)} broadcast(bf16[512,256]{1,0:T(8,128)(2,1)} %param.8), dimensions={1,2} | broadcast | bytes 2359296 | tf_op jit(solution)/shard_map/broadcast_in_dim | solution.py:417
  3.2 5.5 %all-to-all-start = ((bf16[8,512,256]{2,1,0:T(8,128)(2,1)}), bf16[8,512,256]{2,1,0:T(8,128)(2,1)S(1)}, u32[]{:S(2)}, u32[]{:S(2)}) async-start(bf16[8,512,256]{2,1,0:T(8,128)(2,1)} %broadcast_in_dim.34), calls=%async_computation | async-start | bytes 4194304 | tf_op jit(solution)/shard_map/all_to_all | solution.py:385
  8.7 4.8 %shard_map.87 = (bf16[8,1024,256]{2,1,0:T(8,128)(2,1)}, bf16[4,1024,256]{2,1,0:T(8,128)(2,1)}) custom-call(s32[1]{0:T(128)} %bitcast.core_ref, bf16[4,1024,8,256]{3,2,1,0:T(8,128)(2,1)} %bitcast.38), custom_call_target="tpu_custom_call" | custom-call | bytes 10485760 | tf_op jit(solution)/shard_map/pallas_call | solution.py:108
  13.5 3.3 %collective-permute-start.6 = (bf16[4,1024,256]{2,1,0:T(8,128)(2,1)}, bf16[4,1024,256]{2,1,0:T(8,128)(2,1)}, u32[]{:S(2)}, u32[]{:S(2)}) collective-permute-start(bf16[4,1024,256]{2,1,0:T(8,128)(2,1)} %get-tuple-element.74), channel_id=1, source_target_pairs={{0,68},{4,64},{8,76},{12,72},{16,84},{20,80},{24,92},{28,88},{32,1... | collective-permute-start | bytes 6291464 | tf_op jit(solution)/shard_map/ppermute | solution.py:433
  16.8 4.2 %shard_map.86.refs_0_ = bf16[8,1024,256]{2,1,0:T(8,128)(2,1)} custom-call(s32[1]{0:T(128)} %bitcast.core_ref, bf16[4,1024,8,256]{3,2,1,0:T(8,128)(2,1)} %bitcast.39), custom_call_target="tpu_custom_call" | custom-call | bytes 10485760 | tf_op jit(solution)/shard_map/pallas_call | solution.py:108
  21.0 4.9 %shard_map.88 = (bf16[8,1024,256]{2,1,0:T(8,128)(2,1)}, bf16[2,1024,256]{2,1,0:T(8,128)(2,1)}, bf16[2,1024,256]{2,1,0:T(8,128)(2,1)}) custom-call(s32[1]{0:T(128)} %bitcast.core_ref, bf16[4,1024,8,256]{3,2,1,0:T(8,128)(2,1)} %bitcast.40), custom_call_target="tpu_custom_call" | custom-call | bytes 10485760 | tf_op jit(solution)/shard_map/pallas_call | solution.py:108
  25.9 1.2 copy-done.2
  27.2 0.9 shard_map.89
  28.1 0.1 select_reduce_fusion.refs_1_
  28.2 7.4 %all-to-all-done.refs_1_.g_ref = bf16[8,512,256]{2,1,0:T(8,128)(2,1)S(1)} async-done(((bf16[8,512,256]{2,1,0:T(8,128)(2,1)}), bf16[8,512,256]{2,1,0:T(8,128)(2,1)S(1)}, u32[]{:S(2)}, u32[]{:S(2)}) %all-to-all-start) | async-done | bytes 2097184 | tf_op jit(solution)/shard_map/all_to_all | solution.py:385
  35.7 4.2 %shard_map.90 = bf16[8,320,256]{2,1,0:T(8,128)(2,1)S(1)} custom-call(bf16[8,1024,256]{2,1,0:T(8,128)(2,1)} %shard_map.86.refs_0_, bf16[8,512,256]{2,1,0:T(8,128)(2,1)S(1)} %all-to-all-done.refs_1_.g_ref, bf16[8,64,256]{2,1,0:T(8,128)(2,1)S(1)} %bitcast.37), custom_call_target="tpu_custom_call" | custom-call | flops 1073741824 | bytes 4194304 | tf_op jit(solution)/shard_map/pallas_call | solution.py:78
  39.9 22.8 %all_to_all.45.r_ref = bf16[8,320,256]{2,1,0:T(8,128)(2,1)S(1)} all-to-all(bf16[8,320,256]{2,1,0:T(8,128)(2,1)S(1)} %shard_map.90), channel_id=1, replica_groups={{0,1,2,3,4,5,6,7},{8,9,10,11,12,13,14,15},{16,17,18,19,20,21,22,23},{24..., dimensions={0} | all-to-all | bytes 2621440 | tf_op jit(solution)/shard_map/all_to_all | solution.py:385
  62.7 0.8 shard_map.91
  63.5 1.0 copy-done.1
  64.6 0.8 copy-done.3
  65.4 0.7 copy-done.5
  66.1 0.7 collective-permute-start
  66.8 3.9 %all-to-all-start.2 = ((bf16[4,576,256]{2,1,0:T(8,128)(2,1)}), bf16[4,576,256]{2,1,0:T(8,128)(2,1)S(1)}, u32[]{:S(2)}, u32[]{:S(2)}) async-start(bf16[4,576,256]{2,1,0:T(8,128)(2,1)} %copy-done.1), calls=%async_computation.2 | async-start | bytes 2359296 | tf_op jit(solution)/shard_map/all_to_all | solution.py:385
  70.6 1.4 collective-permute-done
  72.0 0.9 collective-permute-start.3
  72.9 1.5 collective-permute-start.2
  74.4 1.8 collective-permute-start.1
  76.2 4.8 %shard_map.92 = (bf16[8,1024,256]{2,1,0:T(8,128)(2,1)}, bf16[2,1024,256]{2,1,0:T(8,128)(2,1)}, bf16[2,1024,256]{2,1,0:T(8,128)(2,1)}) custom-call(s32[1]{0:T(128)} %bitcast.core_ref, bf16[4,1024,8,256]{3,2,1,0:T(8,128)(2,1)} %bitcast.41), custom_call_target="tpu_custom_call" | custom-call | bytes 10485760 | tf_op jit(solution)/shard_map/pallas_call | solution.py:108
  81.0 1.9 collective-permute-start.4
  82.9 0.8 collective-permute-start.5
  83.9 3.6 %all-to-all-done.2.refs_4_ = bf16[4,576,256]{2,1,0:T(8,128)(2,1)S(1)} async-done(((bf16[4,576,256]{2,1,0:T(8,128)(2,1)}), bf16[4,576,256]{2,1,0:T(8,128)(2,1)S(1)}, u32[]{:S(2)}, u32[]{:S(2)}) %all-to-all-start.2) | async-done | bytes 1179680 | tf_op jit(solution)/shard_map/all_to_all | solution.py:385
  87.4 5.1 %shard_map.93 = bf16[4,576,256]{2,1,0:T(8,128)(2,1)S(1)} custom-call(s32[4]{0:T(128)S(1)} %pad_add_fusion.s_ref.refs_0_, bf16[8,1024,256]{2,1,0:T(8,128)(2,1)} %get-tuple-element.73.refs_1_, bf16[4,1024,256]{2,1,0:T(8,128)(2,1)} %collective-permute-done.6.refs_2_, bf16[4,1024,256]{2,1,0:T(8,128)(2,1)} %collective-permute-done.7.refs_3_, ...), custom_call_target="tpu_custom_call" | custom-call | flops 2147483648 | bytes 8388608 | tf_op jit(solution)/shard_map/pallas_call | solution.py:78
  92.5 18.5 %all_to_all.46.r_ref = bf16[4,576,256]{2,1,0:T(8,128)(2,1)S(1)} all-to-all(bf16[4,576,256]{2,1,0:T(8,128)(2,1)S(1)} %shard_map.93), channel_id=1, replica_groups=mesh['dp'=4,'tensor'=8,'layer'=4] {'layer'}, dimensions={0} | all-to-all | bytes 2359296 | tf_op jit(solution)/shard_map/all_to_all | solution.py:385
  111.1 0.1 shard_map.94
  111.3 0.5 collective-permute-start.9
  111.8 2.7 %collective-permute-start.10 = (bf16[2,1024,256]{2,1,0:T(8,128)(2,1)S(1)}, bf16[2,1024,256]{2,1,0:T(8,128)(2,1)S(1)}, u32[]{:S(2)}, u32[]{:S(2)}) collective-permute-start(bf16[2,1024,256]{2,1,0:T(8,128)(2,1)S(1)} %copy-done.16), channel_id=1, source_target_pairs={{0,68},{4,64},{8,76},{12,72},{16,84},{20,80},{24,92},{28,88},{32,1... | collective-permute-start | bytes 3145736 | tf_op jit(solution)/shard_map/ppermute | solution.py:426
  114.6 17.7 %all_to_all.47.refs_7_ = bf16[4,512,256]{2,1,0:T(8,128)(2,1)S(1)} all-to-all(bf16[4,512,256]{2,1,0:T(8,128)(2,1)S(1)} %get-tuple-element.80), channel_id=1, replica_groups={{0,8,16,24},{4,12,20,28},{1,9,17,25},{5,13,21,29},{2,10,18,26},{6,14,22..., dimensions={0} | all-to-all | bytes 2097152 | tf_op jit(solution)/shard_map/all_to_all | solution.py:385
  132.3 1.0 copy-done.8
  133.3 0.3 copy-done.9
  133.7 7.6 %shard_map.95 = bf16[4,528,256]{2,1,0:T(8,128)(2,1)S(1)} custom-call(s32[4]{0:T(128)S(1)} %pad_add_fusion.s_ref.refs_0_, s32[4]{0:T(128)S(1)} %select_reduce_fusion.refs_1_, bf16[8,1024,256]{2,1,0:T(8,128)(2,1)} %get-tuple-element.70.refs_2_, bf16[2,1024,256]{2,1,0:T(8,128)(2,1)} %collective-permute-done.4.refs_3_, ...), custom_call_target="tpu_custom_call" | custom-call | flops 2147483648 | bytes 8388608 | tf_op jit(solution)/shard_map/pallas_call | solution.py:78
  141.4 0.1 collective-permute-start.12
  141.5 0.5 collective-permute-start.13
  142.0 18.4 %all_to_all.48.r_ref = bf16[4,528,256]{2,1,0:T(8,128)(2,1)S(1)} all-to-all(bf16[4,528,256]{2,1,0:T(8,128)(2,1)S(1)} %shard_map.95), channel_id=1, replica_groups=mesh['dp'=4,'tensor'=8,'layer'=4] {'layer'}, dimensions={0} | all-to-all | bytes 2162688 | tf_op jit(solution)/shard_map/all_to_all | solution.py:385
  160.4 0.2 shard_map.96
  160.5 17.5 %all_to_all.49.refs_6_ = bf16[4,528,256]{2,1,0:T(8,128)(2,1)S(1)} all-to-all(bf16[4,528,256]{2,1,0:T(8,128)(2,1)S(1)} %get-tuple-element.100), channel_id=1, replica_groups={{0,8,16,24},{4,12,20,28},{1,9,17,25},{5,13,21,29},{2,10,18,26},{6,14,22..., dimensions={0} | all-to-all | bytes 2162688 | tf_op jit(solution)/shard_map/all_to_all | solution.py:385
  178.1 8.4 %all_to_all.50 = bf16[8,16,256]{2,1,0:T(8,128)(2,1)S(1)} all-to-all(bf16[8,16,256]{2,1,0:T(8,128)(2,1)S(1)} %broadcast_in_dim.36), channel_id=1, replica_groups={{0,4,32,36,64,68,96,100},{8,12,40,44,72,76,104,108},{16,20,48,52,80,84,..., dimensions={0} | all-to-all | bytes 131072 | tf_op jit(solution)/shard_map/all_to_all | solution.py:385
  186.5 0.1 convert_element_type.44
  186.6 0.1 reduce.1
  186.8 0.1 convert_element_type.48
  186.9 0.4 subtract_convert_fusion
  187.3 5.2 %shard_map.97 = bf16[8,272,256]{2,1,0:T(8,128)(2,1)S(1)} custom-call(s32[4]{0:T(128)S(1)} %pad_add_fusion.s_ref.refs_0_, bf16[8,1024,256]{2,1,0:T(8,128)(2,1)} %get-tuple-element.68.refs_1_, bf16[2,1024,256]{2,1,0:T(8,128)(2,1)} %copy-done.10, bf16[2,1024,256]{2,1,0:T(8,128)(2,1)} %copy-done.11, bf16[2,1024,256]{2,1,0:T(8,128)(2,1)} %copy-done.12, ...), custom_call_target="tpu_custom_call" | custom-call | flops 2147483648 | bytes 8388608 | tf_op jit(solution)/shard_map/pallas_call | solution.py:78
  192.5 19.2 %all_to_all.51.r_ref = bf16[8,272,256]{2,1,0:T(8,128)(2,1)S(1)} all-to-all(bf16[8,272,256]{2,1,0:T(8,128)(2,1)S(1)} %shard_map.97), channel_id=1, replica_groups={{0,1,2,3,4,5,6,7},{8,9,10,11,12,13,14,15},{16,17,18,19,20,21,22,23},{24..., dimensions={0} | all-to-all | bytes 2228224 | tf_op jit(solution)/shard_map/all_to_all | solution.py:385
  211.7 1.4 shard_map.98
  (57 shorter events, 0.5 us)
Async XLA Ops:
  0.6 186.2 %copy-start = (bf16[1,128,4096]{2,1,0:T(8,128)(2,1)S(1)}, bf16[1,128,4096]{2,1,0:T(8,128)(2,1)}, u32[]{:S(2)}) copy-start(bf16[1,128,4096]{2,1,0:T(8,128)(2,1)} %param.12) | copy-start | bytes 3145732
  3.2 32.5 %all-to-all-start = ((bf16[8,512,256]{2,1,0:T(8,128)(2,1)}), bf16[8,512,256]{2,1,0:T(8,128)(2,1)S(1)}, u32[]{:S(2)}, u32[]{:S(2)}) async-start(bf16[8,512,256]{2,1,0:T(8,128)(2,1)} %broadcast_in_dim.34), calls=%async_computation | async-start | bytes 4194304 | tf_op jit(solution)/shard_map/all_to_all | solution.py:385
  13.5 52.6 %collective-permute-start.6 = (bf16[4,1024,256]{2,1,0:T(8,128)(2,1)}, bf16[4,1024,256]{2,1,0:T(8,128)(2,1)}, u32[]{:S(2)}, u32[]{:S(2)}) collective-permute-start(bf16[4,1024,256]{2,1,0:T(8,128)(2,1)} %get-tuple-element.74), channel_id=1, source_target_pairs={{0,68},{4,64},{8,76},{12,72},{16,84},{20,80},{24,92},{28,88},{32,1... | collective-permute-start | bytes 6291464 | tf_op jit(solution)/shard_map/ppermute | solution.py:433
  21.0 4.9 %copy-start.7 = (bf16[4,64,256]{2,1,0:T(8,128)(2,1)S(1)}, bf16[4,64,256]{2,1,0:T(8,128)(2,1)}, u32[]{:S(2)}) copy-start(bf16[4,64,256]{2,1,0:T(8,128)(2,1)} %p_ref.1) | copy-start | bytes 393220
  25.9 2.2 %copy-start.17 = (s32[4]{0:T(128)S(1)}, s32[4]{0:T(128)}, u32[]{:S(2)}) copy-start(s32[4]{0:T(128)} %param.13) | copy-start | bytes 52
  25.9 1.2 copy-start.2
  62.7 3.4 %copy-start.14 = (bf16[4,64,256]{2,1,0:T(8,128)(2,1)S(1)}, bf16[4,64,256]{2,1,0:T(8,128)(2,1)}, u32[]{:S(2)}) copy-start(bf16[4,64,256]{2,1,0:T(8,128)(2,1)} %param.11) | copy-start | bytes 393220
  63.5 1.1 copy-start.1
  64.6 0.8 copy-start.3
  65.4 0.7 copy-start.5
  66.1 21.4 %collective-permute-start.7 = (bf16[4,1024,256]{2,1,0:T(8,128)(2,1)}, bf16[4,1024,256]{2,1,0:T(8,128)(2,1)}, u32[]{:S(2)}, u32[]{:S(2)}) collective-permute-start(bf16[4,1024,256]{2,1,0:T(8,128)(2,1)} %collective-permute-done.6.refs_2_), channel_id=1, source_target_pairs={{0,32},{32,0},{64,96},{96,64},{1,33},{33,1},{65,97},{97,65},{2,34}... | collective-permute-start | bytes 6291464 | tf_op jit(solution)/shard_map/ppermute | solution.py:431
  66.1 5.9 %collective-permute-start = (bf16[4,64,256]{2,1,0:T(8,128)(2,1)S(1)}, bf16[4,64,256]{2,1,0:T(8,128)(2,1)S(1)}, u32[]{:S(2)}, u32[]{:S(2)}) collective-permute-start(bf16[4,64,256]{2,1,0:T(8,128)(2,1)S(1)} %copy-done.14), channel_id=1, source_target_pairs={{0,4},{4,0},{8,12},{12,8},{16,20},{20,16},{24,28},{28,24},{1,5},{5... | collective-permute-start | bytes 393224 | tf_op jit(solution)/shard_map/ppermute | solution.py:444
  66.8 20.7 %all-to-all-start.2 = ((bf16[4,576,256]{2,1,0:T(8,128)(2,1)}), bf16[4,576,256]{2,1,0:T(8,128)(2,1)S(1)}, u32[]{:S(2)}, u32[]{:S(2)}) async-start(bf16[4,576,256]{2,1,0:T(8,128)(2,1)} %copy-done.1), calls=%async_computation.2 | async-start | bytes 2359296 | tf_op jit(solution)/shard_map/all_to_all | solution.py:385
  72.0 10.9 %collective-permute-start.3 = (bf16[2,64,256]{2,1,0:T(8,128)(2,1)S(1)}, bf16[2,64,256]{2,1,0:T(8,128)(2,1)S(1)}, u32[]{:S(2)}, u32[]{:S(2)}) collective-permute-start(bf16[2,64,256]{2,1,0:T(8,128)(2,1)S(1)} %slice_bitcast_fusion), channel_id=1, source_target_pairs={{0,3},{1,2},{2,1},{3,0},{4,7},{5,6},{6,5},{7,4},{8,11},{9,10},{10,... | collective-permute-start | bytes 196616 | tf_op jit(solution)/shard_map/ppermute | solution.py:449
  72.9 10.8 %collective-permute-start.2 = (bf16[2,64,256]{2,1,0:T(8,128)(2,1)S(1)}, bf16[2,64,256]{2,1,0:T(8,128)(2,1)S(1)}, u32[]{:S(2)}, u32[]{:S(2)}) collective-permute-start(bf16[2,64,256]{2,1,0:T(8,128)(2,1)S(1)} %slice_bitcast_fusion), channel_id=1, source_target_pairs={{0,2},{1,3},{2,0},{3,1},{4,6},{5,7},{6,4},{7,5},{8,10},{9,11},{10,... | collective-permute-start | bytes 196616 | tf_op jit(solution)/shard_map/ppermute | solution.py:449
  74.4 9.3 %collective-permute-start.1 = (bf16[2,64,256]{2,1,0:T(8,128)(2,1)S(1)}, bf16[2,64,256]{2,1,0:T(8,128)(2,1)S(1)}, u32[]{:S(2)}, u32[]{:S(2)}) collective-permute-start(bf16[2,64,256]{2,1,0:T(8,128)(2,1)S(1)} %slice_bitcast_fusion), channel_id=1, source_target_pairs={{0,1},{1,0},{2,3},{3,2},{4,5},{5,4},{6,7},{7,6},{8,9},{9,8},{10,11... | collective-permute-start | bytes 196616 | tf_op jit(solution)/shard_map/ppermute | solution.py:449
  81.0 30.2 %collective-permute-start.4 = (bf16[2,1024,256]{2,1,0:T(8,128)(2,1)}, bf16[2,1024,256]{2,1,0:T(8,128)(2,1)}, u32[]{:S(2)}, u32[]{:S(2)}) collective-permute-start(bf16[2,1024,256]{2,1,0:T(8,128)(2,1)} %get-tuple-element.71), channel_id=1, source_target_pairs={{0,68},{4,64},{8,76},{12,72},{16,84},{20,80},{24,92},{28,88},{32,1... | collective-permute-start | bytes 3145736 | tf_op jit(solution)/shard_map/ppermute | solution.py:426
  82.9 28.3 %collective-permute-start.5 = (bf16[2,1024,256]{2,1,0:T(8,128)(2,1)}, bf16[2,1024,256]{2,1,0:T(8,128)(2,1)}, u32[]{:S(2)}, u32[]{:S(2)}) collective-permute-start(bf16[2,1024,256]{2,1,0:T(8,128)(2,1)} %get-tuple-element.72), channel_id=1, source_target_pairs={{0,4},{4,0},{8,12},{12,8},{16,20},{20,16},{24,28},{28,24},{1,5},{5... | collective-permute-start | bytes 3145736 | tf_op jit(solution)/shard_map/ppermute | solution.py:427
  92.5 18.5 %copy-start.4 = (f32[512,256]{1,0:T(8,128)S(1)}, f32[512,256]{1,0:T(8,128)}, u32[]{:S(2)}) copy-start(f32[512,256]{1,0:T(8,128)} %copy-done.3) | copy-start | bytes 1572868
  92.5 19.3 %copy-start.16 = (bf16[2,1024,256]{2,1,0:T(8,128)(2,1)S(1)}, bf16[2,1024,256]{2,1,0:T(8,128)(2,1)}, u32[]{:S(2)}) copy-start(bf16[2,1024,256]{2,1,0:T(8,128)(2,1)} %get-tuple-element.92) | copy-start | bytes 3145732
  111.1 3.5 %copy-start.15 = (bf16[2,1024,256]{2,1,0:T(8,128)(2,1)S(1)}, bf16[2,1024,256]{2,1,0:T(8,128)(2,1)}, u32[]{:S(2)}) copy-start(bf16[2,1024,256]{2,1,0:T(8,128)(2,1)} %get-tuple-element.93) | copy-start | bytes 3145732
  111.2 22.5 %copy-start.6 = (bf16[512,256]{1,0:T(8,128)(2,1)S(1)}, bf16[512,256]{1,0:T(8,128)(2,1)}, u32[]{:S(2)}) copy-start(bf16[512,256]{1,0:T(8,128)(2,1)} %copy-done.5) | copy-start | bytes 786436
  111.3 21.1 %collective-permute-start.8 = (bf16[2,1024,256]{2,1,0:T(8,128)(2,1)}, bf16[2,1024,256]{2,1,0:T(8,128)(2,1)S(1)}, u32[]{:S(2)}, u32[]{:S(2)}) collective-permute-start(bf16[2,1024,256]{2,1,0:T(8,128)(2,1)} %collective-permute-done.4.refs_3_), channel_id=1, source_target_pairs={{0,32},{32,0},{64,96},{96,64},{1,33},{33,1},{65,97},{97,65},{2,34}... | collective-permute-start | bytes 3145736 | tf_op jit(solution)/shard_map/ppermute | solution.py:431
  111.3 21.0 %collective-permute-start.9 = (bf16[2,1024,256]{2,1,0:T(8,128)(2,1)}, bf16[2,1024,256]{2,1,0:T(8,128)(2,1)S(1)}, u32[]{:S(2)}, u32[]{:S(2)}) collective-permute-start(bf16[2,1024,256]{2,1,0:T(8,128)(2,1)} %collective-permute-done.5.refs_4_), channel_id=1, source_target_pairs={{0,32},{32,0},{64,96},{96,64},{1,33},{33,1},{65,97},{97,65},{2,34}... | collective-permute-start | bytes 3145736 | tf_op jit(solution)/shard_map/ppermute | solution.py:431
  111.8 29.5 %collective-permute-start.10 = (bf16[2,1024,256]{2,1,0:T(8,128)(2,1)S(1)}, bf16[2,1024,256]{2,1,0:T(8,128)(2,1)S(1)}, u32[]{:S(2)}, u32[]{:S(2)}) collective-permute-start(bf16[2,1024,256]{2,1,0:T(8,128)(2,1)S(1)} %copy-done.16), channel_id=1, source_target_pairs={{0,68},{4,64},{8,76},{12,72},{16,84},{20,80},{24,92},{28,88},{32,1... | collective-permute-start | bytes 3145736 | tf_op jit(solution)/shard_map/ppermute | solution.py:426
  114.5 26.8 %collective-permute-start.11 = (bf16[2,1024,256]{2,1,0:T(8,128)(2,1)S(1)}, bf16[2,1024,256]{2,1,0:T(8,128)(2,1)S(1)}, u32[]{:S(2)}, u32[]{:S(2)}) collective-permute-start(bf16[2,1024,256]{2,1,0:T(8,128)(2,1)S(1)} %copy-done.15), channel_id=1, source_target_pairs={{0,4},{4,0},{8,12},{12,8},{16,20},{20,16},{24,28},{28,24},{1,5},{5... | collective-permute-start | bytes 3145736 | tf_op jit(solution)/shard_map/ppermute | solution.py:427
  132.3 1.0 copy-start.8
  132.3 1.4 copy-start.9
  141.3 19.2 %copy-start.10 = (bf16[2,1024,256]{2,1,0:T(8,128)(2,1)}, bf16[2,1024,256]{2,1,0:T(8,128)(2,1)S(1)}, u32[]{:S(2)}) copy-start(bf16[2,1024,256]{2,1,0:T(8,128)(2,1)S(1)} %collective-permute-done.10.refs_2_) | copy-start | bytes 3145732
  141.4 19.2 %copy-start.11 = (bf16[2,1024,256]{2,1,0:T(8,128)(2,1)}, bf16[2,1024,256]{2,1,0:T(8,128)(2,1)S(1)}, u32[]{:S(2)}) copy-start(bf16[2,1024,256]{2,1,0:T(8,128)(2,1)S(1)} %collective-permute-done.11.refs_3_) | copy-start | bytes 3145732
  141.4 19.0 %collective-permute-start.12 = (bf16[2,1024,256]{2,1,0:T(8,128)(2,1)S(1)}, bf16[2,1024,256]{2,1,0:T(8,128)(2,1)S(1)}, u32[]{:S(2)}, u32[]{:S(2)}) collective-permute-start(bf16[2,1024,256]{2,1,0:T(8,128)(2,1)S(1)} %collective-permute-done.10.refs_2_), channel_id=1, source_target_pairs={{0,32},{32,0},{64,96},{96,64},{1,33},{33,1},{65,97},{97,65},{2,34}... | collective-permute-start | bytes 3145736 | tf_op jit(solution)/shard_map/ppermute | solution.py:431
  141.5 18.9 %collective-permute-start.13 = (bf16[2,1024,256]{2,1,0:T(8,128)(2,1)S(1)}, bf16[2,1024,256]{2,1,0:T(8,128)(2,1)S(1)}, u32[]{:S(2)}, u32[]{:S(2)}) collective-permute-start(bf16[2,1024,256]{2,1,0:T(8,128)(2,1)S(1)} %collective-permute-done.11.refs_3_), channel_id=1, source_target_pairs={{0,32},{32,0},{64,96},{96,64},{1,33},{33,1},{65,97},{97,65},{2,34}... | collective-permute-start | bytes 3145736 | tf_op jit(solution)/shard_map/ppermute | solution.py:431
  160.3 17.7 %copy-start.12 = (bf16[2,1024,256]{2,1,0:T(8,128)(2,1)}, bf16[2,1024,256]{2,1,0:T(8,128)(2,1)S(1)}, u32[]{:S(2)}) copy-start(bf16[2,1024,256]{2,1,0:T(8,128)(2,1)S(1)} %collective-permute-done.12.refs_4_) | copy-start | bytes 3145732
  160.3 17.7 %copy-start.13 = (bf16[2,1024,256]{2,1,0:T(8,128)(2,1)}, bf16[2,1024,256]{2,1,0:T(8,128)(2,1)S(1)}, u32[]{:S(2)}) copy-start(bf16[2,1024,256]{2,1,0:T(8,128)(2,1)S(1)} %collective-permute-done.13.refs_5_) | copy-start | bytes 3145732

commit v6 on v5

--- a/solution.py
+++ b/solution.py
@@ -33,23 +33,32 @@
     return pltpu.with_memory_space_constraint(value, pltpu.HBM)
 
 
-def local_call(body, outs, operands, scalars=(), cost=None):
+def local_call(body, outs, operands, scalars=(), cost=None, to_hbm=()):
+    def whole(out):
+        return pl.BlockSpec(out[0], lambda: (0,) * len(out[0]))
+
     return pl.pallas_call(
         body,
         in_specs=[SCALARS] * len(scalars) + [WIDE] * len(operands),
-        out_specs=[WIDE] * len(outs),
-        out_shape=[jax.ShapeDtypeStruct(*out) for out in outs],
+        out_specs=[whole(out) if i in to_hbm else WIDE for i, out in enumerate(outs)],
+        out_shape=[
+            pltpu.HBM(*out) if i in to_hbm else jax.ShapeDtypeStruct(*out)
+            for i, out in enumerate(outs)
+        ],
         compiler_params=limit(8),
         cost_estimate=cost,
     )(*scalars, *operands)
 
 
-def streamed_call(body, outs, weights, operands, scalars, scratch=()):
+def streamed_call(body, outs, weights, operands, scalars, scratch=(), late=()):
     rows, width = weights[0].shape[1:]
     tokens = operands[0].shape[-1]
     cells = sum(w.shape[0] for w in weights)
     groups = rows // width
-    sizes = [len(scalars), len(weights), len(operands), len(outs), len(weights), len(scratch)]
+    moved = [*weights, *late]
+    sizes = [
+        len(scalars), len(moved), len(operands), len(outs), len(moved), len(scratch),
+    ]
 
     def kernel(*refs):
         parts, at = [], 0
@@ -58,40 +67,56 @@
             at += size
         scalar_refs, far_refs, operand_refs, out_refs, held_refs, scratch_refs = parts
         sems = refs[-1]
-
-        def copy(k, n):
+        count = len(weights)
+
+        def copies(n):
+            if n < 0:
+                return [
+                    pltpu.make_async_copy(far_refs[k], held_refs[k], sems.at[k, 0])
+                    for k in range(count, len(moved))
+                ]
             rows_of = pl.ds(n * width, width)
-            return pltpu.make_async_copy(
-                far_refs[k].at[:, rows_of], held_refs[k].at[:, rows_of], sems.at[k, n]
-            )
-
-        for n in range(groups):
-            for k in range(len(weights)):
-                copy(k, n).start()
+            return [
+                pltpu.make_async_copy(
+                    far_refs[k].at[:, rows_of], held_refs[k].at[:, rows_of], sems.at[k, n]
+                )
+                for k in range(count)
+            ]
+
+        for n in [*range(groups), -1]:
+            for copy in copies(n):
+                copy.start()
 
         def fetch(n):
-            for k in range(len(weights)):
-                copy(k, n).wait()
-
-        body(fetch, scalar_refs, held_refs, operand_refs, out_refs, scratch_refs)
+            for copy in copies(n):
+                copy.wait()
+
+        body(
+            fetch,
+            scalar_refs,
+            held_refs[:count],
+            [*operand_refs, *held_refs[count:]],
+            out_refs,
+            scratch_refs,
+        )
 
     return pl.pallas_call(
         kernel,
         in_specs=[SCALARS] * len(scalars)
-        + [pl.BlockSpec(memory_space=pltpu.HBM)] * len(weights)
+        + [pl.BlockSpec(memory_space=pltpu.HBM)] * len(moved)
         + [WIDE] * len(operands),
         out_specs=[WIDE] * len(outs),
         out_shape=[jax.ShapeDtypeStruct(*out) for out in outs],
-        scratch_shapes=[pltpu.VMEM(w.shape, w.dtype) for w in weights]
+        scratch_shapes=[pltpu.VMEM(w.shape, w.dtype) for w in moved]
         + list(scratch)
-        + [pltpu.SemaphoreType.DMA((len(weights), groups))],
+        + [pltpu.SemaphoreType.DMA((len(moved), groups))],
         compiler_params=limit(20),
         cost_estimate=pl.CostEstimate(
             flops=2 * cells * width * rows * tokens,
             bytes_accessed=2 * cells * width * rows,
             transcendentals=0,
         ),
-    )(*scalars, *weights, *operands)
+    )(*scalars, *moved, *operands)
 
 
 def features_first(weights, level, core, pieces):
@@ -262,14 +287,15 @@
     )[0]
 
 
-def last_partial(place, gathered, held, kept, extra):
+def last_partial(place, gathered, held, kept, under):
     width = held[0].shape[2]
     groups = held[0].shape[1] // width
 
     def body(fetch, scalar_refs, w_refs, operand_refs, out_refs, _):
-        (s_ref,), (g_ref, t_ref, e_ref), (o_ref,) = scalar_refs, operand_refs, out_refs
+        (s_ref,), (g_ref, t_ref), (o_ref,) = scalar_refs, operand_refs, out_refs
         for k in range(2 * groups):
-            o_ref[k, width:] = e_ref[k % groups]
+            o_ref[k, width:] = jnp.zeros((under, o_ref.shape[2]), o_ref.dtype)
+        fetch(-1)
         for n in range(groups):
             fetch(n)
             for column, total in pair_totals(s_ref, g_ref, w_refs, n):
@@ -280,11 +306,39 @@
 
     return streamed_call(
         body,
-        [((2 * groups, width + extra.shape[1], gathered.shape[2]), BF16)],
+        [((2 * groups, width + under, gathered.shape[2]), BF16)],
         held,
-        [gathered, kept, extra],
+        [gathered],
         [place],
+        late=[kept],
     )[0]
+
+
+def put_under(partial, extra):
+    blocks, deep, _ = partial.shape
+    groups, rows, _ = extra.shape
+
+    def body(_, e_ref, o_ref, sems):
+        copies = [
+            pltpu.make_async_copy(
+                e_ref.at[k % groups], o_ref.at[k, pl.ds(deep - rows, rows)], sems.at[k]
+            )
+            for k in range(blocks)
+        ]
+        for copy in copies:
+            copy.start()
+        for copy in copies:
+            copy.wait()
+
+    return pl.pallas_call(
+        body,
+        in_specs=[pl.BlockSpec(memory_space=pl.ANY), WIDE],
+        out_specs=pl.BlockSpec(memory_space=pl.ANY),
+        out_shape=jax.ShapeDtypeStruct(partial.shape, partial.dtype),
+        scratch_shapes=[pltpu.SemaphoreType.DMA((blocks,))],
+        input_output_aliases={0: 0},
+        compiler_params=limit(4),
+    )(partial, extra)
 
 
 def settle_first(place, arrived, gathered):
@@ -318,6 +372,7 @@
         ],
         [arrived, gathered],
         [place],
+        to_hbm=(0, 1, 2, 3),
     )
 
 
@@ -360,7 +415,10 @@
             c_ref[j, depth:] = blocks
 
     return local_call(
-        body, [(total.shape, F32), ((groups, deep, half), BF16)], [arrived, total]
+        body,
+        [(total.shape, F32), ((groups, deep, half), BF16)],
+        [arrived, total],
+        to_hbm=(0,),
     )
 
 
@@ -500,7 +558,10 @@
     low = (scored - high.astype(F32)).astype(BF16)
     carried = jnp.concatenate([high, low], axis=1)[:, None, :]
     carried = jnp.broadcast_to(carried, (n_dp, 16, carried.shape[2]))
-    partial = last_partial(place, gathered, [own[0], *near[0], *far[0]], total, carried)
+    partial = last_partial(
+        place, gathered, [own[0], *near[0], *far[0]], total, carried.shape[1]
+    )
+    partial = put_under(partial, carried)
     arrived = exchange(partial, ("tensor", "layer"), along_xz)
     input_grad, scores = finish(place, arrived)
     return input_grad, scores

time: 214 us -> 213 us (level)
  blocking collectives: 123 us -> 115 us
  starting transfers between devices: 24 us -> 28.5 us
  Pallas kernels: 44.3 us -> 46.9 us
    all_to_all x7 -> x6, blocking collectives: 123 us -> 115 us  [exchange(): lax.all_to_all(blocks, axes, 0, 0, tiled=True, axis_index_groups=groups)]
    all_to_all x2 -> x3, starting transfers between devices: 9.33 us -> 12.7 us  [exchange(): lax.all_to_all(blocks, axes, 0, 0, tiled=True, axis_index_groups=groups)]
    pallas_call x4, Pallas kernels: 2.59 us -> 4.9 us  [local_call(): pl.pallas_call(body, in_specs=[SCALARS] * len(scalars) + [WIDE] * len(ope...]
    unnamed x37 -> x35, local copies, waits for them, and re-layouts: 5.2 us -> 3.7 us
    all_to_all x2 -> x3, waiting for transfers between devices: 11 us -> 11 us  [exchange(): lax.all_to_all(blocks, axes, 0, 0, tiled=True, axis_index_groups=groups)]
  transfers between devices with their start and end apart: 16 -> 17, of which waited for: 3 -> 3; matrix products, arithmetic and copies ran while one was open for 0% -> 0% of each run, Pallas kernels for 18% -> 21%
where the time goes in v6:
time: 213 us; the launch traced here: 212 us
  blocking collectives  115 us (54%)
  Pallas kernels  46.9 us (22%)
  starting transfers between devices  28.5 us (13%)
  waiting for transfers between devices  12.4 us (6%)
  local copies, waits for them, and re-layouts  7.17 us (3%)
    all_to_all x6, blocking collectives, exchange(): lax.all_to_all(blocks, axes, 0, 0, tiled=True, axis_index_groups=groups)  115 us
    pallas_call x4, Pallas kernels, streamed_call(): pl.pallas_call(kernel, in_specs=[SCALARS] * len(scalars) + [pl.BlockSpec(...  22.1 us
    pallas_call x4, Pallas kernels, features_first(): pl.pallas_call(body, grid_spec=pltpu.PrefetchScalarGridSpec(num_scalar_pr...  18.8 us
    all_to_all x3, starting transfers between devices, exchange(): lax.all_to_all(blocks, axes, 0, 0, tiled=True, axis_index_groups=groups)  12.7 us
    all_to_all x3, waiting for transfers between devices, exchange(): lax.all_to_all(blocks, axes, 0, 0, tiled=True, axis_index_groups=groups)  11 us
    pallas_call x4, Pallas kernels, local_call(): pl.pallas_call(body, in_specs=[SCALARS] * len(scalars) + [WIDE] * len(ope...  4.9 us
    ppermute x2, starting transfers between devices, over_both(): lax.ppermute(values[0], ('dp', 'tensor'), across)  4.85 us
  transfers between devices with their start and end apart: 17, of which 3 were waited for; matrix products, arithmetic and copies ran while one was open for 0% of the time, Pallas kernels for 21%

profile of v6, /device:TPU:0, one launch (start us, length us, event | category | flops | bytes accessed | tf_op | source)
XLA Modules:
  0.0 211.9 jit_solution(6779043927850786299)
XLA Ops:
  0.6 2.6 %broadcast_in_dim.34 = bf16[8,512,256]{2,1,0:T(8,128)(2,1)} broadcast(bf16[512,256]{1,0:T(8,128)(2,1)} %param.8), dimensions={1,2} | broadcast | bytes 2359296 | tf_op jit(solution)/shard_map/broadcast_in_dim | solution.py:475
  3.2 5.5 %all-to-all-start = ((bf16[8,512,256]{2,1,0:T(8,128)(2,1)}), bf16[8,512,256]{2,1,0:T(8,128)(2,1)S(1)}, u32[]{:S(2)}, u32[]{:S(2)}) async-start(bf16[8,512,256]{2,1,0:T(8,128)(2,1)} %broadcast_in_dim.34), calls=%async_computation | async-start | bytes 4194304 | tf_op jit(solution)/shard_map/all_to_all | solution.py:443
  8.7 4.8 %shard_map.87 = (bf16[8,1024,256]{2,1,0:T(8,128)(2,1)}, bf16[4,1024,256]{2,1,0:T(8,128)(2,1)}) custom-call(s32[1]{0:T(128)} %bitcast.core_ref, bf16[4,1024,8,256]{3,2,1,0:T(8,128)(2,1)} %bitcast.38), custom_call_target="tpu_custom_call" | custom-call | bytes 10485760 | tf_op jit(solution)/shard_map/pallas_call | solution.py:133
  13.5 3.3 %collective-permute-start.6 = (bf16[4,1024,256]{2,1,0:T(8,128)(2,1)}, bf16[4,1024,256]{2,1,0:T(8,128)(2,1)}, u32[]{:S(2)}, u32[]{:S(2)}) collective-permute-start(bf16[4,1024,256]{2,1,0:T(8,128)(2,1)} %get-tuple-element.74), channel_id=1, source_target_pairs={{0,68},{4,64},{8,76},{12,72},{16,84},{20,80},{24,92},{28,88},{32,1... | collective-permute-start | bytes 6291464 | tf_op jit(solution)/shard_map/ppermute | solution.py:491
  16.8 4.2 %shard_map.86.refs_0_ = bf16[8,1024,256]{2,1,0:T(8,128)(2,1)} custom-call(s32[1]{0:T(128)} %bitcast.core_ref, bf16[4,1024,8,256]{3,2,1,0:T(8,128)(2,1)} %bitcast.39), custom_call_target="tpu_custom_call" | custom-call | bytes 10485760 | tf_op jit(solution)/shard_map/pallas_call | solution.py:133
  21.0 4.9 %shard_map.88 = (bf16[8,1024,256]{2,1,0:T(8,128)(2,1)}, bf16[2,1024,256]{2,1,0:T(8,128)(2,1)}, bf16[2,1024,256]{2,1,0:T(8,128)(2,1)}) custom-call(s32[1]{0:T(128)} %bitcast.core_ref, bf16[4,1024,8,256]{3,2,1,0:T(8,128)(2,1)} %bitcast.40), custom_call_target="tpu_custom_call" | custom-call | bytes 10485760 | tf_op jit(solution)/shard_map/pallas_call | solution.py:133
  26.0 1.2 copy-done.1
  27.2 0.9 shard_map.89
  28.2 0.1 select_reduce_fusion.refs_1_
  28.3 7.4 %all-to-all-done.refs_1_.g_ref = bf16[8,512,256]{2,1,0:T(8,128)(2,1)S(1)} async-done(((bf16[8,512,256]{2,1,0:T(8,128)(2,1)}), bf16[8,512,256]{2,1,0:T(8,128)(2,1)S(1)}, u32[]{:S(2)}, u32[]{:S(2)}) %all-to-all-start) | async-done | bytes 2097184 | tf_op jit(solution)/shard_map/all_to_all | solution.py:443
  35.7 4.2 %shard_map.90 = bf16[8,320,256]{2,1,0:T(8,128)(2,1)S(1)} custom-call(bf16[8,1024,256]{2,1,0:T(8,128)(2,1)} %shard_map.86.refs_0_, bf16[8,512,256]{2,1,0:T(8,128)(2,1)S(1)} %all-to-all-done.refs_1_.g_ref, bf16[8,64,256]{2,1,0:T(8,128)(2,1)S(1)} %bitcast.37), custom_call_target="tpu_custom_call" | custom-call | flops 1073741824 | bytes 4194304 | tf_op jit(solution)/shard_map/pallas_call | solution.py:103
  39.9 22.8 %all_to_all.45.r_ref = bf16[8,320,256]{2,1,0:T(8,128)(2,1)S(1)} all-to-all(bf16[8,320,256]{2,1,0:T(8,128)(2,1)S(1)} %shard_map.90), channel_id=1, replica_groups={{0,1,2,3,4,5,6,7},{8,9,10,11,12,13,14,15},{16,17,18,19,20,21,22,23},{24..., dimensions={0} | all-to-all | bytes 2621440 | tf_op jit(solution)/shard_map/all_to_all | solution.py:443
  62.7 2.2 %shard_map.91 = (f32[512,256]{1,0:T(8,128)}, bf16[4,576,256]{2,1,0:T(8,128)(2,1)}, bf16[512,256]{1,0:T(8,128)(2,1)}, bf16[512,256]{1,0:T(8,128)(2,1)}) custom-call(s32[4]{0:T(128)S(1)} %pad_add_fusion.s_ref.refs_0_, bf16[8,320,256]{2,1,0:T(8,128)(2,1)S(1)} %all_to_all.45.r_ref, bf16[8,512,256]{2,1,0:T(8,128)(2,1)S(1)} %all-to-all-done.refs_1_.g_ref), custom_call_target="tpu_custom_call" | custom-call | tf_op jit(solution)/shard_map/pallas_call | solution.py:40
  64.9 0.7 collective-permute-start
  65.5 3.9 %all-to-all-start.2 = ((bf16[4,576,256]{2,1,0:T(8,128)(2,1)}), bf16[4,576,256]{2,1,0:T(8,128)(2,1)S(1)}, u32[]{:S(2)}, u32[]{:S(2)}) async-start(bf16[4,576,256]{2,1,0:T(8,128)(2,1)} %get-tuple-element.60), calls=%async_computation.2 | async-start | bytes 2359296 | tf_op jit(solution)/shard_map/all_to_all | solution.py:443
  69.4 1.4 collective-permute-done
  70.8 1.5 collective-permute-start.3
  72.3 0.9 collective-permute-start.2
  73.2 1.8 collective-permute-start.1
  75.0 4.8 %shard_map.92 = (bf16[8,1024,256]{2,1,0:T(8,128)(2,1)}, bf16[2,1024,256]{2,1,0:T(8,128)(2,1)}, bf16[2,1024,256]{2,1,0:T(8,128)(2,1)}) custom-call(s32[1]{0:T(128)} %bitcast.core_ref, bf16[4,1024,8,256]{3,2,1,0:T(8,128)(2,1)} %bitcast.41), custom_call_target="tpu_custom_call" | custom-call | bytes 10485760 | tf_op jit(solution)/shard_map/pallas_call | solution.py:133
  79.8 1.9 collective-permute-start.4
  81.7 0.8 collective-permute-start.5
  82.7 3.5 %all-to-all-done.2.refs_4_ = bf16[4,576,256]{2,1,0:T(8,128)(2,1)S(1)} async-done(((bf16[4,576,256]{2,1,0:T(8,128)(2,1)}), bf16[4,576,256]{2,1,0:T(8,128)(2,1)S(1)}, u32[]{:S(2)}, u32[]{:S(2)}) %all-to-all-start.2) | async-done | bytes 1179680 | tf_op jit(solution)/shard_map/all_to_all | solution.py:443
  86.2 5.1 %shard_map.93 = bf16[4,576,256]{2,1,0:T(8,128)(2,1)S(1)} custom-call(s32[4]{0:T(128)S(1)} %pad_add_fusion.s_ref.refs_0_, bf16[8,1024,256]{2,1,0:T(8,128)(2,1)} %get-tuple-element.73.refs_1_, bf16[4,1024,256]{2,1,0:T(8,128)(2,1)} %collective-permute-done.6.refs_2_, bf16[4,1024,256]{2,1,0:T(8,128)(2,1)} %collective-permute-done.7.refs_3_, ...), custom_call_target="tpu_custom_call" | custom-call | flops 2147483648 | bytes 8388608 | tf_op jit(solution)/shard_map/pallas_call | solution.py:103
  91.3 18.7 %all_to_all.46.r_ref = bf16[4,576,256]{2,1,0:T(8,128)(2,1)S(1)} all-to-all(bf16[4,576,256]{2,1,0:T(8,128)(2,1)S(1)} %shard_map.93), channel_id=1, replica_groups=mesh['dp'=4,'tensor'=8,'layer'=4] {'layer'}, dimensions={0} | all-to-all | bytes 2359296 | tf_op jit(solution)/shard_map/all_to_all | solution.py:443
  110.0 0.1 shard_map.94
  110.3 0.5 collective-permute-start.9
  110.8 3.0 %collective-permute-start.10 = (bf16[2,1024,256]{2,1,0:T(8,128)(2,1)S(1)}, bf16[2,1024,256]{2,1,0:T(8,128)(2,1)S(1)}, u32[]{:S(2)}, u32[]{:S(2)}) collective-permute-start(bf16[2,1024,256]{2,1,0:T(8,128)(2,1)S(1)} %copy-done.15), channel_id=1, source_target_pairs={{0,68},{4,64},{8,76},{12,72},{16,84},{20,80},{24,92},{28,88},{32,1... | collective-permute-start | bytes 3145736 | tf_op jit(solution)/shard_map/ppermute | solution.py:484
  113.8 0.8 collective-permute-start.11
  114.6 17.5 %all_to_all.47.refs_7_ = bf16[4,512,256]{2,1,0:T(8,128)(2,1)S(1)} all-to-all(bf16[4,512,256]{2,1,0:T(8,128)(2,1)S(1)} %get-tuple-element.80), channel_id=1, replica_groups={{0,8,16,24},{4,12,20,28},{1,9,17,25},{5,13,21,29},{2,10,18,26},{6,14,22..., dimensions={0} | all-to-all | bytes 2097152 | tf_op jit(solution)/shard_map/all_to_all | solution.py:443
  132.1 1.0 copy-done.7
  133.1 0.4 copy-done.8
  133.5 7.6 %shard_map.95 = bf16[4,528,256]{2,1,0:T(8,128)(2,1)S(1)} custom-call(s32[4]{0:T(128)S(1)} %pad_add_fusion.s_ref.refs_0_, s32[4]{0:T(128)S(1)} %select_reduce_fusion.refs_1_, bf16[8,1024,256]{2,1,0:T(8,128)(2,1)} %get-tuple-element.70.refs_2_, bf16[2,1024,256]{2,1,0:T(8,128)(2,1)} %collective-permute-done.4.refs_3_, ...), custom_call_target="tpu_custom_call" | custom-call | flops 2147483648 | bytes 8388608 | tf_op jit(solution)/shard_map/pallas_call | solution.py:103
  141.3 0.5 collective-permute-start.13
  141.8 18.4 %all_to_all.48.r_ref = bf16[4,528,256]{2,1,0:T(8,128)(2,1)S(1)} all-to-all(bf16[4,528,256]{2,1,0:T(8,128)(2,1)S(1)} %shard_map.95), channel_id=1, replica_groups=mesh['dp'=4,'tensor'=8,'layer'=4] {'layer'}, dimensions={0} | all-to-all | bytes 2162688 | tf_op jit(solution)/shard_map/all_to_all | solution.py:443
  160.2 1.1 shard_map.96
  161.3 17.5 %all_to_all.49.refs_7_ = bf16[4,528,256]{2,1,0:T(8,128)(2,1)S(1)} all-to-all(bf16[4,528,256]{2,1,0:T(8,128)(2,1)S(1)} %get-tuple-element.101), channel_id=1, replica_groups={{0,8,16,24},{4,12,20,28},{1,9,17,25},{5,13,21,29},{2,10,18,26},{6,14,22..., dimensions={0} | all-to-all | bytes 2162688 | tf_op jit(solution)/shard_map/all_to_all | solution.py:443
  178.8 0.6 broadcast_in_dim.36
  179.4 3.4 %all-to-all-start.7 = ((bf16[8,16,256]{2,1,0:T(8,128)(2,1)}), bf16[8,16,256]{2,1,0:T(8,128)(2,1)S(1)}, u32[]{:S(2)}, u32[]{:S(2)}) async-start(bf16[8,16,256]{2,1,0:T(8,128)(2,1)} %broadcast_in_dim.36), calls=%async_computation.7 | async-start | bytes 131072 | tf_op jit(solution)/shard_map/all_to_all | solution.py:443
  182.8 1.0 copy-done.2
  183.8 5.2 %shard_map.97._ = bf16[8,272,256]{2,1,0:T(8,128)(2,1)S(1)} custom-call(s32[4]{0:T(128)S(1)} %pad_add_fusion.s_ref.refs_0_, bf16[8,1024,256]{2,1,0:T(8,128)(2,1)} %get-tuple-element.68.refs_1_, bf16[2,1024,256]{2,1,0:T(8,128)(2,1)} %copy-done.9, bf16[2,1024,256]{2,1,0:T(8,128)(2,1)} %copy-done.10, bf16[2,1024,256]{2,1,0:T(8,128)(2,1)} %copy-done.11, ...), custom_call_target="tpu_custom_call" | custom-call | flops 2147483648 | bytes 8388608 | tf_op jit(solution)/shard_map/pallas_call | solution.py:103
  189.1 0.1 convert_element_type.44
  189.2 0.1 reduce.1
  189.3 0.1 convert_element_type.48
  189.4 0.4 subtract_convert_fusion
  189.8 0.2 shard_map.98
  190.0 20.4 %all_to_all.50.r_ref = bf16[8,272,256]{2,1,0:T(8,128)(2,1)S(1)} all-to-all(bf16[8,272,256]{2,1,0:T(8,128)(2,1)S(1)} %shard_map.98), channel_id=1, replica_groups={{0,1,2,3,4,5,6,7},{8,9,10,11,12,13,14,15},{16,17,18,19,20,21,22,23},{24..., dimensions={0} | all-to-all | bytes 2228224 | tf_op jit(solution)/shard_map/all_to_all | solution.py:443
  210.5 1.4 shard_map.99
  (57 shorter events, 0.6 us)
Async XLA Ops:
  0.6 188.8 %copy-start = (bf16[1,128,4096]{2,1,0:T(8,128)(2,1)S(1)}, bf16[1,128,4096]{2,1,0:T(8,128)(2,1)}, u32[]{:S(2)}) copy-start(bf16[1,128,4096]{2,1,0:T(8,128)(2,1)} %param.12) | copy-start | bytes 3145732
  3.2 32.5 %all-to-all-start = ((bf16[8,512,256]{2,1,0:T(8,128)(2,1)}), bf16[8,512,256]{2,1,0:T(8,128)(2,1)S(1)}, u32[]{:S(2)}, u32[]{:S(2)}) async-start(bf16[8,512,256]{2,1,0:T(8,128)(2,1)} %broadcast_in_dim.34), calls=%async_computation | async-start | bytes 4194304 | tf_op jit(solution)/shard_map/all_to_all | solution.py:443
  13.5 51.3 %collective-permute-start.6 = (bf16[4,1024,256]{2,1,0:T(8,128)(2,1)}, bf16[4,1024,256]{2,1,0:T(8,128)(2,1)}, u32[]{:S(2)}, u32[]{:S(2)}) collective-permute-start(bf16[4,1024,256]{2,1,0:T(8,128)(2,1)} %get-tuple-element.74), channel_id=1, source_target_pairs={{0,68},{4,64},{8,76},{12,72},{16,84},{20,80},{24,92},{28,88},{32,1... | collective-permute-start | bytes 6291464 | tf_op jit(solution)/shard_map/ppermute | solution.py:491
  21.0 4.9 %copy-start.6 = (bf16[4,64,256]{2,1,0:T(8,128)(2,1)S(1)}, bf16[4,64,256]{2,1,0:T(8,128)(2,1)}, u32[]{:S(2)}) copy-start(bf16[4,64,256]{2,1,0:T(8,128)(2,1)} %p_ref.1) | copy-start | bytes 393220
  26.0 2.2 %copy-start.16 = (s32[4]{0:T(128)S(1)}, s32[4]{0:T(128)}, u32[]{:S(2)}) copy-start(s32[4]{0:T(128)} %param.13) | copy-start | bytes 52
  26.0 1.2 copy-start.1
  62.7 2.2 %copy-start.13 = (bf16[4,64,256]{2,1,0:T(8,128)(2,1)S(1)}, bf16[4,64,256]{2,1,0:T(8,128)(2,1)}, u32[]{:S(2)}) copy-start(bf16[4,64,256]{2,1,0:T(8,128)(2,1)} %param.11) | copy-start | bytes 393220
  64.8 21.4 %collective-permute-start.7 = (bf16[4,1024,256]{2,1,0:T(8,128)(2,1)}, bf16[4,1024,256]{2,1,0:T(8,128)(2,1)}, u32[]{:S(2)}, u32[]{:S(2)}) collective-permute-start(bf16[4,1024,256]{2,1,0:T(8,128)(2,1)} %collective-permute-done.6.refs_2_), channel_id=1, source_target_pairs={{0,32},{32,0},{64,96},{96,64},{1,33},{33,1},{65,97},{97,65},{2,34}... | collective-permute-start | bytes 6291464 | tf_op jit(solution)/shard_map/ppermute | solution.py:489
  64.9 5.9 %collective-permute-start = (bf16[4,64,256]{2,1,0:T(8,128)(2,1)S(1)}, bf16[4,64,256]{2,1,0:T(8,128)(2,1)S(1)}, u32[]{:S(2)}, u32[]{:S(2)}) collective-permute-start(bf16[4,64,256]{2,1,0:T(8,128)(2,1)S(1)} %copy-done.13), channel_id=1, source_target_pairs={{0,4},{4,0},{8,12},{12,8},{16,20},{20,16},{24,28},{28,24},{1,5},{5... | collective-permute-start | bytes 393224 | tf_op jit(solution)/shard_map/ppermute | solution.py:502
  65.5 20.7 %all-to-all-start.2 = ((bf16[4,576,256]{2,1,0:T(8,128)(2,1)}), bf16[4,576,256]{2,1,0:T(8,128)(2,1)S(1)}, u32[]{:S(2)}, u32[]{:S(2)}) async-start(bf16[4,576,256]{2,1,0:T(8,128)(2,1)} %get-tuple-element.60), calls=%async_computation.2 | async-start | bytes 2359296 | tf_op jit(solution)/shard_map/all_to_all | solution.py:443
  70.8 10.9 %collective-permute-start.3 = (bf16[2,64,256]{2,1,0:T(8,128)(2,1)S(1)}, bf16[2,64,256]{2,1,0:T(8,128)(2,1)S(1)}, u32[]{:S(2)}, u32[]{:S(2)}) collective-permute-start(bf16[2,64,256]{2,1,0:T(8,128)(2,1)S(1)} %slice_bitcast_fusion), channel_id=1, source_target_pairs={{0,3},{1,2},{2,1},{3,0},{4,7},{5,6},{6,5},{7,4},{8,11},{9,10},{10,... | collective-permute-start | bytes 196616 | tf_op jit(solution)/shard_map/ppermute | solution.py:507
  72.3 10.2 %collective-permute-start.2 = (bf16[2,64,256]{2,1,0:T(8,128)(2,1)S(1)}, bf16[2,64,256]{2,1,0:T(8,128)(2,1)S(1)}, u32[]{:S(2)}, u32[]{:S(2)}) collective-permute-start(bf16[2,64,256]{2,1,0:T(8,128)(2,1)S(1)} %slice_bitcast_fusion), channel_id=1, source_target_pairs={{0,2},{1,3},{2,0},{3,1},{4,6},{5,7},{6,4},{7,5},{8,10},{9,11},{10,... | collective-permute-start | bytes 196616 | tf_op jit(solution)/shard_map/ppermute | solution.py:507
  73.2 9.3 %collective-permute-start.1 = (bf16[2,64,256]{2,1,0:T(8,128)(2,1)S(1)}, bf16[2,64,256]{2,1,0:T(8,128)(2,1)S(1)}, u32[]{:S(2)}, u32[]{:S(2)}) collective-permute-start(bf16[2,64,256]{2,1,0:T(8,128)(2,1)S(1)} %slice_bitcast_fusion), channel_id=1, source_target_pairs={{0,1},{1,0},{2,3},{3,2},{4,5},{5,4},{6,7},{7,6},{8,9},{9,8},{10,11... | collective-permute-start | bytes 196616 | tf_op jit(solution)/shard_map/ppermute | solution.py:507
  79.8 30.3 %collective-permute-start.4 = (bf16[2,1024,256]{2,1,0:T(8,128)(2,1)}, bf16[2,1024,256]{2,1,0:T(8,128)(2,1)}, u32[]{:S(2)}, u32[]{:S(2)}) collective-permute-start(bf16[2,1024,256]{2,1,0:T(8,128)(2,1)} %get-tuple-element.71), channel_id=1, source_target_pairs={{0,68},{4,64},{8,76},{12,72},{16,84},{20,80},{24,92},{28,88},{32,1... | collective-permute-start | bytes 3145736 | tf_op jit(solution)/shard_map/ppermute | solution.py:484
  81.7 28.5 %collective-permute-start.5 = (bf16[2,1024,256]{2,1,0:T(8,128)(2,1)}, bf16[2,1024,256]{2,1,0:T(8,128)(2,1)}, u32[]{:S(2)}, u32[]{:S(2)}) collective-permute-start(bf16[2,1024,256]{2,1,0:T(8,128)(2,1)} %get-tuple-element.72), channel_id=1, source_target_pairs={{0,4},{4,0},{8,12},{12,8},{16,20},{20,16},{24,28},{28,24},{1,5},{5... | collective-permute-start | bytes 3145736 | tf_op jit(solution)/shard_map/ppermute | solution.py:485
  91.3 18.7 %copy-start.3 = (f32[512,256]{1,0:T(8,128)S(1)}, f32[512,256]{1,0:T(8,128)}, u32[]{:S(2)}) copy-start(f32[512,256]{1,0:T(8,128)} %get-tuple-element.66.t_ref) | copy-start | bytes 1572868
  91.3 19.5 %copy-start.15 = (bf16[2,1024,256]{2,1,0:T(8,128)(2,1)S(1)}, bf16[2,1024,256]{2,1,0:T(8,128)(2,1)}, u32[]{:S(2)}) copy-start(bf16[2,1024,256]{2,1,0:T(8,128)(2,1)} %get-tuple-element.92) | copy-start | bytes 3145732
  110.0 3.8 %copy-start.14 = (bf16[2,1024,256]{2,1,0:T(8,128)(2,1)S(1)}, bf16[2,1024,256]{2,1,0:T(8,128)(2,1)}, u32[]{:S(2)}) copy-start(bf16[2,1024,256]{2,1,0:T(8,128)(2,1)} %get-tuple-element.93) | copy-start | bytes 3145732
  110.1 23.3 %copy-start.4 = (bf16[512,256]{1,0:T(8,128)(2,1)S(1)}, bf16[512,256]{1,0:T(8,128)(2,1)}, u32[]{:S(2)}) copy-start(bf16[512,256]{1,0:T(8,128)(2,1)} %get-tuple-element.84.refs_8_) | copy-start | bytes 786436
  110.2 23.3 %copy-start.5 = (bf16[512,256]{1,0:T(8,128)(2,1)S(1)}, bf16[512,256]{1,0:T(8,128)(2,1)}, u32[]{:S(2)}) copy-start(bf16[512,256]{1,0:T(8,128)(2,1)} %get-tuple-element.85.refs_9_) | copy-start | bytes 786436
  110.2 21.9 %collective-permute-start.8 = (bf16[2,1024,256]{2,1,0:T(8,128)(2,1)}, bf16[2,1024,256]{2,1,0:T(8,128)(2,1)S(1)}, u32[]{:S(2)}, u32[]{:S(2)}) collective-permute-start(bf16[2,1024,256]{2,1,0:T(8,128)(2,1)} %collective-permute-done.4.refs_3_), channel_id=1, source_target_pairs={{0,32},{32,0},{64,96},{96,64},{1,33},{33,1},{65,97},{97,65},{2,34}... | collective-permute-start | bytes 3145736 | tf_op jit(solution)/shard_map/ppermute | solution.py:489
  110.3 21.8 %collective-permute-start.9 = (bf16[2,1024,256]{2,1,0:T(8,128)(2,1)}, bf16[2,1024,256]{2,1,0:T(8,128)(2,1)S(1)}, u32[]{:S(2)}, u32[]{:S(2)}) collective-permute-start(bf16[2,1024,256]{2,1,0:T(8,128)(2,1)} %collective-permute-done.5.refs_4_), channel_id=1, source_target_pairs={{0,32},{32,0},{64,96},{96,64},{1,33},{33,1},{65,97},{97,65},{2,34}... | collective-permute-start | bytes 3145736 | tf_op jit(solution)/shard_map/ppermute | solution.py:489
  110.8 30.4 %collective-permute-start.10 = (bf16[2,1024,256]{2,1,0:T(8,128)(2,1)S(1)}, bf16[2,1024,256]{2,1,0:T(8,128)(2,1)S(1)}, u32[]{:S(2)}, u32[]{:S(2)}) collective-permute-start(bf16[2,1024,256]{2,1,0:T(8,128)(2,1)S(1)} %copy-done.15), channel_id=1, source_target_pairs={{0,68},{4,64},{8,76},{12,72},{16,84},{20,80},{24,92},{28,88},{32,1... | collective-permute-start | bytes 3145736 | tf_op jit(solution)/shard_map/ppermute | solution.py:484
  113.8 27.4 %collective-permute-start.11 = (bf16[2,1024,256]{2,1,0:T(8,128)(2,1)S(1)}, bf16[2,1024,256]{2,1,0:T(8,128)(2,1)S(1)}, u32[]{:S(2)}, u32[]{:S(2)}) collective-permute-start(bf16[2,1024,256]{2,1,0:T(8,128)(2,1)S(1)} %copy-done.14), channel_id=1, source_target_pairs={{0,4},{4,0},{8,12},{12,8},{16,20},{20,16},{24,28},{28,24},{1,5},{5... | collective-permute-start | bytes 3145736 | tf_op jit(solution)/shard_map/ppermute | solution.py:485
  132.1 1.0 copy-start.7
  132.1 1.4 copy-start.8
  141.1 20.2 %copy-start.9 = (bf16[2,1024,256]{2,1,0:T(8,128)(2,1)}, bf16[2,1024,256]{2,1,0:T(8,128)(2,1)S(1)}, u32[]{:S(2)}) copy-start(bf16[2,1024,256]{2,1,0:T(8,128)(2,1)S(1)} %collective-permute-done.10.refs_2_) | copy-start | bytes 3145732
  141.2 20.1 %copy-start.10 = (bf16[2,1024,256]{2,1,0:T(8,128)(2,1)}, bf16[2,1024,256]{2,1,0:T(8,128)(2,1)S(1)}, u32[]{:S(2)}) copy-start(bf16[2,1024,256]{2,1,0:T(8,128)(2,1)S(1)} %collective-permute-done.11.refs_3_) | copy-start | bytes 3145732
  141.2 19.0 %collective-permute-start.12 = (bf16[2,1024,256]{2,1,0:T(8,128)(2,1)S(1)}, bf16[2,1024,256]{2,1,0:T(8,128)(2,1)S(1)}, u32[]{:S(2)}, u32[]{:S(2)}) collective-permute-start(bf16[2,1024,256]{2,1,0:T(8,128)(2,1)S(1)} %collective-permute-done.10.refs_2_), channel_id=1, source_target_pairs={{0,32},{32,0},{64,96},{96,64},{1,33},{33,1},{65,97},{97,65},{2,34}... | collective-permute-start | bytes 3145736 | tf_op jit(solution)/shard_map/ppermute | solution.py:489
  141.3 18.9 %collective-permute-start.13 = (bf16[2,1024,256]{2,1,0:T(8,128)(2,1)S(1)}, bf16[2,1024,256]{2,1,0:T(8,128)(2,1)S(1)}, u32[]{:S(2)}, u32[]{:S(2)}) collective-permute-start(bf16[2,1024,256]{2,1,0:T(8,128)(2,1)S(1)} %collective-permute-done.11.refs_3_), channel_id=1, source_target_pairs={{0,32},{32,0},{64,96},{96,64},{1,33},{33,1},{65,97},{97,65},{2,34}... | collective-permute-start | bytes 3145736 | tf_op jit(solution)/shard_map/ppermute | solution.py:489
  160.1 18.7 %copy-start.11 = (bf16[2,1024,256]{2,1,0:T(8,128)(2,1)}, bf16[2,1024,256]{2,1,0:T(8,128)(2,1)S(1)}, u32[]{:S(2)}) copy-start(bf16[2,1024,256]{2,1,0:T(8,128)(2,1)S(1)} %collective-permute-done.12.refs_4_) | copy-start | bytes 3145732
  160.1 18.6 %copy-start.12 = (bf16[2,1024,256]{2,1,0:T(8,128)(2,1)}, bf16[2,1024,256]{2,1,0:T(8,128)(2,1)S(1)}, u32[]{:S(2)}) copy-start(bf16[2,1024,256]{2,1,0:T(8,128)(2,1)S(1)} %collective-permute-done.13.refs_5_) | copy-start | bytes 3145732
  179.4 9.6 %all-to-all-start.7 = ((bf16[8,16,256]{2,1,0:T(8,128)(2,1)}), bf16[8,16,256]{2,1,0:T(8,128)(2,1)S(1)}, u32[]{:S(2)}, u32[]{:S(2)}) async-start(bf16[8,16,256]{2,1,0:T(8,128)(2,1)} %broadcast_in_dim.36), calls=%async_computation.7 | async-start | bytes 131072 | tf_op jit(solution)/shard_map/all_to_all | solution.py:443
  182.8 1.0 copy-start.2

commit v7 on v6

--- a/solution.py
+++ b/solution.py
@@ -87,8 +87,8 @@
             for copy in copies(n):
                 copy.start()
 
-        def fetch(n):
-            for copy in copies(n):
+        def fetch(n, which=slice(None)):
+            for copy in copies(n)[which]:
                 copy.wait()
 
         body(
@@ -205,7 +205,7 @@
     )[0]
 
 
-def pair_totals(s_ref, g_ref, w_refs, n):
+def pair_totals(fetch, s_ref, g_ref, w_refs, n):
     own_ref, *others = w_refs
     cells, _, width = own_ref.shape
     half = cells // 2
@@ -213,10 +213,12 @@
     pieces = half // deep
     x, core = s_ref[0], s_ref[1]
     cut = slice(n * width, (n + 1) * width)
+    fetch(n, slice(0, 1))
     yield x, sum_of(
         dot(own_ref[a, cut], g_ref[a // 2, (a % 2) * width : (a % 2 + 1) * width])
         for a in range(cells)
     )
+    fetch(n, slice(1, None))
     yield 1 - x, sum_of(
         dot(
             refs[i // deep][i % deep, cut],
@@ -236,8 +238,7 @@
         whole = sum_of(g_ref[k, 2 * width :].astype(F32) for k in range(g_ref.shape[0]))
         for n in range(groups):
             o_ref[n, 2 * width :] = whole.astype(o_ref.dtype)
-            fetch(n)
-            for column, total in pair_totals(s_ref, g_ref, w_refs, n):
+            for column, total in pair_totals(fetch, s_ref, g_ref, w_refs, n):
                 start = pl.multiple_of(column * width, width)
                 o_ref[n, pl.ds(start, width)] = total.astype(o_ref.dtype)
 
@@ -264,8 +265,7 @@
             f_ref[layers - 1 - k] = factor(layers - 1 - k, ref).astype(f_ref.dtype)
         final = factor(0, grad_refs[-1])
         for n in range(groups):
-            fetch(n)
-            for column, total in pair_totals(s_ref, g_ref, w_refs, n):
+            for column, total in pair_totals(fetch, s_ref, g_ref, w_refs, n):
                 start = pl.multiple_of(column * width, width)
                 rounded = total.astype(o_ref.dtype)
                 o_ref[n, pl.ds(start, width)] = rounded
@@ -297,8 +297,7 @@
             o_ref[k, width:] = jnp.zeros((under, o_ref.shape[2]), o_ref.dtype)
         fetch(-1)
         for n in range(groups):
-            fetch(n)
-            for column, total in pair_totals(s_ref, g_ref, w_refs, n):
+            for column, total in pair_totals(fetch, s_ref, g_ref, w_refs, n):
                 start = pl.multiple_of(column * width, width)
                 mine = t_ref[pl.ds(start, width)]
                 total = total + jnp.where(n == s_ref[2], mine, jnp.zeros_like(mine))

time: 213 us -> 218 us (1.023)
  Pallas kernels: 46.9 us -> 52.2 us
    pallas_call x4, Pallas kernels: 22.1 us -> 27.4 us  [streamed_call(): pl.pallas_call(kernel, in_specs=[SCALARS] * len(scalars) + [pl.BlockSpec(...]
  transfers between devices with their start and end apart: 17 -> 17, of which waited for: 3 -> 3; matrix products, arithmetic and copies ran while one was open for 0% -> 0% of each run, Pallas kernels for 21% -> 23%
where the time goes in v7:
time: 218 us; the launch traced here: 217 us
  blocking collectives  115 us (53%)
  Pallas kernels  52.2 us (24%)
  starting transfers between devices  28.5 us (13%)
  waiting for transfers between devices  12.4 us (6%)
  local copies, waits for them, and re-layouts  7.17 us (3%)
    all_to_all x6, blocking collectives, exchange(): lax.all_to_all(blocks, axes, 0, 0, tiled=True, axis_index_groups=groups)  115 us
    pallas_call x4, Pallas kernels, streamed_call(): pl.pallas_call(kernel, in_specs=[SCALARS] * len(scalars) + [pl.BlockSpec(...  27.4 us
    pallas_call x4, Pallas kernels, features_first(): pl.pallas_call(body, grid_spec=pltpu.PrefetchScalarGridSpec(num_scalar_pr...  18.8 us
    all_to_all x3, starting transfers between devices, exchange(): lax.all_to_all(blocks, axes, 0, 0, tiled=True, axis_index_groups=groups)  12.7 us
    all_to_all x3, waiting for transfers between devices, exchange(): lax.all_to_all(blocks, axes, 0, 0, tiled=True, axis_index_groups=groups)  11 us
    pallas_call x4, Pallas kernels, local_call(): pl.pallas_call(body, in_specs=[SCALARS] * len(scalars) + [WIDE] * len(ope...  4.9 us
    ppermute x2, starting transfers between devices, over_both(): lax.ppermute(values[0], ('dp', 'tensor'), across)  4.85 us
  transfers between devices with their start and end apart: 17, of which 3 were waited for; matrix products, arithmetic and copies ran while one was open for 0% of the time, Pallas kernels for 23%

profile of v7, /device:TPU:0, one launch (start us, length us, event | category | flops | bytes accessed | tf_op | source)
XLA Modules:
  0.0 217.2 jit_solution(55868548121731816)
XLA Ops:
  0.6 2.6 %broadcast_in_dim.34 = bf16[8,512,256]{2,1,0:T(8,128)(2,1)} broadcast(bf16[512,256]{1,0:T(8,128)(2,1)} %param.8), dimensions={1,2} | broadcast | bytes 2359296 | tf_op jit(solution)/shard_map/broadcast_in_dim | solution.py:474
  3.2 5.5 %all-to-all-start = ((bf16[8,512,256]{2,1,0:T(8,128)(2,1)}), bf16[8,512,256]{2,1,0:T(8,128)(2,1)S(1)}, u32[]{:S(2)}, u32[]{:S(2)}) async-start(bf16[8,512,256]{2,1,0:T(8,128)(2,1)} %broadcast_in_dim.34), calls=%async_computation | async-start | bytes 4194304 | tf_op jit(solution)/shard_map/all_to_all | solution.py:442
  8.7 4.8 %shard_map.87 = (bf16[8,1024,256]{2,1,0:T(8,128)(2,1)}, bf16[4,1024,256]{2,1,0:T(8,128)(2,1)}) custom-call(s32[1]{0:T(128)} %bitcast.core_ref, bf16[4,1024,8,256]{3,2,1,0:T(8,128)(2,1)} %bitcast.38), custom_call_target="tpu_custom_call" | custom-call | bytes 10485760 | tf_op jit(solution)/shard_map/pallas_call | solution.py:133
  13.5 3.3 %collective-permute-start.6 = (bf16[4,1024,256]{2,1,0:T(8,128)(2,1)}, bf16[4,1024,256]{2,1,0:T(8,128)(2,1)}, u32[]{:S(2)}, u32[]{:S(2)}) collective-permute-start(bf16[4,1024,256]{2,1,0:T(8,128)(2,1)} %get-tuple-element.74), channel_id=1, source_target_pairs={{0,68},{4,64},{8,76},{12,72},{16,84},{20,80},{24,92},{28,88},{32,1... | collective-permute-start | bytes 6291464 | tf_op jit(solution)/shard_map/ppermute | solution.py:490
  16.8 4.2 %shard_map.86.refs_0_ = bf16[8,1024,256]{2,1,0:T(8,128)(2,1)} custom-call(s32[1]{0:T(128)} %bitcast.core_ref, bf16[4,1024,8,256]{3,2,1,0:T(8,128)(2,1)} %bitcast.39), custom_call_target="tpu_custom_call" | custom-call | bytes 10485760 | tf_op jit(solution)/shard_map/pallas_call | solution.py:133
  21.0 4.9 %shard_map.88 = (bf16[8,1024,256]{2,1,0:T(8,128)(2,1)}, bf16[2,1024,256]{2,1,0:T(8,128)(2,1)}, bf16[2,1024,256]{2,1,0:T(8,128)(2,1)}) custom-call(s32[1]{0:T(128)} %bitcast.core_ref, bf16[4,1024,8,256]{3,2,1,0:T(8,128)(2,1)} %bitcast.40), custom_call_target="tpu_custom_call" | custom-call | bytes 10485760 | tf_op jit(solution)/shard_map/pallas_call | solution.py:133
  26.0 1.2 copy-done.1
  27.2 0.9 shard_map.89
  28.2 0.1 select_reduce_fusion.refs_1_
  28.3 7.4 %all-to-all-done.refs_1_.g_ref = bf16[8,512,256]{2,1,0:T(8,128)(2,1)S(1)} async-done(((bf16[8,512,256]{2,1,0:T(8,128)(2,1)}), bf16[8,512,256]{2,1,0:T(8,128)(2,1)S(1)}, u32[]{:S(2)}, u32[]{:S(2)}) %all-to-all-start) | async-done | bytes 2097184 | tf_op jit(solution)/shard_map/all_to_all | solution.py:442
  35.7 4.2 %shard_map.90 = bf16[8,320,256]{2,1,0:T(8,128)(2,1)S(1)} custom-call(bf16[8,1024,256]{2,1,0:T(8,128)(2,1)} %shard_map.86.refs_0_, bf16[8,512,256]{2,1,0:T(8,128)(2,1)S(1)} %all-to-all-done.refs_1_.g_ref, bf16[8,64,256]{2,1,0:T(8,128)(2,1)S(1)} %bitcast.37), custom_call_target="tpu_custom_call" | custom-call | flops 1073741824 | bytes 4194304 | tf_op jit(solution)/shard_map/pallas_call | solution.py:103
  39.9 22.8 %all_to_all.45.r_ref = bf16[8,320,256]{2,1,0:T(8,128)(2,1)S(1)} all-to-all(bf16[8,320,256]{2,1,0:T(8,128)(2,1)S(1)} %shard_map.90), channel_id=1, replica_groups={{0,1,2,3,4,5,6,7},{8,9,10,11,12,13,14,15},{16,17,18,19,20,21,22,23},{24..., dimensions={0} | all-to-all | bytes 2621440 | tf_op jit(solution)/shard_map/all_to_all | solution.py:442
  62.7 2.2 shard_map.91
  64.9 0.7 collective-permute-start
  65.5 3.9 %all-to-all-start.2 = ((bf16[4,576,256]{2,1,0:T(8,128)(2,1)}), bf16[4,576,256]{2,1,0:T(8,128)(2,1)S(1)}, u32[]{:S(2)}, u32[]{:S(2)}) async-start(bf16[4,576,256]{2,1,0:T(8,128)(2,1)} %get-tuple-element.60), calls=%async_computation.2 | async-start | bytes 2359296 | tf_op jit(solution)/shard_map/all_to_all | solution.py:442
  69.4 1.4 collective-permute-done
  70.8 1.5 collective-permute-start.3
  72.3 0.9 collective-permute-start.2
  73.2 1.8 collective-permute-start.1
  75.0 4.8 %shard_map.92 = (bf16[8,1024,256]{2,1,0:T(8,128)(2,1)}, bf16[2,1024,256]{2,1,0:T(8,128)(2,1)}, bf16[2,1024,256]{2,1,0:T(8,128)(2,1)}) custom-call(s32[1]{0:T(128)} %bitcast.core_ref, bf16[4,1024,8,256]{3,2,1,0:T(8,128)(2,1)} %bitcast.41), custom_call_target="tpu_custom_call" | custom-call | bytes 10485760 | tf_op jit(solution)/shard_map/pallas_call | solution.py:133
  79.8 1.9 collective-permute-start.4
  81.7 0.8 collective-permute-start.5
  82.7 3.5 %all-to-all-done.2.refs_4_ = bf16[4,576,256]{2,1,0:T(8,128)(2,1)S(1)} async-done(((bf16[4,576,256]{2,1,0:T(8,128)(2,1)}), bf16[4,576,256]{2,1,0:T(8,128)(2,1)S(1)}, u32[]{:S(2)}, u32[]{:S(2)}) %all-to-all-start.2) | async-done | bytes 1179680 | tf_op jit(solution)/shard_map/all_to_all | solution.py:442
  86.2 7.4 %shard_map.93 = bf16[4,576,256]{2,1,0:T(8,128)(2,1)S(1)} custom-call(s32[4]{0:T(128)S(1)} %pad_add_fusion.s_ref.refs_0_, bf16[8,1024,256]{2,1,0:T(8,128)(2,1)} %get-tuple-element.73.refs_1_, bf16[4,1024,256]{2,1,0:T(8,128)(2,1)} %collective-permute-done.6.refs_2_, bf16[4,1024,256]{2,1,0:T(8,128)(2,1)} %collective-permute-done.7.refs_3_, ...), custom_call_target="tpu_custom_call" | custom-call | flops 2147483648 | bytes 8388608 | tf_op jit(solution)/shard_map/pallas_call | solution.py:103
  93.7 18.7 %all_to_all.46.r_ref = bf16[4,576,256]{2,1,0:T(8,128)(2,1)S(1)} all-to-all(bf16[4,576,256]{2,1,0:T(8,128)(2,1)S(1)} %shard_map.93), channel_id=1, replica_groups=mesh['dp'=4,'tensor'=8,'layer'=4] {'layer'}, dimensions={0} | all-to-all | bytes 2359296 | tf_op jit(solution)/shard_map/all_to_all | solution.py:442
  112.3 0.1 shard_map.94
  112.6 0.5 collective-permute-start.9
  113.1 3.0 %collective-permute-start.10 = (bf16[2,1024,256]{2,1,0:T(8,128)(2,1)S(1)}, bf16[2,1024,256]{2,1,0:T(8,128)(2,1)S(1)}, u32[]{:S(2)}, u32[]{:S(2)}) collective-permute-start(bf16[2,1024,256]{2,1,0:T(8,128)(2,1)S(1)} %copy-done.15), channel_id=1, source_target_pairs={{0,68},{4,64},{8,76},{12,72},{16,84},{20,80},{24,92},{28,88},{32,1... | collective-permute-start | bytes 3145736 | tf_op jit(solution)/shard_map/ppermute | solution.py:483
  116.1 0.8 collective-permute-start.11
  117.0 17.5 %all_to_all.47.refs_7_ = bf16[4,512,256]{2,1,0:T(8,128)(2,1)S(1)} all-to-all(bf16[4,512,256]{2,1,0:T(8,128)(2,1)S(1)} %get-tuple-element.80), channel_id=1, replica_groups={{0,8,16,24},{4,12,20,28},{1,9,17,25},{5,13,21,29},{2,10,18,26},{6,14,22..., dimensions={0} | all-to-all | bytes 2097152 | tf_op jit(solution)/shard_map/all_to_all | solution.py:442
  134.5 1.0 copy-done.7
  135.5 0.4 copy-done.8
  135.8 8.2 %shard_map.95 = bf16[4,528,256]{2,1,0:T(8,128)(2,1)S(1)} custom-call(s32[4]{0:T(128)S(1)} %pad_add_fusion.s_ref.refs_0_, s32[4]{0:T(128)S(1)} %select_reduce_fusion.refs_1_, bf16[8,1024,256]{2,1,0:T(8,128)(2,1)} %get-tuple-element.70.refs_2_, bf16[2,1024,256]{2,1,0:T(8,128)(2,1)} %collective-permute-done.4.refs_3_, ...), custom_call_target="tpu_custom_call" | custom-call | flops 2147483648 | bytes 8388608 | tf_op jit(solution)/shard_map/pallas_call | solution.py:103
  144.2 0.5 collective-permute-start.13
  144.7 18.4 %all_to_all.48.r_ref = bf16[4,528,256]{2,1,0:T(8,128)(2,1)S(1)} all-to-all(bf16[4,528,256]{2,1,0:T(8,128)(2,1)S(1)} %shard_map.95), channel_id=1, replica_groups=mesh['dp'=4,'tensor'=8,'layer'=4] {'layer'}, dimensions={0} | all-to-all | bytes 2162688 | tf_op jit(solution)/shard_map/all_to_all | solution.py:442
  163.1 1.1 shard_map.96
  164.2 17.5 %all_to_all.49.refs_7_ = bf16[4,528,256]{2,1,0:T(8,128)(2,1)S(1)} all-to-all(bf16[4,528,256]{2,1,0:T(8,128)(2,1)S(1)} %get-tuple-element.101), channel_id=1, replica_groups={{0,8,16,24},{4,12,20,28},{1,9,17,25},{5,13,21,29},{2,10,18,26},{6,14,22..., dimensions={0} | all-to-all | bytes 2162688 | tf_op jit(solution)/shard_map/all_to_all | solution.py:442
  181.7 0.6 broadcast_in_dim.36
  182.4 3.4 %all-to-all-start.7 = ((bf16[8,16,256]{2,1,0:T(8,128)(2,1)}), bf16[8,16,256]{2,1,0:T(8,128)(2,1)S(1)}, u32[]{:S(2)}, u32[]{:S(2)}) async-start(bf16[8,16,256]{2,1,0:T(8,128)(2,1)} %broadcast_in_dim.36), calls=%async_computation.7 | async-start | bytes 131072 | tf_op jit(solution)/shard_map/all_to_all | solution.py:442
  185.7 1.0 copy-done.2
  186.8 7.6 %shard_map.97._ = bf16[8,272,256]{2,1,0:T(8,128)(2,1)S(1)} custom-call(s32[4]{0:T(128)S(1)} %pad_add_fusion.s_ref.refs_0_, bf16[8,1024,256]{2,1,0:T(8,128)(2,1)} %get-tuple-element.68.refs_1_, bf16[2,1024,256]{2,1,0:T(8,128)(2,1)} %copy-done.9, bf16[2,1024,256]{2,1,0:T(8,128)(2,1)} %copy-done.10, bf16[2,1024,256]{2,1,0:T(8,128)(2,1)} %copy-done.11, ...), custom_call_target="tpu_custom_call" | custom-call | flops 2147483648 | bytes 8388608 | tf_op jit(solution)/shard_map/pallas_call | solution.py:103
  194.3 0.1 convert_element_type.44
  194.5 0.1 reduce.1
  194.6 0.1 convert_element_type.48
  194.7 0.4 subtract_convert_fusion
  195.1 0.2 shard_map.98
  195.3 20.4 %all_to_all.50.r_ref = bf16[8,272,256]{2,1,0:T(8,128)(2,1)S(1)} all-to-all(bf16[8,272,256]{2,1,0:T(8,128)(2,1)S(1)} %shard_map.98), channel_id=1, replica_groups={{0,1,2,3,4,5,6,7},{8,9,10,11,12,13,14,15},{16,17,18,19,20,21,22,23},{24..., dimensions={0} | all-to-all | bytes 2228224 | tf_op jit(solution)/shard_map/all_to_all | solution.py:442
  215.7 1.4 shard_map.99
  (57 shorter events, 0.6 us)
Async XLA Ops:
  0.6 194.1 %copy-start = (bf16[1,128,4096]{2,1,0:T(8,128)(2,1)S(1)}, bf16[1,128,4096]{2,1,0:T(8,128)(2,1)}, u32[]{:S(2)}) copy-start(bf16[1,128,4096]{2,1,0:T(8,128)(2,1)} %param.12) | copy-start | bytes 3145732
  3.2 32.5 %all-to-all-start = ((bf16[8,512,256]{2,1,0:T(8,128)(2,1)}), bf16[8,512,256]{2,1,0:T(8,128)(2,1)S(1)}, u32[]{:S(2)}, u32[]{:S(2)}) async-start(bf16[8,512,256]{2,1,0:T(8,128)(2,1)} %broadcast_in_dim.34), calls=%async_computation | async-start | bytes 4194304 | tf_op jit(solution)/shard_map/all_to_all | solution.py:442
  13.5 51.3 %collective-permute-start.6 = (bf16[4,1024,256]{2,1,0:T(8,128)(2,1)}, bf16[4,1024,256]{2,1,0:T(8,128)(2,1)}, u32[]{:S(2)}, u32[]{:S(2)}) collective-permute-start(bf16[4,1024,256]{2,1,0:T(8,128)(2,1)} %get-tuple-element.74), channel_id=1, source_target_pairs={{0,68},{4,64},{8,76},{12,72},{16,84},{20,80},{24,92},{28,88},{32,1... | collective-permute-start | bytes 6291464 | tf_op jit(solution)/shard_map/ppermute | solution.py:490
  21.0 4.9 %copy-start.6 = (bf16[4,64,256]{2,1,0:T(8,128)(2,1)S(1)}, bf16[4,64,256]{2,1,0:T(8,128)(2,1)}, u32[]{:S(2)}) copy-start(bf16[4,64,256]{2,1,0:T(8,128)(2,1)} %p_ref.1) | copy-start | bytes 393220
  26.0 2.2 %copy-start.16 = (s32[4]{0:T(128)S(1)}, s32[4]{0:T(128)}, u32[]{:S(2)}) copy-start(s32[4]{0:T(128)} %param.13) | copy-start | bytes 52
  26.0 1.2 copy-start.1
  62.7 2.2 %copy-start.13 = (bf16[4,64,256]{2,1,0:T(8,128)(2,1)S(1)}, bf16[4,64,256]{2,1,0:T(8,128)(2,1)}, u32[]{:S(2)}) copy-start(bf16[4,64,256]{2,1,0:T(8,128)(2,1)} %param.11) | copy-start | bytes 393220
  64.8 21.4 %collective-permute-start.7 = (bf16[4,1024,256]{2,1,0:T(8,128)(2,1)}, bf16[4,1024,256]{2,1,0:T(8,128)(2,1)}, u32[]{:S(2)}, u32[]{:S(2)}) collective-permute-start(bf16[4,1024,256]{2,1,0:T(8,128)(2,1)} %collective-permute-done.6.refs_2_), channel_id=1, source_target_pairs={{0,32},{32,0},{64,96},{96,64},{1,33},{33,1},{65,97},{97,65},{2,34}... | collective-permute-start | bytes 6291464 | tf_op jit(solution)/shard_map/ppermute | solution.py:488
  64.9 5.9 %collective-permute-start = (bf16[4,64,256]{2,1,0:T(8,128)(2,1)S(1)}, bf16[4,64,256]{2,1,0:T(8,128)(2,1)S(1)}, u32[]{:S(2)}, u32[]{:S(2)}) collective-permute-start(bf16[4,64,256]{2,1,0:T(8,128)(2,1)S(1)} %copy-done.13), channel_id=1, source_target_pairs={{0,4},{4,0},{8,12},{12,8},{16,20},{20,16},{24,28},{28,24},{1,5},{5... | collective-permute-start | bytes 393224 | tf_op jit(solution)/shard_map/ppermute | solution.py:501
  65.5 20.7 %all-to-all-start.2 = ((bf16[4,576,256]{2,1,0:T(8,128)(2,1)}), bf16[4,576,256]{2,1,0:T(8,128)(2,1)S(1)}, u32[]{:S(2)}, u32[]{:S(2)}) async-start(bf16[4,576,256]{2,1,0:T(8,128)(2,1)} %get-tuple-element.60), calls=%async_computation.2 | async-start | bytes 2359296 | tf_op jit(solution)/shard_map/all_to_all | solution.py:442
  70.8 10.9 %collective-permute-start.3 = (bf16[2,64,256]{2,1,0:T(8,128)(2,1)S(1)}, bf16[2,64,256]{2,1,0:T(8,128)(2,1)S(1)}, u32[]{:S(2)}, u32[]{:S(2)}) collective-permute-start(bf16[2,64,256]{2,1,0:T(8,128)(2,1)S(1)} %slice_bitcast_fusion), channel_id=1, source_target_pairs={{0,3},{1,2},{2,1},{3,0},{4,7},{5,6},{6,5},{7,4},{8,11},{9,10},{10,... | collective-permute-start | bytes 196616 | tf_op jit(solution)/shard_map/ppermute | solution.py:506
  72.3 10.2 %collective-permute-start.2 = (bf16[2,64,256]{2,1,0:T(8,128)(2,1)S(1)}, bf16[2,64,256]{2,1,0:T(8,128)(2,1)S(1)}, u32[]{:S(2)}, u32[]{:S(2)}) collective-permute-start(bf16[2,64,256]{2,1,0:T(8,128)(2,1)S(1)} %slice_bitcast_fusion), channel_id=1, source_target_pairs={{0,2},{1,3},{2,0},{3,1},{4,6},{5,7},{6,4},{7,5},{8,10},{9,11},{10,... | collective-permute-start | bytes 196616 | tf_op jit(solution)/shard_map/ppermute | solution.py:506
  73.2 9.3 %collective-permute-start.1 = (bf16[2,64,256]{2,1,0:T(8,128)(2,1)S(1)}, bf16[2,64,256]{2,1,0:T(8,128)(2,1)S(1)}, u32[]{:S(2)}, u32[]{:S(2)}) collective-permute-start(bf16[2,64,256]{2,1,0:T(8,128)(2,1)S(1)} %slice_bitcast_fusion), channel_id=1, source_target_pairs={{0,1},{1,0},{2,3},{3,2},{4,5},{5,4},{6,7},{7,6},{8,9},{9,8},{10,11... | collective-permute-start | bytes 196616 | tf_op jit(solution)/shard_map/ppermute | solution.py:506
  79.8 32.7 %collective-permute-start.4 = (bf16[2,1024,256]{2,1,0:T(8,128)(2,1)}, bf16[2,1024,256]{2,1,0:T(8,128)(2,1)}, u32[]{:S(2)}, u32[]{:S(2)}) collective-permute-start(bf16[2,1024,256]{2,1,0:T(8,128)(2,1)} %get-tuple-element.71), channel_id=1, source_target_pairs={{0,68},{4,64},{8,76},{12,72},{16,84},{20,80},{24,92},{28,88},{32,1... | collective-permute-start | bytes 3145736 | tf_op jit(solution)/shard_map/ppermute | solution.py:483
  81.7 30.8 %collective-permute-start.5 = (bf16[2,1024,256]{2,1,0:T(8,128)(2,1)}, bf16[2,1024,256]{2,1,0:T(8,128)(2,1)}, u32[]{:S(2)}, u32[]{:S(2)}) collective-permute-start(bf16[2,1024,256]{2,1,0:T(8,128)(2,1)} %get-tuple-element.72), channel_id=1, source_target_pairs={{0,4},{4,0},{8,12},{12,8},{16,20},{20,16},{24,28},{28,24},{1,5},{5... | collective-permute-start | bytes 3145736 | tf_op jit(solution)/shard_map/ppermute | solution.py:484
  93.7 18.7 %copy-start.3 = (f32[512,256]{1,0:T(8,128)S(1)}, f32[512,256]{1,0:T(8,128)}, u32[]{:S(2)}) copy-start(f32[512,256]{1,0:T(8,128)} %get-tuple-element.66.t_ref) | copy-start | bytes 1572868
  93.7 19.5 %copy-start.15 = (bf16[2,1024,256]{2,1,0:T(8,128)(2,1)S(1)}, bf16[2,1024,256]{2,1,0:T(8,128)(2,1)}, u32[]{:S(2)}) copy-start(bf16[2,1024,256]{2,1,0:T(8,128)(2,1)} %get-tuple-element.92) | copy-start | bytes 3145732
  112.3 3.8 %copy-start.14 = (bf16[2,1024,256]{2,1,0:T(8,128)(2,1)S(1)}, bf16[2,1024,256]{2,1,0:T(8,128)(2,1)}, u32[]{:S(2)}) copy-start(bf16[2,1024,256]{2,1,0:T(8,128)(2,1)} %get-tuple-element.93) | copy-start | bytes 3145732
  112.5 23.3 %copy-start.4 = (bf16[512,256]{1,0:T(8,128)(2,1)S(1)}, bf16[512,256]{1,0:T(8,128)(2,1)}, u32[]{:S(2)}) copy-start(bf16[512,256]{1,0:T(8,128)(2,1)} %get-tuple-element.84.refs_8_) | copy-start | bytes 786436
  112.5 23.3 %copy-start.5 = (bf16[512,256]{1,0:T(8,128)(2,1)S(1)}, bf16[512,256]{1,0:T(8,128)(2,1)}, u32[]{:S(2)}) copy-start(bf16[512,256]{1,0:T(8,128)(2,1)} %get-tuple-element.85.refs_9_) | copy-start | bytes 786436
  112.5 21.9 %collective-permute-start.8 = (bf16[2,1024,256]{2,1,0:T(8,128)(2,1)}, bf16[2,1024,256]{2,1,0:T(8,128)(2,1)S(1)}, u32[]{:S(2)}, u32[]{:S(2)}) collective-permute-start(bf16[2,1024,256]{2,1,0:T(8,128)(2,1)} %collective-permute-done.4.refs_3_), channel_id=1, source_target_pairs={{0,32},{32,0},{64,96},{96,64},{1,33},{33,1},{65,97},{97,65},{2,34}... | collective-permute-start | bytes 3145736 | tf_op jit(solution)/shard_map/ppermute | solution.py:488
  112.6 21.8 %collective-permute-start.9 = (bf16[2,1024,256]{2,1,0:T(8,128)(2,1)}, bf16[2,1024,256]{2,1,0:T(8,128)(2,1)S(1)}, u32[]{:S(2)}, u32[]{:S(2)}) collective-permute-start(bf16[2,1024,256]{2,1,0:T(8,128)(2,1)} %collective-permute-done.5.refs_4_), channel_id=1, source_target_pairs={{0,32},{32,0},{64,96},{96,64},{1,33},{33,1},{65,97},{97,65},{2,34}... | collective-permute-start | bytes 3145736 | tf_op jit(solution)/shard_map/ppermute | solution.py:488
  113.1 30.9 %collective-permute-start.10 = (bf16[2,1024,256]{2,1,0:T(8,128)(2,1)S(1)}, bf16[2,1024,256]{2,1,0:T(8,128)(2,1)S(1)}, u32[]{:S(2)}, u32[]{:S(2)}) collective-permute-start(bf16[2,1024,256]{2,1,0:T(8,128)(2,1)S(1)} %copy-done.15), channel_id=1, source_target_pairs={{0,68},{4,64},{8,76},{12,72},{16,84},{20,80},{24,92},{28,88},{32,1... | collective-permute-start | bytes 3145736 | tf_op jit(solution)/shard_map/ppermute | solution.py:483
  116.1 28.0 %collective-permute-start.11 = (bf16[2,1024,256]{2,1,0:T(8,128)(2,1)S(1)}, bf16[2,1024,256]{2,1,0:T(8,128)(2,1)S(1)}, u32[]{:S(2)}, u32[]{:S(2)}) collective-permute-start(bf16[2,1024,256]{2,1,0:T(8,128)(2,1)S(1)} %copy-done.14), channel_id=1, source_target_pairs={{0,4},{4,0},{8,12},{12,8},{16,20},{20,16},{24,28},{28,24},{1,5},{5... | collective-permute-start | bytes 3145736 | tf_op jit(solution)/shard_map/ppermute | solution.py:484
  134.5 1.0 copy-start.7
  134.5 1.4 copy-start.8
  144.1 20.2 %copy-start.9 = (bf16[2,1024,256]{2,1,0:T(8,128)(2,1)}, bf16[2,1024,256]{2,1,0:T(8,128)(2,1)S(1)}, u32[]{:S(2)}) copy-start(bf16[2,1024,256]{2,1,0:T(8,128)(2,1)S(1)} %collective-permute-done.10.refs_2_) | copy-start | bytes 3145732
  144.1 20.1 %copy-start.10 = (bf16[2,1024,256]{2,1,0:T(8,128)(2,1)}, bf16[2,1024,256]{2,1,0:T(8,128)(2,1)S(1)}, u32[]{:S(2)}) copy-start(bf16[2,1024,256]{2,1,0:T(8,128)(2,1)S(1)} %collective-permute-done.11.refs_3_) | copy-start | bytes 3145732
  144.1 19.0 %collective-permute-start.12 = (bf16[2,1024,256]{2,1,0:T(8,128)(2,1)S(1)}, bf16[2,1024,256]{2,1,0:T(8,128)(2,1)S(1)}, u32[]{:S(2)}, u32[]{:S(2)}) collective-permute-start(bf16[2,1024,256]{2,1,0:T(8,128)(2,1)S(1)} %collective-permute-done.10.refs_2_), channel_id=1, source_target_pairs={{0,32},{32,0},{64,96},{96,64},{1,33},{33,1},{65,97},{97,65},{2,34}... | collective-permute-start | bytes 3145736 | tf_op jit(solution)/shard_map/ppermute | solution.py:488
  144.2 18.9 %collective-permute-start.13 = (bf16[2,1024,256]{2,1,0:T(8,128)(2,1)S(1)}, bf16[2,1024,256]{2,1,0:T(8,128)(2,1)S(1)}, u32[]{:S(2)}, u32[]{:S(2)}) collective-permute-start(bf16[2,1024,256]{2,1,0:T(8,128)(2,1)S(1)} %collective-permute-done.11.refs_3_), channel_id=1, source_target_pairs={{0,32},{32,0},{64,96},{96,64},{1,33},{33,1},{65,97},{97,65},{2,34}... | collective-permute-start | bytes 3145736 | tf_op jit(solution)/shard_map/ppermute | solution.py:488
  163.1 18.7 %copy-start.11 = (bf16[2,1024,256]{2,1,0:T(8,128)(2,1)}, bf16[2,1024,256]{2,1,0:T(8,128)(2,1)S(1)}, u32[]{:S(2)}) copy-start(bf16[2,1024,256]{2,1,0:T(8,128)(2,1)S(1)} %collective-permute-done.12.refs_4_) | copy-start | bytes 3145732
  163.1 18.6 %copy-start.12 = (bf16[2,1024,256]{2,1,0:T(8,128)(2,1)}, bf16[2,1024,256]{2,1,0:T(8,128)(2,1)S(1)}, u32[]{:S(2)}) copy-start(bf16[2,1024,256]{2,1,0:T(8,128)(2,1)S(1)} %collective-permute-done.13.refs_5_) | copy-start | bytes 3145732
  182.4 12.0 %all-to-all-start.7 = ((bf16[8,16,256]{2,1,0:T(8,128)(2,1)}), bf16[8,16,256]{2,1,0:T(8,128)(2,1)S(1)}, u32[]{:S(2)}, u32[]{:S(2)}) async-start(bf16[8,16,256]{2,1,0:T(8,128)(2,1)} %broadcast_in_dim.36), calls=%async_computation.7 | async-start | bytes 131072 | tf_op jit(solution)/shard_map/all_to_all | solution.py:442
  185.7 1.0 copy-start.2
